TPU v7x, 32 devices: a whole 2x2x4 slice. The times are simulated.
32 devices in a mesh: dp: 4 (over z), hid: 2 (over core), wid: 4 (over y, x).
Axes of the slice: x: 2, y: 2, z: 4, core: 2. Of those that a mesh axis runs over, the one named last changes fastest.
Arguments:
- tokens: bfloat16 [4096, 1536], P('dp', 'wid'), may hold values from -6 to 6
- cotangent: bfloat16 [4096, 1536], P('dp', 'wid'), may hold values from -6 to 6
- lengths: int32 [16], P(('dp', 'wid')), may hold values from 64 to 256, as said below
- w_project: bfloat16 [1536, 4, 1536], P('wid', None, 'hid'), may hold values from -0.15625 to 0.15625
- w_beta: bfloat16 [1536, 12], P('wid', 'hid'), may hold values from -0.15625 to 0.15625
- w_out: bfloat16 [1536, 1536], P('wid', 'hid'), may hold values from -1.25 to 1.25
- w_gate_up: bfloat16 [1536, 2, 4096], P('wid', None, 'hid'), may hold values from -0.15625 to 0.15625
- w_down: bfloat16 [1536, 4096], P('wid', 'hid'), may hold values from -0.09375 to 0.09375
- gain_attn: bfloat16 [1536], P('wid'), may hold values from 0.5 to 1.5
- gain_ffn: bfloat16 [1536], P('wid'), may hold values from 0.5 to 1.5
Outputs:
- output: bfloat16 [4096, 1536], P('dp', 'wid')
- input_grad: bfloat16 [4096, 1536], P('dp', 'wid')
- grad_project: float32 [1536, 4, 1536], P(('dp', 'wid'), None, 'hid')
- grad_beta: float32 [1536, 12], P(('dp', 'wid'), 'hid')
- grad_out: float32 [1536, 1536], P(('dp', 'wid'), 'hid')
- grad_gate_up: float32 [1536, 2, 4096], P(('dp', 'wid'), None, 'hid')
- grad_down: float32 [1536, 4096], P(('dp', 'wid'), 'hid')
- grad_gain_attn: float32 [1536], P(('dp', 'wid'))
- grad_gain_ffn: float32 [1536], P(('dp', 'wid'))
Inputs may be any that keep to these rules, and one draw needn't show every extreme that they name: `lengths`: some bucket is full and some bucket holds exactly 64 valid tokens.
All inputs are finite; a program needn't handle non-finite values.
Results may differ from a plain program's by a relative error of at most 0.015.
Values may be sent and summed in bfloat16 or wider, within the bound.
No kernel may reach another device: no remote copies, remote signals or barrier semaphores. Data moves between devices by JAX's collectives and lax.ppermute only.
A program may use at most 192 MiB of HBM per device.

v0:
```python
import jax
import jax.numpy as jnp
from jax import lax
from jax.sharding import PartitionSpec as P

GROUP = 64


highest = lax.Precision.HIGHEST
masked_score = -1e30


def path_attention(queries, key_rows, value_rows, house_raw, beta_logit, valid):
    seq_len, heads, head_size = queries.shape
    count = seq_len // GROUP
    scale = head_size ** (-0.5)
    house = house_raw * lax.rsqrt(jnp.sum(house_raw * house_raw, axis=-1, keepdims=True) + 1e-06)
    strength = 2.0 * jax.nn.sigmoid(beta_logit)

    def blocks(array):
        return array.reshape(count, GROUP, heads, head_size).transpose(0, 2, 1, 3)

    query_blocks = blocks(queries)
    key_blocks = blocks(key_rows)
    value_blocks = blocks(value_rows)
    house_blocks = blocks(house)
    value_all = value_rows.transpose(1, 0, 2)
    strength_blocks = strength.reshape(count, GROUP, heads).transpose(0, 2, 1)
    inner = jnp.arange(GROUP, dtype=jnp.int32)
    lower_incl = (inner[:, None] >= inner[None, :]).astype(jnp.float32)
    lower_strict = (inner[:, None] > inner[None, :]).astype(jnp.float32)
    gram = (
        jnp.einsum("nhie,nhje->nhij", house_blocks, house_blocks, precision=highest) * lower_strict
    )
    identity = jnp.eye(GROUP, dtype=jnp.float32)
    system = identity + strength_blocks[..., :, None] * gram
    diagonal = identity * strength_blocks[..., None, :]
    mixing = lax.linalg.triangular_solve(
        system, diagonal, left_side=True, lower=True, unit_diagonal=True
    )
    update = jnp.einsum("nhst,nhte->nhse", mixing, house_blocks, precision=highest)
    query_house = (
        jnp.einsum("nhie,nhse->nhis", query_blocks, house_blocks, precision=highest) * lower_incl
    )
    house_key = (
        jnp.einsum("nhte,nhje->nhtj", house_blocks, key_blocks, precision=highest) * lower_strict
    )
    carried = jnp.einsum("nhst,nhtj->nhsj", mixing, house_key, precision=highest)
    intra = jnp.einsum("nhie,nhje->nhij", query_blocks, key_blocks, precision=highest) - jnp.einsum(
        "nhis,nhsj->nhij", query_house, carried, precision=highest
    )
    query_hat = query_blocks - jnp.einsum("nhis,nhse->nhie", query_house, update, precision=highest)
    key_hat = key_blocks - jnp.einsum("nhsj,nhse->nhje", carried, house_blocks, precision=highest)
    positions = jnp.arange(seq_len, dtype=jnp.int32)
    key_valid = valid > 0.5

    def step(state, inputs):
        index, query_part, intra_part, update_part, house_part, key_part, value_part = inputs
        start = index * GROUP
        far = jnp.einsum("hie,hje->hij", query_part, state, precision=highest) * scale
        far_mask = (positions < start) & key_valid
        far = jnp.where(far_mask[None, None, :], far, masked_score)
        group_valid = lax.dynamic_slice_in_dim(valid, start, GROUP) > 0.5
        near_mask = (lower_incl > 0.5) & group_valid[None, :]
        near = jnp.where(near_mask[None], intra_part * scale, masked_score)
        top_score = jnp.maximum(
            jnp.max(far, axis=-1, keepdims=True), jnp.max(near, axis=-1, keepdims=True)
        )
        far_weight = jnp.exp(far - top_score)
        near_weight = jnp.exp(near - top_score)
        total = jnp.sum(far_weight, axis=-1, keepdims=True) + jnp.sum(
            near_weight, axis=-1, keepdims=True
        )
        mixed = jnp.einsum("hij,hje->hie", far_weight, value_all, precision=highest) + jnp.einsum(
            "hij,hje->hie", near_weight, value_part, precision=highest
        )
        mixed = mixed / total
        along = jnp.einsum("hje,hce->hjc", state, update_part, precision=highest)
        moved = state - jnp.einsum("hjc,hce->hje", along, house_part, precision=highest)
        state = lax.dynamic_update_slice_in_dim(moved, key_part, start, axis=1)
        return (state, mixed)

    initial = jnp.zeros((heads, seq_len, head_size), jnp.float32)
    indices = jnp.arange(count, dtype=jnp.int32)
    xs_all = (indices, query_hat, intra, update, house_blocks, key_hat, value_blocks)
    final_state, outputs = lax.scan(jax.checkpoint(step), initial, xs_all)
    result = outputs.transpose(0, 2, 1, 3).reshape(seq_len, heads, head_size)
    return result * valid[:, None, None]


def norm_back(grad_normed, source, factor, gain):
    scaled = grad_normed * gain
    return factor * scaled - factor * factor * factor * source * jnp.mean(
        scaled * source, axis=-1, keepdims=True
    )


def per_device(
    tokens, cotangent, lengths, w_project, w_beta, w_out, w_gate_up, w_down, gain_attn, gain_ffn
):
    rows, grad_rows = (
        lax.all_to_all(tokens, "wid", split_axis=0, concat_axis=1, tiled=True),
        lax.all_to_all(cotangent, "wid", split_axis=0, concat_axis=1, tiled=True),
    )
    shards = (w_project, w_beta, w_out, w_gate_up, w_down, gain_attn, gain_ffn)
    gathered = (
        lax.all_gather(shards[0], "wid", axis=0, tiled=True),
        lax.all_gather(shards[1], "wid", axis=0, tiled=True),
        lax.all_gather(shards[2], "wid", axis=0, tiled=True),
        lax.all_gather(shards[3], "wid", axis=0, tiled=True),
        lax.all_gather(shards[4], "wid", axis=0, tiled=True),
        lax.all_gather(shards[5], "wid", axis=0, tiled=True),
        lax.all_gather(shards[6], "wid", axis=0, tiled=True),
    )
    project_full, beta_full, out_full, gate_up_full, down_full, gain_one, gain_two = gathered
    seq_len, width = rows.shape
    heads_here = beta_full.shape[1]
    head_size = project_full.shape[2] // heads_here
    positions = jnp.arange(seq_len, dtype=jnp.int32)
    valid = (positions < lengths[0]).astype(jnp.float32)
    gain_one_f = gain_one.astype(jnp.float32)
    gain_two_f = gain_two.astype(jnp.float32)
    source = rows.astype(jnp.float32)
    factor_one = lax.rsqrt(jnp.mean(source * source, axis=-1, keepdims=True) + 1e-06)
    normed_one = (source * factor_one * gain_one_f).astype(jnp.bfloat16)
    project_flat = project_full.reshape(width, -1)
    projected = jnp.dot(normed_one, project_flat, preferred_element_type=jnp.float32).astype(
        jnp.bfloat16
    )
    beta_logit = jnp.dot(normed_one, beta_full, preferred_element_type=jnp.float32)
    parts = projected.reshape(seq_len, 4, heads_here, head_size).astype(jnp.float32)

    def attend(queries, key_rows, value_rows, house_raw, logits):
        return path_attention(queries, key_rows, value_rows, house_raw, logits, valid)

    attended, attend_back = jax.vjp(
        attend, parts[:, 0], parts[:, 1], parts[:, 2], parts[:, 3], beta_logit
    )
    attended_low = attended.reshape(seq_len, heads_here * head_size).astype(jnp.bfloat16)
    attn_part = jnp.einsum("sk,dk->sd", attended_low, out_full, preferred_element_type=jnp.float32)
    attn_sum = lax.psum(attn_part, "hid")
    hidden = source + attn_sum
    factor_two = lax.rsqrt(jnp.mean(hidden * hidden, axis=-1, keepdims=True) + 1e-06)
    normed_two = (hidden * factor_two * gain_two_f).astype(jnp.bfloat16)
    gate_up = jnp.einsum(
        "sd,dgf->sgf", normed_two, gate_up_full, preferred_element_type=jnp.float32
    )
    gate = gate_up[:, 0]
    upward = gate_up[:, 1]
    sigmoid_gate = jax.nn.sigmoid(gate)
    active = gate * sigmoid_gate
    mixed_low = (active * upward).astype(jnp.bfloat16)
    ffn_part = jnp.einsum("sf,df->sd", mixed_low, down_full, preferred_element_type=jnp.float32)
    ffn_sum = lax.psum(ffn_part.astype(jnp.bfloat16), "hid").astype(jnp.float32)
    output_rows = ((hidden + ffn_sum) * valid[:, None]).astype(jnp.bfloat16)
    grad_low = grad_rows * valid[:, None].astype(jnp.bfloat16)
    grad_top = grad_low.astype(jnp.float32)
    grad_mixed = jnp.einsum("sd,df->sf", grad_low, down_full, preferred_element_type=jnp.float32)
    grad_down = jnp.einsum("sd,sf->df", grad_low, mixed_low, preferred_element_type=jnp.float32)
    grad_gate = grad_mixed * upward * sigmoid_gate * (1.0 + gate * (1.0 - sigmoid_gate))
    grad_up = grad_mixed * active
    grad_pair = jnp.stack([grad_gate, grad_up], axis=1).astype(jnp.bfloat16)
    grad_gate_up = jnp.einsum(
        "sd,sgf->dgf", normed_two, grad_pair, preferred_element_type=jnp.float32
    )
    normed_two_part = jnp.einsum(
        "sgf,dgf->sd", grad_pair, gate_up_full, preferred_element_type=jnp.float32
    )
    grad_normed_two = lax.psum(normed_two_part, "hid")
    grad_gain_two = jnp.sum(grad_normed_two * hidden * factor_two, axis=0)
    grad_hidden = grad_top + norm_back(grad_normed_two, hidden, factor_two, gain_two_f)
    grad_branch = grad_hidden.astype(jnp.bfloat16)
    grad_out = jnp.einsum(
        "sd,sk->dk", grad_branch, attended_low, preferred_element_type=jnp.float32
    )
    grad_attended = jnp.einsum(
        "sd,dk->sk", grad_branch, out_full, preferred_element_type=jnp.float32
    ).astype(jnp.bfloat16)
    grad_parts = attend_back(
        grad_attended.astype(jnp.float32).reshape(seq_len, heads_here, head_size)
    )
    grad_projected = jnp.stack(grad_parts[:4], axis=1).reshape(seq_len, -1).astype(jnp.bfloat16)
    grad_logit = grad_parts[4].astype(jnp.bfloat16)
    grad_project = jnp.einsum(
        "sd,sk->dk", normed_one, grad_projected, preferred_element_type=jnp.float32
    ).reshape(project_full.shape)
    grad_beta = jnp.einsum("sd,sh->dh", normed_one, grad_logit, preferred_element_type=jnp.float32)
    normed_one_part = jnp.einsum(
        "sk,dk->sd", grad_projected, project_flat, preferred_element_type=jnp.float32
    )
    normed_one_part = normed_one_part + jnp.einsum(
        "sh,dh->sd", grad_logit, beta_full, preferred_element_type=jnp.float32
    )
    grad_normed_one = lax.psum(normed_one_part.astype(jnp.bfloat16), "hid").astype(jnp.float32)
    grad_gain_one = jnp.sum(grad_normed_one * source * factor_one, axis=0)
    grad_source = grad_hidden + norm_back(grad_normed_one, source, factor_one, gain_one_f)
    output_back, input_back = (
        lax.all_to_all(output_rows, "wid", split_axis=1, concat_axis=0, tiled=True),
        lax.all_to_all(
            grad_source.astype(jnp.bfloat16), "wid", split_axis=1, concat_axis=0, tiled=True
        ),
    )
    gradients = (
        grad_project,
        grad_beta,
        grad_out,
        grad_gate_up,
        grad_down,
        grad_gain_one,
        grad_gain_two,
    )
    reduced = (
        lax.psum_scatter(gradients[0], ("dp", "wid"), scatter_dimension=0, tiled=True),
        lax.psum_scatter(gradients[1], ("dp", "wid"), scatter_dimension=0, tiled=True),
        lax.psum_scatter(gradients[2], ("dp", "wid"), scatter_dimension=0, tiled=True),
        lax.psum_scatter(gradients[3], ("dp", "wid"), scatter_dimension=0, tiled=True),
        lax.psum_scatter(gradients[4], ("dp", "wid"), scatter_dimension=0, tiled=True),
        lax.psum_scatter(gradients[5], ("dp", "wid"), scatter_dimension=0, tiled=True),
        lax.psum_scatter(gradients[6], ("dp", "wid"), scatter_dimension=0, tiled=True),
    )
    return (
        output_back,
        input_back,
        reduced[0],
        reduced[1],
        reduced[2],
        reduced[3],
        reduced[4],
        reduced[5],
        reduced[6],
    )


def solution(mesh):
    return jax.shard_map(
        per_device,
        mesh=mesh,
        in_specs=(
            P("dp", "wid"),
            P("dp", "wid"),
            P(("dp", "wid")),
            P("wid", None, "hid"),
            P("wid", "hid"),
            P("wid", "hid"),
            P("wid", None, "hid"),
            P("wid", "hid"),
            P("wid"),
            P("wid"),
        ),
        out_specs=(
            P("dp", "wid"),
            P("dp", "wid"),
            P(("dp", "wid"), None, "hid"),
            P(("dp", "wid"), "hid"),
            P(("dp", "wid"), "hid"),
            P(("dp", "wid"), None, "hid"),
            P(("dp", "wid"), "hid"),
            P(("dp", "wid")),
            P(("dp", "wid")),
        ),
        check_vma=False,
    )
```

profile of v0, /device:TPU:0, one launch (start us, length us, event | category | flops | bytes accessed | tf_op | source)
XLA Modules:
  0.0 1983.1 jit_solution(2933681333365888468)
XLA Ops:
  7.9 5.3 all-to-all-start
  14.1 13.3 all-gather
  28.7 7.7 all_gather.22
  44.0 64.9 %all-gather.7.cloned.1.call-done = bf16[1536,4,768]{2,1,0:T(4,128)(2,1)} async-done(((bf16[384,4,768]{2,1,0:T(4,128)(2,1)}), bf16[1536,4,768]{2,1,0:T(4,128)(2,1)}) %all-gather.7.cloned.1.call-update) | async-done | bytes 9437200 | tf_op jit(solution)/shard_map/all_gather | solution.py:107
  109.0 9.5 copy.372
  118.5 7.6 convolution_convert_fusion
  135.7 118.1 %custom-call.6 = f32[4,6,1,64,64]{3,4,2,1,0:T(8,128)S(1)} custom-call(f32[4,6,1,64,64]{4,3,2,1,0:T(8,128)S(1)} %add_bitcast_fusion), custom_call_target="InvertDiagBlocksLowerTriangular" | custom-call | tf_op jit(solution)/shard_map/jvp()/triangular_solve | solution.py:38
  280.1 59.8 %while.47 = (s32[]{:T(128)}, f32[6,256,128]{2,1,0:T(8,128)S(1)}, f32[4,6,64,128]{3,2,1,0:T(8,128)S(1)}, f32[4,6,256,128]{3,2,1,0:T(8,128)}, f32[4,6,64,128]{3,2,...) while((s32[]{:T(128)}, f32[6,256,128]{2,1,0:T(8,128)S(1)}, ...), condition=%wide.region_7.8_spmd.clone, body=%wide.region_2.7_spmd.clone.sunk | while | flops 642875968 | bytes 9687163 | solution.py:86
  340.4 4.1 fusion.175
  344.6 5.0 copy.286
  353.8 14.0 all-gather.1
  371.2 119.4 %all-gather.11.cloned.1.call-done = bf16[1536,2,2048]{2,0,1:T(8,128)(2,1)} async-done(((bf16[384,2,2048]{2,0,1:T(8,128)(2,1)}), bf16[1536,2,2048]{2,0,1:T(8,128)(2,1)}) %all-gather.11.cloned.1.call-update) | async-done | bytes 12582928 | tf_op jit(solution)/shard_map/all_gather | solution.py:110
  490.6 9.8 fusion.163
  500.4 62.0 %all-gather.13.cloned.1.call-done = bf16[1536,2048]{1,0:T(8,128)(2,1)} async-done(((bf16[384,2048]{1,0:T(8,128)(2,1)}), bf16[1536,2048]{1,0:T(8,128)(2,1)}) %all-gather.13.cloned.1.call-update) | async-done | bytes 6291472 | tf_op jit(solution)/shard_map/all_gather | solution.py:111
  562.4 6.5 fusion.111
  570.3 7.6 convolution_bitcast_fusion.4
  578.0 6.8 convolution_convert_fusion.1
  584.8 13.7 all-reduce.10.cloned.1.call-done
  611.0 144.7 %while.48 = (s32[]{:T(128)}, f32[6,256,128]{2,1,0:T(8,128)}, f32[6,256,128]{2,1,0:T(8,128)}, f32[4,6,64,128]{3,2,1,0:T(8,128)}, f32[4,6,64,64]{2,3,1,0:T(8,128)}...) while((s32[]{:T(128)}, f32[6,256,128]{2,1,0:T(8,128)}, ...), condition=%wide.region_23.24_spmd.clone.clone.clone, body=%wide.region_13.0_spmd.clone.clone.clone.sunk | while | flops 1778783744 | bytes 42850756 | solution.py:86
  807.8 5.8 fusion.203
  816.6 9.6 fusion.204
  827.6 12.2 fusion.96
  840.5 4.8 fusion.140
  849.1 8.7 fusion.109
  861.1 3.9 all-to-all-start.3
  867.4 9.2 all-to-all-done.3
  881.4 87.3 %reduce-scatter.16.cloned.1.call-done = f32[96,6]{1,0:T(8,128)} async-done(((f32[1536,6]{1,0:T(8,128)}), f32[96,6]{1,0:T(8,128)}) %reduce-scatter.16.cloned.1.call-update) | async-done | bytes 2320
  970.1 79.1 %all-reduce.2 = (f32[1536]{0:T(1024)S(1)}, f32[1536]{0:T(1024)S(1)}) all-reduce(f32[1536]{0:T(1024)S(1)} %get-tuple-element.1040, f32[1536]{0:T(1024)S(1)} %copy-done.86), channel_id=7, replica_groups=mesh['dp'=4,'hid'=2,'wid'=4] {'dp','wid'}, use_global_device_ids=true, to_apply=%region_35.37.clone | all-reduce | flops 3072 | bytes 24576
  1050.4 208.8 %reduce-scatter.8.cloned.1.call-done = f32[96,4,768]{2,0,1:T(8,128)} async-done(((f32[1536,4,768]{2,0,1:T(8,128)}), f32[96,4,768]{2,0,1:T(8,128)}) %reduce-scatter.8.cloned.1.call-update) | async-done | bytes 1179664 | tf_op jit(solution)/shard_map/reduce_scatter | solution.py:213
  1262.2 360.3 %reduce-scatter.12.cloned.1.call-done = f32[96,2,2048]{2,0,1:T(8,128)} async-done(((f32[1536,2,2048]{2,0,1:T(8,128)}), f32[96,2,2048]{2,0,1:T(8,128)}) %reduce-scatter.12.cloned.1.call-update) | async-done | bytes 1572880 | tf_op jit(solution)/shard_map/reduce_scatter | solution.py:216
  1626.3 140.0 %reduce-scatter.10.cloned.1.call-done = f32[96,768]{1,0:T(8,128)} async-done(((f32[1536,768]{1,0:T(8,128)}), f32[96,768]{1,0:T(8,128)}) %reduce-scatter.10.cloned.1.call-update) | async-done | bytes 294928 | tf_op jit(solution)/shard_map/reduce_scatter | solution.py:215
  1766.3 207.8 %reduce-scatter.14.cloned.1.call-done = f32[96,2048]{1,0:T(8,128)} async-done(((f32[1536,2048]{1,0:T(8,128)}), f32[96,2048]{1,0:T(8,128)}) %reduce-scatter.14.cloned.1.call-update) | async-done | bytes 786448 | tf_op jit(solution)/shard_map/reduce_scatter | solution.py:217
  (624 shorter events, 345.5 us)
Async XLA Ops:
  7.2 101.8 %all-gather.7.cloned.1.call-start = ((), (), s32[]{:S(2)}) async-start(), calls=%async_computation.9 | async-start | bytes 11796480 | tf_op jit(solution)/shard_map/all_gather | solution.py:107
  7.9 6.1 copy-start.94
  7.9 20.7 %copy-start.90 = (bf16[384,6]{0,1:T(8,128)(2,1)S(1)}, bf16[384,6]{0,1:T(8,128)(2,1)}, u32[]{:S(2)}) copy-start(bf16[384,6]{0,1:T(8,128)(2,1)} %param.20) | copy-start | bytes 13828
  7.9 30.4 %all-to-all-start = ((bf16[4,256,384]{2,1,0:T(8,128)(2,1)}), bf16[4,256,384]{2,1,0:T(8,128)(2,1)S(1)}, u32[]{:S(2)}, u32[]{:S(2)}) async-start(bf16[4,256,384]{2,1,0:T(8,128)(2,1)} %bitcast), calls=%async_computation | async-start | bytes 1572864 | tf_op jit(solution)/shard_map/all_to_all | solution.py:102
  13.3 327.2 %all-gather.9.cloned.1.call-start = ((), (), s32[]{:S(2)}) async-start(), calls=%async_computation.10 | async-start | bytes 2949120 | tf_op jit(solution)/shard_map/all_gather | solution.py:109
  14.0 355.1 %all-reduce.8.cloned.1.call-start = ((), (), s32[]{:S(2)}) async-start(), calls=%async_computation.11 | async-start | bytes 3145728 | tf_op jit(solution)/shard_map/psum | solution.py:141
  28.6 14.2 copy-start.72
  36.4 6.5 copy-start.70
  36.4 97.0 %copy-start.61 = (f32[64,64]{1,0:T(8,128)}, f32[64,64]{1,0:T(8,128)S(1)}, u32[]{:S(2)}) copy-start(f32[64,64]{1,0:T(8,128)S(1)} %fusion.159) | copy-start | bytes 49156
  42.9 75.6 %copy-start.28 = (bf16[4,256,384]{1,2,0:T(8,128)(2,1)}, bf16[4,256,384]{1,2,0:T(8,128)(2,1)S(1)}, u32[]{:S(2)}) copy-start(bf16[4,256,384]{1,2,0:T(8,128)(2,1)S(1)} %multiply_convert_fusion.4) | copy-start | bytes 2359300
  256.2 8.3 copy-start.23
  260.5 8.7 copy-start.13
  263.6 12.7 copy-start.15
  344.6 146.1 %all-gather.11.cloned.1.call-start = ((), (), s32[]{:S(2)}) async-start(), calls=%async_computation.12 | async-start | bytes 15728640 | tf_op jit(solution)/shard_map/all_gather | solution.py:110
  349.6 212.8 %all-gather.13.cloned.1.call-start = ((), (), s32[]{:S(2)}) async-start(), calls=%async_computation.13 | async-start | bytes 7864320 | tf_op jit(solution)/shard_map/all_gather | solution.py:111
  350.2 17.7 all-to-all-start.2
  353.7 244.7 %all-reduce.10.cloned.1.call-start = ((), (), s32[]{:S(2)}) async-start(), calls=%async_computation.14 | async-start | bytes 3145728 | tf_op jit(solution)/shard_map/psum | solution.py:169
  367.9 233.1 %copy-start.68 = (f32[1536]{0:T(1024)}, f32[1536]{0:T(1024)S(1)}, u32[]{:S(2)}) copy-start(f32[1536]{0:T(1024)S(1)} %reshape.388) | copy-start | bytes 18436
  367.9 233.1 %copy-start.92 = (bf16[256]{0:T(256)(128)(2,1)}, bf16[256]{0:T(256)(128)(2,1)S(1)}, u32[]{:S(2)}) copy-start(bf16[256]{0:T(256)(128)(2,1)S(1)} %fusion.168) | copy-start | bytes 1540
  371.2 229.8 %copy-start = (f32[256,1536]{1,0:T(8,128)}, f32[256,1536]{1,0:T(8,128)S(1)}, u32[]{:S(2)}) copy-start(f32[256,1536]{1,0:T(8,128)S(1)} %get-tuple-element.1119) | copy-start | bytes 4718596
  371.2 229.8 %copy-start.81 = (f32[256]{0:T(256)}, f32[256]{0:T(256)S(1)}, u32[]{:S(2)}) copy-start(f32[256]{0:T(256)S(1)} %get-tuple-element.1149) | copy-start | bytes 3076
  577.9 279.9 %all-reduce.12.cloned.1.call-start = ((), (), s32[]{:S(2)}) async-start(), calls=%async_computation.20 | async-start | bytes 3145728 | tf_op jit(solution)/shard_map/psum | solution.py:154
  807.8 5.9 copy-start.71
  815.0 153.6 %reduce-scatter.16.cloned.1.call-start = ((), (), s32[]{:S(2)}) async-start(), calls=%async_computation.19 | async-start | bytes 835584
  816.5 442.7 %reduce-scatter.8.cloned.1.call-start = ((), (), s32[]{:S(2)}) async-start(), calls=%async_computation.15 | async-start | bytes 20054016 | tf_op jit(solution)/shard_map/reduce_scatter | solution.py:213
  826.3 796.3 %reduce-scatter.12.cloned.1.call-start = ((), (), s32[]{:S(2)}) async-start(), calls=%async_computation.17 | async-start | bytes 26738688 | tf_op jit(solution)/shard_map/reduce_scatter | solution.py:216
  839.9 926.4 %reduce-scatter.10.cloned.1.call-start = ((), (), s32[]{:S(2)}) async-start(), calls=%async_computation.16 | async-start | bytes 5013504 | tf_op jit(solution)/shard_map/reduce_scatter | solution.py:215
  845.3 1128.8 %reduce-scatter.14.cloned.1.call-start = ((), (), s32[]{:S(2)}) async-start(), calls=%async_computation.18 | async-start | bytes 13369344 | tf_op jit(solution)/shard_map/reduce_scatter | solution.py:217
  861.1 15.5 all-to-all-start.3
  866.4 13.7 copy-start.96
  866.4 103.7 %copy-start.86 = (f32[1536]{0:T(1024)S(1)}, f32[1536]{0:T(1024)}, u32[]{:S(2)}) copy-start(f32[1536]{0:T(1024)} %get-tuple-element.1038) | copy-start | bytes 18436
  876.6 173.8 %all-to-all-start.1 = ((bf16[256,4,384]{2,0,1:T(8,128)(2,1)}), bf16[256,4,384]{2,0,1:T(8,128)(2,1)S(1)}, u32[]{:S(2)}, u32[]{:S(2)}) async-start(bf16[256,4,384]{2,0,1:T(8,128)(2,1)} %bitcast.331), calls=%async_computation.1 | async-start | bytes 1572864 | tf_op jit(solution)/shard_map/all_to_all | solution.py:198
  (105 other events, 243.8 us)
Sparse Core Ops, SparseCore 0:
  9.8 99.1 all-gather.6
  110.8 37.5 all-gather.8
  344.7 20.5 all-reduce.7
  367.0 123.5 all-gather.10
  492.3 70.0 all-gather.12
  578.0 20.3 all-reduce.9
  815.2 21.6 all-reduce.11
  842.1 126.4 reduce-scatter.15
  974.4 284.7 reduce-scatter.7
  1264.8 357.7 reduce-scatter.11
  1628.3 137.9 reduce-scatter.9
  1772.4 201.6 reduce-scatter.13
where the time goes:
time: 1990 us; the launch traced here: 1980 us
  waiting for transfers between devices  1280 us (64%)
  matrix products  248 us (12%)
  other arithmetic  175 us (9%)
  local copies, waits for them, and re-layouts  129 us (6%)
  blocking collectives  114 us (6%)
    reduce_scatter x1, waiting for transfers between devices, per_device(): lax.psum_scatter(gradients[3], ('dp', 'wid'), scatter_dimension=0, tiled=...  360 us
    reduce_scatter x1, waiting for transfers between devices, per_device(): lax.psum_scatter(gradients[0], ('dp', 'wid'), scatter_dimension=0, tiled=...  209 us
    reduce_scatter x1, waiting for transfers between devices, per_device(): lax.psum_scatter(gradients[4], ('dp', 'wid'), scatter_dimension=0, tiled=...  208 us
    reduce_scatter x1, waiting for transfers between devices, per_device(): lax.psum_scatter(gradients[2], ('dp', 'wid'), scatter_dimension=0, tiled=...  140 us
    another operation x5, other arithmetic, path_attention(): lax.linalg.triangular_solve(system, diagonal, left_side=True, lower=True,...  120 us
    all_gather x1, waiting for transfers between devices, per_device(): lax.all_gather(shards[3], 'wid', axis=0, tiled=True)  119 us
    unnamed x13, waiting for transfers between devices  89.4 us
    unnamed x1, blocking collectives  79.1 us
  transfers between devices with their start and end apart: 16, of which 10 were waited for; matrix products, arithmetic and copies ran while one was open for 16% of the time, Pallas kernels for 0%

commit v1 on v0

v1 whole, which is shorter than its diff:
```python
import functools

import jax
import jax.numpy as jnp
from jax import lax
from jax.experimental import pallas as pl
from jax.experimental.pallas import tpu as pltpu
from jax.sharding import PartitionSpec as P

f32 = jnp.float32
bf16 = jnp.bfloat16

SEQ = 256
HD = 128


def dot_of(a, b, ca, cb):
    return lax.dot_general(a, b, (((ca,), (cb,)), ((), ())), preferred_element_type=f32)


def halves_of(a):
    high = a.astype(bf16)
    return high, (a - high.astype(f32)).astype(bf16)


def mul(a, b, ca=1, cb=0, passes=3):
    if passes == 1:
        return dot_of(a.astype(bf16), b.astype(bf16), ca, cb)
    if a.dtype == bf16:
        bh, bl = halves_of(b)
        return dot_of(a, bh, ca, cb) + dot_of(a, bl, ca, cb)
    if b.dtype == bf16:
        ah, al = halves_of(a)
        return dot_of(ah, b, ca, cb) + dot_of(al, b, ca, cb)
    ah, al = halves_of(a)
    bh, bl = halves_of(b)
    return dot_of(ah, bh, ca, cb) + (dot_of(ah, bl, ca, cb) + dot_of(al, bh, ca, cb))


def iotas():
    rows = lax.broadcasted_iota(jnp.int32, (SEQ, SEQ), 0)
    cols = lax.broadcasted_iota(jnp.int32, (SEQ, SEQ), 1)
    return rows, cols


def prepare(raw, logit_row, i, j):
    eye = i == j
    raw_f = raw.astype(f32)
    norm = lax.rsqrt(jnp.sum(raw_f * raw_f, axis=1, keepdims=True) + 1e-6)
    norm_row = jnp.sum(jnp.where(eye, norm, 0.0), axis=0, keepdims=True)
    beta_row = 2.0 / (1.0 + jnp.exp(-logit_row))
    beta = jnp.sum(jnp.where(eye, beta_row, 0.0), axis=1, keepdims=True)
    return raw_f, norm, norm_row, beta_row, beta


def inverses(lowers, i, j):
    eye = jnp.where(i == j, 1.0, 0.0)
    first = ((i >> 1) == (j >> 1)) & (i > j)
    inv = [eye - jnp.where(first, n, 0.0) for n in lowers]
    s = 1
    while (1 << s) < SEQ:
        mask = ((i >> (s + 1)) == (j >> (s + 1))) & ((i >> s) > (j >> s))
        mids = [mul(d, jnp.where(mask, n, 0.0)) for d, n in zip(inv, lowers)]
        inv = [d - mul(x, d) for d, x in zip(inv, mids)]
        s += 1
    return inv


def forward_kernel(count, len_ref, x_ref, l_ref, o_ref, inv_ref, carry_ref, prob_ref):
    base = pl.program_id(0) * count
    i, j = iotas()
    row = lax.broadcasted_iota(jnp.int32, (SEQ, 1), 0)
    xs = [x_ref[t] for t in range(count)]
    qs = [x[:, 0:HD] for x in xs]
    ks = [x[:, HD : 2 * HD] for x in xs]
    vs = [x[:, 2 * HD : 3 * HD] for x in xs]
    us = [x[:, 3 * HD : 4 * HD] for x in xs]
    pre = [prepare(us[t], l_ref[t], i, j) for t in range(count)]
    lowers = [
        p[4] * jnp.where(i > j, dot_of(u, u, 1, 1) * p[1] * p[2], 0.0) for u, p in zip(us, pre)
    ]
    inv = inverses(lowers, i, j)
    bs = [jnp.where(i > j, dot_of(u, k, 1, 1) * p[1], 0.0) for u, k, p in zip(us, ks, pre)]
    carries = [mul(d * p[3], b) for d, p, b in zip(inv, pre, bs)]
    as_ = [jnp.where(i >= j, dot_of(q, u, 1, 1) * p[2], 0.0) for q, u, p in zip(qs, us, pre)]
    scores = [
        (dot_of(q, k, 1, 1) - mul(a, c)) * (HD**-0.5) for q, k, a, c in zip(qs, ks, as_, carries)
    ]
    for t in range(count):
        length = len_ref[base + t]
        score = jnp.where((j <= i) & (j < length), scores[t], -1e30)
        weight = jnp.exp(score - jnp.max(score, axis=1, keepdims=True))
        prob = weight * (1.0 / jnp.sum(weight, axis=1, keepdims=True))
        out = jnp.where(row < length, mul(prob, vs[t], passes=1), 0.0)
        o_ref[t] = out.astype(bf16)
        inv_ref[t] = inv[t]
        carry_ref[t] = carries[t]
        prob_ref[t] = prob


def backward_kernel(
    count, len_ref, x_ref, l_ref, inv_ref, carry_ref, prob_ref, do_ref, dx_ref, dl_ref
):
    base = pl.program_id(0) * count
    i, j = iotas()
    row = lax.broadcasted_iota(jnp.int32, (SEQ, 1), 0)
    for t in range(count):
        x = x_ref[t]
        q, k = x[:, 0:HD], x[:, HD : 2 * HD]
        v, u = x[:, 2 * HD : 3 * HD], x[:, 3 * HD : 4 * HD]
        do = do_ref[t]
        do = jnp.where(row < len_ref[base + t], do, jnp.zeros_like(do))
        inv, carry, prob = inv_ref[t], carry_ref[t], prob_ref[t]
        raw, norm, norm_row, beta_row, beta = prepare(u, l_ref[t], i, j)
        gram = jnp.where(i > j, dot_of(u, u, 1, 1) * norm * norm_row, 0.0)
        a = jnp.where(i >= j, dot_of(q, u, 1, 1) * norm_row, 0.0)
        b = jnp.where(i > j, dot_of(u, k, 1, 1) * norm, 0.0)
        m = inv * beta_row
        dv = mul(prob, do, 0, 0, passes=1)
        dprob = dot_of(do, v, 1, 1)
        ds = prob * (dprob - jnp.sum(dprob * prob, axis=1, keepdims=True)) * (HD**-0.5)
        da = jnp.where(i >= j, -mul(ds, carry, 1, 1), 0.0)
        dc = -mul(a, ds, 0, 0)
        dm = mul(dc, b, 1, 1)
        db = jnp.where(i > j, mul(m, dc, 0, 0), 0.0)
        dn = jnp.where(i > j, -mul(mul(inv, dm, 0, 0), m, 1, 1), 0.0)
        dgram = beta * dn
        dbeta = jnp.sum(dm * inv, axis=0, keepdims=True)
        dbeta_col = jnp.sum(dn * gram, axis=1, keepdims=True)
        dbeta = dbeta + jnp.sum(jnp.where(i == j, dbeta_col, 0.0), axis=0, keepdims=True)
        dq = mul(ds, k, passes=1) + mul(da * norm_row, u, passes=1)
        dk = mul(ds, q, 0, 0, passes=1) + mul(db * norm, u, 0, 0, passes=1)
        dw = mul(da, q, 0, 0, passes=1) + mul(db, k, passes=1)
        dw = dw + mul(dgram * norm_row, u, passes=1) + mul(dgram * norm, u, 0, 0, passes=1)
        du = norm * dw - (norm * norm * norm) * raw * jnp.sum(dw * raw, axis=1, keepdims=True)
        dx_ref[t] = jnp.concatenate([dq, dk, dv, du], axis=1).astype(bf16)
        dl_ref[t] = dbeta * beta_row * (1.0 - 0.5 * beta_row)


def block_of(count, *shape):
    return pl.BlockSpec((count,) + shape, lambda g, lens: (g, 0, 0))


def attention_forward(lens, x, logits, count=3):
    pairs = x.shape[0]
    square = jax.ShapeDtypeStruct((pairs, SEQ, SEQ), f32)
    return pl.pallas_call(
        functools.partial(forward_kernel, count),
        out_shape=[jax.ShapeDtypeStruct((pairs, SEQ, HD), bf16), square, square, square],
        grid_spec=pltpu.PrefetchScalarGridSpec(
            num_scalar_prefetch=1,
            grid=(pairs // count,),
            in_specs=[block_of(count, SEQ, 4 * HD), block_of(count, 1, SEQ)],
            out_specs=[block_of(count, SEQ, HD)] + [block_of(count, SEQ, SEQ)] * 3,
        ),
        compiler_params=pltpu.CompilerParams(vmem_limit_bytes=48 << 20),
        cost_estimate=pl.CostEstimate(
            flops=pairs * 1600000000, bytes_accessed=pairs * 1100000, transcendentals=pairs * 65536
        ),
    )(lens, x, logits)


def attention_backward(lens, x, logits, inv, carry, prob, do, count=1):
    pairs = x.shape[0]
    return pl.pallas_call(
        functools.partial(backward_kernel, count),
        out_shape=[
            jax.ShapeDtypeStruct((pairs, SEQ, 4 * HD), bf16),
            jax.ShapeDtypeStruct((pairs, 1, SEQ), f32),
        ],
        grid_spec=pltpu.PrefetchScalarGridSpec(
            num_scalar_prefetch=1,
            grid=(pairs // count,),
            in_specs=[block_of(count, SEQ, 4 * HD), block_of(count, 1, SEQ)]
            + [block_of(count, SEQ, SEQ)] * 3
            + [block_of(count, SEQ, HD)],
            out_specs=[block_of(count, SEQ, 4 * HD), block_of(count, 1, SEQ)],
        ),
        compiler_params=pltpu.CompilerParams(vmem_limit_bytes=48 << 20),
        cost_estimate=pl.CostEstimate(
            flops=pairs * 1400000000, bytes_accessed=pairs * 1400000, transcendentals=pairs * 512
        ),
    )(lens, x, logits, inv, carry, prob, do)


def swap(x, axis, size, k):
    return lax.ppermute(x, axis, [(n, n ^ k) for n in range(size)])


def shift_rows(x, start, size):
    return lax.dynamic_slice_in_dim(x, start, size, axis=0)


def shift_cols(x, start, size):
    return lax.dynamic_slice_in_dim(x, start, size, axis=x.ndim - 1)


def mm(a, b, ca=1, cb=0):
    return dot_of(a, b, ca, cb)


def per_device(
    dp_size,
    wid_size,
    tokens,
    cotangent,
    lengths,
    w_project,
    w_beta,
    w_out,
    w_gate_up,
    w_down,
    gain_attn,
    gain_ffn,
):
    wid = lax.axis_index("wid")
    hid = lax.axis_index("hid")
    dp = lax.axis_index("dp")
    ws = range(wid_size)
    rows, part = tokens.shape
    half = rows // 2
    width = part * wid_size
    ff = w_down.shape[1] // wid_size
    heads = w_beta.shape[1]
    per_half = half // SEQ

    def wid_all(x):
        return [x] + [swap(x, "wid", wid_size, k) for k in ws if k > 0]

    def wid_to(pieces):
        return [pieces[0]] + [swap(pieces[k], "wid", wid_size, k) for k in ws if k > 0]

    def hid_swap(x):
        return swap(x, "hid", 2, 1)

    def head_a(w):
        return (3 * w + 1) // 2

    def head_b(w):
        return 1 + 3 * (w // 2)

    half_b = (wid & 1) ^ hid

    def own_rows(x):
        return shift_rows(x, hid * half, half)

    len_rel = jnp.concatenate(wid_all(lengths))
    len_of = [lax.dynamic_index_in_dim(len_rel, b ^ wid, keepdims=False) for b in ws]
    len_abs = jnp.stack(len_of)
    gains = wid_all(jnp.stack([gain_attn, gain_ffn]))
    gain_one_full = jnp.concatenate([g[0] for g in gains])[None].astype(f32)
    beta_full = jnp.concatenate(wid_all(w_beta), axis=0)

    def gather_rows(x):
        mine = own_rows(x)
        other = shift_rows(x, (1 - hid) * half, half)
        got = [swap(mine, "wid", wid_size, k) for k in ws if k > 0]
        far = [hid_swap(g) for g in got]
        return jnp.concatenate(
            [jnp.concatenate([mine] + got, axis=1), jnp.concatenate([other] + far, axis=1)], axis=0
        )

    x_full = gather_rows(tokens)
    project_flat = w_project.reshape(part, 4, heads, HD)

    def head_of(h):
        piece = lax.dynamic_index_in_dim(project_flat, h, axis=2, keepdims=False)
        return piece.reshape(part, 4 * HD)

    proj_a = jnp.concatenate(wid_to([head_of(head_a(wid ^ k)) for k in ws]), axis=0)
    proj_b = jnp.concatenate(wid_to([head_of(head_b(wid ^ k)) for k in ws]), axis=0)
    gate_up_w = jnp.concatenate(
        wid_to([shift_cols(w_gate_up, (wid ^ k) * ff, ff).reshape(part, 2 * ff) for k in ws]),
        axis=0,
    )
    g_raw = gather_rows(cotangent)
    down_w = jnp.concatenate(
        wid_to([shift_cols(w_down, (wid ^ k) * ff, ff) for k in ws]), axis=0
    )
    out_w = jnp.concatenate(
        [shift_cols(w_out, head_a(wid ^ k) * HD, HD) for k in ws]
        + [shift_cols(w_out, head_b(wid ^ (2 * q)) * HD, HD) for q in range(wid_size // 2)],
        axis=1,
    )

    def bucket_len(place, t):
        return lax.dynamic_index_in_dim(len_abs, (hid ^ place) * per_half + t, keepdims=False)

    lens_a = [bucket_len(p, t) for p in range(2) for t in range(per_half)]
    lens_b = [
        lax.dynamic_index_in_dim(len_abs, (wid & 1) * per_half + t, keepdims=False)
        for t in range(per_half)
    ]
    lens = jnp.stack(lens_a + lens_b)
    slot = jnp.arange(SEQ, dtype=jnp.int32)
    valid_rows = jnp.concatenate([(slot < n).astype(f32) for n in lens_a])[:, None]
    valid_half = valid_rows[:half]

    x_f = x_full.astype(f32)
    factor_one = lax.rsqrt(jnp.mean(x_f * x_f, axis=1, keepdims=True) + 1e-6)
    normed_one = (x_f * factor_one * gain_one_full).astype(bf16)
    normed_b = shift_rows(normed_one, half_b * half, half)
    pa = mm(normed_one, proj_a).astype(bf16)
    pb = mm(normed_b, proj_b).astype(bf16)
    pairs = jnp.concatenate([pa, pb], axis=0).reshape(-1, SEQ, 4 * HD)
    beta_w = jnp.concatenate(
        [shift_cols(beta_full, head_a(wid), 1), shift_cols(beta_full, head_b(wid), 1)], axis=1
    )
    logits = mm(beta_w, normed_one, 0, 1)
    logit_b = shift_cols(logits[1:2], half_b * half, half)
    logit_pairs = jnp.concatenate([logits[0:1], logit_b], axis=1).reshape(-1, 1, SEQ)
    attended, inv, carry, prob = attention_forward(lens, pairs, logit_pairs)

    o_all = wid_all(attended.reshape(-1, HD))
    pair_rows = []
    for q in range(wid_size // 2):
        one, two = o_all[2 * q][rows:], o_all[2 * q + 1][rows:]
        first = jnp.where(half_b == 0, one, two)
        second = jnp.where(half_b == 0, two, one)
        pair_rows.append(jnp.concatenate([first, second], axis=0))
    o_cat = jnp.concatenate([o[:rows] for o in o_all] + pair_rows, axis=1)
    attn_part = mm(o_cat, out_w, 1, 1)
    attn_half = attn_part[:half] + hid_swap(attn_part[half:])
    hidden = own_rows(tokens).astype(f32) + attn_half

    def row_mean(x):
        own = jnp.sum(x, axis=1).reshape(-1, 128)
        total = own
        for k in ws:
            if k > 0:
                total = total + swap(own, "wid", wid_size, k)
        return total.reshape(-1, 1) * (1.0 / width)

    gain_one = gain_attn[None].astype(f32)
    gain_two = gain_ffn[None].astype(f32)
    factor_two = lax.rsqrt(row_mean(hidden * hidden) + 1e-6)
    normed_half = (hidden * factor_two * gain_two).astype(bf16)
    n_got = jnp.concatenate(wid_all(normed_half), axis=1)
    normed_two = jnp.concatenate([n_got, hid_swap(n_got)], axis=0)
    grad_full = jnp.where(valid_rows > 0.5, g_raw, jnp.zeros_like(g_raw))
    gate_up = mm(normed_two, gate_up_w)
    gate, upward = gate_up[:, :ff], gate_up[:, ff:]
    sigmoid_gate = jax.nn.sigmoid(gate)
    active = gate * sigmoid_gate
    mixed = (active * upward).astype(bf16)
    grad_mixed = mm(grad_full, down_w)
    grad_gate = grad_mixed * upward * sigmoid_gate * (1.0 + gate * (1.0 - sigmoid_gate))
    grad_pair = jnp.concatenate([grad_gate, grad_mixed * active], axis=1).astype(bf16)

    def scatter_rows(x):
        low = x.astype(bf16)
        mine = x[:half] + hid_swap(low[half:]).astype(f32)
        sent = mine.astype(bf16)
        pieces = [sent[:, k * part : (k + 1) * part] for k in ws]
        total = mine[:, :part]
        for k in ws:
            if k > 0:
                total = total + swap(pieces[k], "wid", wid_size, k).astype(f32)
        return total

    grad_normed_two = scatter_rows(mm(grad_pair, gate_up_w, 1, 1))

    def dp_sum(pieces):
        k = 1
        held = list(pieces)
        while k < dp_size:
            keep = held[0::2]
            send = jnp.stack([h.astype(bf16) for h in held[1::2]])
            got = swap(send, "dp", dp_size, k)
            held = [a.astype(f32) + got[n].astype(f32) for n, a in enumerate(keep)]
            k *= 2
        return held[0]

    chunk = width // dp_size

    def dp_rows(x):
        low = x.astype(bf16)
        out = []
        for t in range(dp_size):
            row = (dp ^ t) * chunk
            start = ((row // part) ^ wid) * part + row % part
            out.append(shift_rows(low, start, chunk))
        return dp_sum(out)

    sub = chunk // wid_size

    def to_rows(x):
        low = x.astype(bf16)
        return wid_to([shift_rows(low, (wid ^ k) * sub, sub) for k in ws])

    g_down = dp_rows(mm(grad_full, mixed, 0, 0))
    g_gate_up = dp_rows(mm(normed_two, grad_pair, 0, 0))

    scaled = grad_normed_two * gain_two
    mean_two = row_mean(scaled * hidden)
    grad_half = own_rows(cotangent).astype(f32) * valid_half
    grad_hidden = grad_half + factor_two * scaled - (factor_two**3) * hidden * mean_two
    gain_two_part = jnp.sum(grad_normed_two * hidden * factor_two, axis=0)
    da_half = grad_hidden.astype(bf16)
    da = jnp.concatenate([da_half, hid_swap(da_half)], axis=0)
    do_part = mm(da, out_w).astype(bf16)
    do_pieces = []
    for k in ws:
        col = (wid_size + k // 2) * HD
        piece_b = shift_rows(do_part[:, col : col + HD], ((k & 1) ^ half_b) * half, half)
        do_pieces.append(jnp.concatenate([do_part[:, k * HD : (k + 1) * HD], piece_b], axis=0))
    do_sum = sum(d.astype(f32) for d in wid_to(do_pieces)).astype(bf16)
    grad_pairs, grad_logits = attention_backward(
        lens, pairs, logit_pairs, inv, carry, prob, do_sum.reshape(-1, SEQ, HD)
    )
    g_out = mm(da, o_cat, 0, 0)

    grad_pairs = grad_pairs.reshape(-1, 4 * HD)
    flat_logits = grad_logits.reshape(1, -1).astype(bf16)

    def spread(x):
        zero = jnp.zeros_like(x)
        return jnp.concatenate(
            [jnp.where(half_b == 0, x, zero), jnp.where(half_b == 0, zero, x)], axis=0
        )

    logit_a = flat_logits[:, :rows]
    logit_full = jnp.concatenate([logit_a, spread(flat_logits[:, rows:].T).T], axis=0)
    d_all = jnp.concatenate([grad_pairs[:rows], spread(grad_pairs[rows:])], axis=1)
    w_all = jnp.concatenate([proj_a, proj_b], axis=1)
    n1_part = mm(d_all, w_all, 1, 1) + mm(logit_full, beta_w, 0, 1)
    grad_normed_one = scatter_rows(n1_part)
    g_proj = dp_rows(mm(normed_one, d_all, 0, 0))
    g_beta = mm(logit_full, normed_one, 1, 0)

    scaled_one = grad_normed_one * gain_one
    source = own_rows(tokens).astype(f32)
    factor_half = factor_one[:half]
    mean_one = row_mean(scaled_one * source)
    gain_one_part = jnp.sum(grad_normed_one * source * factor_half, axis=0)
    input_half = grad_hidden + factor_half * scaled_one - (factor_half**3) * source * mean_one

    def whole_rows(x):
        other = hid_swap(x)
        return jnp.concatenate(
            [jnp.where(hid == 0, x, other), jnp.where(hid == 0, other, x)], axis=0
        )

    input_grad = whole_rows(input_half.astype(bf16))
    ffn = scatter_rows(mm(mixed, down_w, 1, 1))
    output = whole_rows(((hidden + ffn) * valid_half).astype(bf16))

    def place(pieces):
        stacked = jnp.stack(pieces)
        return [lax.dynamic_index_in_dim(stacked, n ^ wid, keepdims=False) for n in ws]

    down_rows = place(to_rows(g_down))
    out_down = jnp.concatenate(down_rows, axis=1).astype(f32)
    gu_rows = place([r.reshape(sub, 2, ff) for r in to_rows(g_gate_up)])
    out_gate_up = jnp.concatenate(gu_rows, axis=2).astype(f32)

    def heads_of(got, size):
        a = [g[..., :size].astype(f32) for g in got]
        b = [g[..., size:].astype(f32) for g in got]
        return [a[0], b[0] + b[1], a[1], a[2], b[2] + b[3], a[3]]

    proj_rows = heads_of(place(to_rows(g_proj)), 4 * HD)
    out_project = jnp.concatenate([p.reshape(sub, 4, HD) for p in proj_rows], axis=2)

    beta_low = dp_rows(jnp.concatenate([g_beta.T, jnp.zeros((width, 126), f32)], axis=1))
    out_beta = jnp.concatenate(heads_of([b[:, :2] for b in place(to_rows(beta_low))], 1), axis=1)

    fine = part // dp_size
    to_place = [
        (c * wid_size + w, w * dp_size + c) for c in range(dp_size) for w in range(wid_size)
    ]

    def dp_fine(x):
        pieces = [shift_rows(x, (dp ^ t) * fine, fine) for t in range(dp_size)]
        return dp_sum(pieces)

    head_cols = [0 ^ wid, wid_size + (wid // 2), 1 ^ wid, 2 ^ wid, wid_size + (1 ^ (wid // 2)), 3 ^ wid]
    out_sum = dp_fine(g_out)
    out_sum = jnp.concatenate([shift_cols(out_sum, h * HD, HD) for h in head_cols], axis=1)
    out_out = lax.ppermute(out_sum, ("dp", "wid"), to_place)

    gain_part = jnp.stack([gain_one_part, gain_two_part], axis=1)
    gain_part = gain_part + hid_swap(gain_part)
    gain_sum = lax.ppermute(dp_fine(gain_part), ("dp", "wid"), to_place)

    return (
        output,
        input_grad,
        out_project,
        out_beta,
        out_out,
        out_gate_up,
        out_down,
        gain_sum[:, 0],
        gain_sum[:, 1],
    )


def solution(mesh):
    return jax.shard_map(
        functools.partial(per_device, mesh.shape["dp"], mesh.shape["wid"]),
        mesh=mesh,
        in_specs=(
            P("dp", "wid"),
            P("dp", "wid"),
            P(("dp", "wid")),
            P("wid", None, "hid"),
            P("wid", "hid"),
            P("wid", "hid"),
            P("wid", None, "hid"),
            P("wid", "hid"),
            P("wid"),
            P("wid"),
        ),
        out_specs=(
            P("dp", "wid"),
            P("dp", "wid"),
            P(("dp", "wid"), None, "hid"),
            P(("dp", "wid"), "hid"),
            P(("dp", "wid"), "hid"),
            P(("dp", "wid"), None, "hid"),
            P(("dp", "wid"), "hid"),
            P(("dp", "wid")),
            P(("dp", "wid")),
        ),
        check_vma=False,
    )
```

time: 1990 us -> 580 us (0.29)
  waiting for transfers between devices: 1280 us -> 239 us
  matrix products: 248 us -> 44.1 us
  blocking collectives: 114 us -> 0 us
  other arithmetic: 175 us -> 77.2 us
  starting transfers between devices: 17 us -> 111 us
  local copies, waits for them, and re-layouts: 129 us -> 66.8 us
  Pallas kernels: 0 us -> 29.5 us
    reduce_scatter x4 -> x0, waiting for transfers between devices: 917 us -> none  [the longest x1 360 us: per_device(): lax.psum_scatter(gradients[3], ('dp', 'wid'), scatter_dimension=0, tiled=...]
    all_gather x4 -> x0, waiting for transfers between devices: 246 us -> none  [the longest x1 119 us: per_device(): lax.all_gather(shards[3], 'wid', axis=0, tiled=True)]
    ppermute x0 -> x95, waiting for transfers between devices: none -> 239 us  [the longest x93 239 us: swap(): return lax.ppermute(x, axis, [(n, n ^ k) for n in range(size)])]
    dot_general x118 -> x16, matrix products: 241 us -> 44.1 us  [dot_of(): lax.dot_general(a, b, (((ca,), (cb,)), ((), ())), preferred_element_type=...]
    another operation x11 -> x18, other arithmetic: 124 us -> 10.1 us  [the longest x12 6.14 us: dp_sum(): send = jnp.stack([h.astype(bf16) for h in held[1::2]])]
    ppermute x0 -> x95, starting transfers between devices: none -> 111 us  [the longest x93 107 us: swap(): return lax.ppermute(x, axis, [(n, n ^ k) for n in range(size)])]
    unnamed x13 -> x0, waiting for transfers between devices: 89.4 us -> none
    unnamed x1 -> x0, blocking collectives: 79.1 us -> none
  transfers between devices with their start and end apart: 16 -> 95, of which waited for: 10 -> 35; matrix products, arithmetic and copies ran while one was open for 16% -> 29% of each run, Pallas kernels for 0% -> 2%
where the time goes in v1:
time: 580 us; the launch traced here: 571 us
  waiting for transfers between devices  239 us (41%)
  starting transfers between devices  111 us (19%)
  other arithmetic  77.2 us (13%)
  local copies, waits for them, and re-layouts  66.8 us (12%)
  matrix products  44.1 us (8%)
  Pallas kernels  29.5 us (5%)
    ppermute x93, waiting for transfers between devices, swap(): return lax.ppermute(x, axis, [(n, n ^ k) for n in range(size)])  239 us
    ppermute x93, starting transfers between devices, swap(): return lax.ppermute(x, axis, [(n, n ^ k) for n in range(size)])  107 us
    dot_general x16, matrix products, dot_of(): lax.dot_general(a, b, (((ca,), (cb,)), ((), ())), preferred_element_type=...  44.1 us
    unnamed x132, local copies, waits for them, and re-layouts  32.1 us
    reduce_sum x1, other arithmetic, per_device(): factor_one = lax.rsqrt(jnp.mean(x_f * x_f, axis=1, keepdims=True) + 1e-06)  16.8 us
    pallas_call x1, Pallas kernels, attention_forward(): pl.pallas_call(functools.partial(forward_kernel, count), out_shape=[jax.S...  15.6 us
    select_n x1, other arithmetic, per_device(): grad_full = jnp.where(valid_rows > 0.5, g_raw, jnp.zeros_like(g_raw))  15.4 us
    pallas_call x1, Pallas kernels, attention_backward(): pl.pallas_call(functools.partial(backward_kernel, count), out_shape=[jax....  13.9 us
  transfers between devices with their start and end apart: 95, of which 35 were waited for; matrix products, arithmetic and copies ran while one was open for 29% of the time, Pallas kernels for 2%

profile of v1, /device:TPU:0, one launch (start us, length us, event | category | flops | bytes accessed | tf_op | source)
XLA Modules:
  0.0 570.6 jit_solution(9853390832708627721)
XLA Ops:
  12.6 4.1 copy.19
  31.0 3.9 stack.153.len_ref
  40.0 5.7 collective-permute-done.18
  55.9 16.8 %fusion = (f32[1024]{0:T(1024)S(1)}, bf16[1024,1536]{1,0:T(8,128)(2,1)S(1)}) fusion(bf16[512,384]{1,0:T(8,128)(2,1)S(1)} %collective-permute-done.8, bf16[512,384]{1,0:T(8,128)(2,1)S(1)} %collective-permute-done.7, bf16[512,384]{1,0:T(8,128)(2,1)S(1)} %collective-permute-done.6, bf16[512,384]{1,0:T(8,128)(2,1)S(1)} %get-tuple-element.110, ...), kind=kLoop, calls=%fused_computation.2 | loop fusion | flops 29883392 | bytes 6295552 | tf_op jit(solution)/shard_map/reduce_sum | solution.py:300
  76.3 4.4 collective-permute-done.13
  80.7 4.4 collective-permute-done.12
  88.3 15.6 %shard_map.169 = (bf16[6,256,128]{2,1,0:T(8,128)(2,1)S(1)}, f32[6,256,256]{2,1,0:T(8,128)S(1)}, f32[6,256,256]{2,1,0:T(8,128)S(1)}, f32[6,256,256]{2,1,0:T(8,128)S(1)}) custom-call(s32[6]{0:T(128)S(1)} %stack.153.len_ref, bf16[6,256,512]{2,1,0:T(8,128)(2,1)} %bitcast.234, f32[6,1,256]{2,1,0:T(1,128)S(1)} %bitcast.240), custom_call_target="tpu_custom_call" | custom-call | flops 9600000000 | bytes 6600000 | tf_op jit(solution)/shard_map/pallas_call | solution.py:147
  111.9 6.4 %collective-permute-done.21 = bf16[1536,128]{1,0:T(8,128)(2,1)S(1)} collective-permute-done((bf16[1536,128]{1,0:T(8,128)(2,1)S(1)}, bf16[1536,128]{1,0:T(8,128)(2,1)S(1)}, u32[]{:S(2)}, u32[]{:S(2)}) %collective-permute-start.21) | collective-permute-done | bytes 393248 | tf_op jit(solution)/shard_map/ppermute | solution.py:187
  118.3 10.4 %collective-permute-done.22 = bf16[1536,128]{1,0:T(8,128)(2,1)S(1)} collective-permute-done((bf16[1536,128]{1,0:T(8,128)(2,1)S(1)}, bf16[1536,128]{1,0:T(8,128)(2,1)S(1)}, u32[]{:S(2)}, u32[]{:S(2)}) %collective-permute-start.22) | collective-permute-done | bytes 393248 | tf_op jit(solution)/shard_map/ppermute | solution.py:187
  143.7 4.5 constant_dynamic-slice_fusion.27
  168.6 15.8 %collective-permute-done.28 = bf16[512,384]{1,0:T(8,128)(2,1)} collective-permute-done((bf16[512,384]{1,0:T(8,128)(2,1)S(1)}, bf16[512,384]{1,0:T(8,128)(2,1)}, u32[]{:S(2)}, u32[]{:S(2)}) %collective-permute-start.28) | collective-permute-done | bytes 393248 | tf_op jit(solution)/shard_map/ppermute | solution.py:187
  186.4 22.6 %collective-permute-done.44 = bf16[512,384]{1,0:T(8,128)(2,1)} collective-permute-done((bf16[512,384]{1,0:T(8,128)(2,1)S(1)}, bf16[512,384]{1,0:T(8,128)(2,1)}, u32[]{:S(2)}, u32[]{:S(2)}) %collective-permute-start.44) | collective-permute-done | bytes 393248 | tf_op jit(solution)/shard_map/ppermute | solution.py:187
  217.5 15.4 %maximum_select_fusion = bf16[1024,1536]{1,0:T(8,128)(2,1)S(1)} fusion(bf16[512,384]{1,0:T(8,128)(2,1)S(1)} %collective-permute-done.48, bf16[512,384]{1,0:T(8,128)(2,1)S(1)} %collective-permute-done.47, bf16[512,384]{1,0:T(8,128)(2,1)S(1)} %collective-permute-done.46, bf16[512,384]{1,0:T(8,128)(2,1)S(1)} %copy-done.9, ...), kind=kLoop, calls=%fused_computation.16 | loop fusion | flops 26738688 | bytes 6292480 | tf_op jit(solution)/shard_map/jit(_where)/select_n | solution.py:340
  233.0 4.9 fusion.108
  244.8 4.8 convolution_convert_fusion
  250.7 13.0 %collective-permute-done.86 = bf16[2,384,512]{2,1,0:T(8,128)(2,1)S(1)} collective-permute-done((bf16[2,384,512]{2,1,0:T(8,128)(2,1)S(1)}, bf16[2,384,512]{2,1,0:T(8,128)(2,1)S(1)}, u32[]{:S(2)}, u32[]{:S(2)}) %collective-permute-start.86) | collective-permute-done | bytes 786464 | tf_op jit(solution)/shard_map/ppermute | solution.py:187
  270.6 32.5 %collective-permute-done.87 = bf16[1,384,512]{2,1,0:T(8,128)(2,1)S(1)} collective-permute-done((bf16[1,384,512]{2,1,0:T(8,128)(2,1)S(1)}, bf16[1,384,512]{2,1,0:T(8,128)(2,1)S(1)}, u32[]{:S(2)}, u32[]{:S(2)}) %collective-permute-start.87) | collective-permute-done | bytes 393248 | tf_op jit(solution)/shard_map/ppermute | solution.py:187
  322.4 7.9 %collective-permute-done.50 = bf16[512,384]{1,0:T(8,128)(2,1)S(1)} collective-permute-done((bf16[512,384]{1,0:T(8,128)(2,1)S(1)}, bf16[512,384]{1,0:T(8,128)(2,1)S(1)}, u32[]{:S(2)}, u32[]{:S(2)}) %collective-permute-start.50) | collective-permute-done | bytes 393248 | tf_op jit(solution)/shard_map/ppermute | solution.py:187
  330.3 5.9 %collective-permute-done.52 = bf16[512,384]{1,0:T(8,128)(2,1)S(1)} collective-permute-done((bf16[512,384]{1,0:T(8,128)(2,1)S(1)}, bf16[512,384]{1,0:T(8,128)(2,1)S(1)}, u32[]{:S(2)}, u32[]{:S(2)}) %collective-permute-start.52) | collective-permute-done | bytes 393248 | tf_op jit(solution)/shard_map/ppermute | solution.py:187
  347.2 9.9 %collective-permute-done.53 = f32[4,128]{1,0:T(4,128)S(1)} collective-permute-done((f32[4,128]{1,0:T(4,128)S(1)}, f32[4,128]{1,0:T(4,128)S(1)}, u32[]{:S(2)}, u32[]{:S(2)}) %collective-permute-start.53) | collective-permute-done | bytes 2080 | tf_op jit(solution)/shard_map/ppermute | solution.py:187
  395.4 4.2 collective-permute-done.58
  401.0 13.9 %shard_map.170 = (bf16[6,256,512]{2,1,0:T(8,128)(2,1)S(1)}, f32[6,1,256]{2,1,0:T(1,128)S(1)}) custom-call(s32[6]{0:T(128)S(1)} %stack.153.len_ref, bf16[6,256,512]{2,1,0:T(8,128)(2,1)S(1)} %bitcast.235, f32[6,1,256]{2,1,0:T(1,128)S(1)} %bitcast.241, f32[6,256,256]{2,1,0:T(8,128)S(1)} %get-tuple-element.16.inv_ref, f32[6,256,256]{2,1,0:T(8,128)} %copy-done.1, ...), custom_call_target="tpu_custom_call" | custom-call | flops 8400000000 | bytes 8400000 | tf_op jit(solution)/shard_map/pallas_call | solution.py:165
  419.9 6.6 %convolution_convert_fusion.1 = bf16[1536,1024]{1,0:T(8,128)(2,1)S(1)} fusion(bf16[1024,1536]{1,0:T(8,128)(2,1)S(1)} %copy-done.4, bf16[512,512]{1,0:T(8,128)(2,1)S(1)} %bitcast.254, bf16[512,512]{1,0:T(8,128)(2,1)S(1)} %bitcast.252, bf16[1024,512]{1,0:T(8,128)(2,1)S(1)} %bitcast.248), kind=kOutput, calls=%fused_computation.7 | convolution fusion | flops 3229089792 | bytes 8388608 | tf_op jit(solution)/shard_map/dot_general | solution.py:18
  428.8 5.0 convolution_add_fusion
  441.7 21.3 %collective-permute-done.74 = bf16[1,384,128]{1,2,0:T(8,128)(2,1)S(1)} collective-permute-done((bf16[1,384,128]{1,2,0:T(8,128)(2,1)S(1)}, bf16[1,384,128]{1,2,0:T(8,128)(2,1)S(1)}, u32[]{:S(2)}, u32[]{:S(2)}) %collective-permute-start.74) | collective-permute-done | bytes 98336 | tf_op jit(solution)/shard_map/ppermute | solution.py:187
  469.0 3.9 collective-permute-start.80
  481.1 12.5 %collective-permute-done.61 = bf16[512,384]{1,0:T(8,128)(2,1)S(1)} collective-permute-done((bf16[512,384]{1,0:T(8,128)(2,1)S(1)}, bf16[512,384]{1,0:T(8,128)(2,1)S(1)}, u32[]{:S(2)}, u32[]{:S(2)}) %collective-permute-start.61) | collective-permute-done | bytes 393248 | tf_op jit(solution)/shard_map/ppermute | solution.py:187
  493.6 7.0 %collective-permute-done.63 = bf16[512,384]{1,0:T(8,128)(2,1)S(1)} collective-permute-done((bf16[512,384]{1,0:T(8,128)(2,1)S(1)}, bf16[512,384]{1,0:T(8,128)(2,1)S(1)}, u32[]{:S(2)}, u32[]{:S(2)}) %collective-permute-start.63) | collective-permute-done | bytes 393248 | tf_op jit(solution)/shard_map/ppermute | solution.py:187
  506.6 5.2 collective-permute-start.69
  518.1 28.4 %collective-permute-done.93 = bf16[1,96,2]{1,2,0:T(2,128)(2,1)S(1)} collective-permute-done((bf16[1,96,2]{1,2,0:T(2,128)(2,1)S(1)}, bf16[1,96,2]{1,2,0:T(2,128)(2,1)S(1)}, u32[]{:S(2)}, u32[]{:S(2)}) %collective-permute-start.93) | collective-permute-done | bytes 416 | tf_op jit(solution)/shard_map/ppermute | solution.py:187
  550.6 8.8 %collective-permute-start.72 = (bf16[96,1024]{1,0:T(8,128)(2,1)S(1)}, bf16[96,1024]{1,0:T(8,128)(2,1)S(1)}, u32[]{:S(2)}, u32[]{:S(2)}) collective-permute-start(bf16[96,1024]{1,0:T(8,128)(2,1)S(1)} %get-tuple-element.99), channel_id=1, source_target_pairs={{0,3},{1,2},{2,1},{3,0},{4,7},{5,6},{6,5},{7,4},{8,11},{9,10},{10,... | collective-permute-start | bytes 589832 | tf_op jit(solution)/shard_map/ppermute | solution.py:187
  561.1 3.7 collective-permute-done.72
  (456 shorter events, 238.1 us)
Async XLA Ops:
  7.2 27.7 %collective-permute-start.11 = (bf16[2,384]{1,0:T(2,128)(2,1)}, bf16[2,384]{1,0:T(2,128)(2,1)}, u32[]{:S(2)}, u32[]{:S(2)}) collective-permute-start(bf16[2,384]{1,0:T(2,128)(2,1)} %pad_maximum_fusion.30), channel_id=1, source_target_pairs={{0,3},{1,2},{2,1},{3,0},{4,7},{5,6},{6,5},{7,4},{8,11},{9,10},{10,... | collective-permute-start | bytes 4616 | tf_op jit(solution)/shard_map/ppermute | solution.py:187
  10.1 27.0 %collective-permute-start.10 = (bf16[2,384]{1,0:T(2,128)(2,1)}, bf16[2,384]{1,0:T(2,128)(2,1)}, u32[]{:S(2)}, u32[]{:S(2)}) collective-permute-start(bf16[2,384]{1,0:T(2,128)(2,1)} %pad_maximum_fusion.30), channel_id=1, source_target_pairs={{0,2},{1,3},{2,0},{3,1},{4,6},{5,7},{6,4},{7,5},{8,10},{9,11},{10,... | collective-permute-start | bytes 4616 | tf_op jit(solution)/shard_map/ppermute | solution.py:187
  21.6 24.9 %collective-permute-start.19 = (bf16[384,6]{0,1:T(8,128)(2,1)S(1)}, bf16[384,6]{0,1:T(8,128)(2,1)S(1)}, u32[]{:S(2)}, u32[]{:S(2)}) collective-permute-start(bf16[384,6]{0,1:T(8,128)(2,1)S(1)} %copy-done.41), channel_id=1, source_target_pairs={{0,2},{1,3},{2,0},{3,1},{4,6},{5,7},{6,4},{7,5},{8,10},{9,11},{10,... | collective-permute-start | bytes 13832 | tf_op jit(solution)/shard_map/ppermute | solution.py:187
  23.6 25.6 %collective-permute-start.5 = (bf16[512,384]{1,0:T(8,128)(2,1)S(1)}, bf16[512,384]{1,0:T(8,128)(2,1)S(1)}, u32[]{:S(2)}, u32[]{:S(2)}) collective-permute-start(bf16[512,384]{1,0:T(8,128)(2,1)S(1)} %get-tuple-element.111), channel_id=1, source_target_pairs={{0,3},{1,2},{2,1},{3,0},{4,7},{5,6},{6,5},{7,4},{8,11},{9,10},{10,... | collective-permute-start | bytes 1179656 | tf_op jit(solution)/shard_map/ppermute | solution.py:187
  46.6 28.0 %collective-permute-start.17 = (bf16[384,512]{0,1:T(8,128)(2,1)}, bf16[384,512]{0,1:T(8,128)(2,1)S(1)}, u32[]{:S(2)}, u32[]{:S(2)}) collective-permute-start(bf16[384,512]{0,1:T(8,128)(2,1)} %bitcast.265), channel_id=1, source_target_pairs={{0,3},{1,2},{2,1},{3,0},{4,7},{5,6},{6,5},{7,4},{8,11},{9,10},{10,... | collective-permute-start | bytes 1179656 | tf_op jit(solution)/shard_map/ppermute | solution.py:187
  50.4 24.8 %collective-permute-start.16 = (bf16[384,512]{0,1:T(8,128)(2,1)}, bf16[384,512]{0,1:T(8,128)(2,1)S(1)}, u32[]{:S(2)}, u32[]{:S(2)}) collective-permute-start(bf16[384,512]{0,1:T(8,128)(2,1)} %bitcast.264), channel_id=1, source_target_pairs={{0,2},{1,3},{2,0},{3,1},{4,6},{5,7},{6,4},{7,5},{8,10},{9,11},{10,... | collective-permute-start | bytes 1179656 | tf_op jit(solution)/shard_map/ppermute | solution.py:187
  52.3 22.9 %collective-permute-start.15 = (bf16[384,512]{0,1:T(8,128)(2,1)}, bf16[384,512]{0,1:T(8,128)(2,1)S(1)}, u32[]{:S(2)}, u32[]{:S(2)}) collective-permute-start(bf16[384,512]{0,1:T(8,128)(2,1)} %bitcast.263), channel_id=1, source_target_pairs={{0,1},{1,0},{2,3},{3,2},{4,5},{5,4},{6,7},{7,6},{8,9},{9,8},{10,11... | collective-permute-start | bytes 1179656 | tf_op jit(solution)/shard_map/ppermute | solution.py:187
  52.8 23.5 %collective-permute-start.14 = (bf16[384,512]{0,1:T(8,128)(2,1)}, bf16[384,512]{0,1:T(8,128)(2,1)S(1)}, u32[]{:S(2)}, u32[]{:S(2)}) collective-permute-start(bf16[384,512]{0,1:T(8,128)(2,1)} %bitcast.262), channel_id=1, source_target_pairs={{0,3},{1,2},{2,1},{3,0},{4,7},{5,6},{6,5},{7,4},{8,11},{9,10},{10,... | collective-permute-start | bytes 1179656 | tf_op jit(solution)/shard_map/ppermute | solution.py:187
  55.4 25.3 %collective-permute-start.13 = (bf16[384,512]{0,1:T(8,128)(2,1)}, bf16[384,512]{0,1:T(8,128)(2,1)S(1)}, u32[]{:S(2)}, u32[]{:S(2)}) collective-permute-start(bf16[384,512]{0,1:T(8,128)(2,1)} %bitcast.261), channel_id=1, source_target_pairs={{0,2},{1,3},{2,0},{3,1},{4,6},{5,7},{6,4},{7,5},{8,10},{9,11},{10,... | collective-permute-start | bytes 1179656 | tf_op jit(solution)/shard_map/ppermute | solution.py:187
  142.5 24.5 %collective-permute-start.29 = (bf16[512,384]{1,0:T(8,128)(2,1)S(1)}, bf16[512,384]{1,0:T(8,128)(2,1)}, u32[]{:S(2)}, u32[]{:S(2)}) collective-permute-start(bf16[512,384]{1,0:T(8,128)(2,1)S(1)} %multiply_convert_fusion.3), channel_id=1, source_target_pairs={{0,2},{1,3},{2,0},{3,1},{4,6},{5,7},{6,4},{7,5},{8,10},{9,11},{10,... | collective-permute-start | bytes 1179656 | tf_op jit(solution)/shard_map/ppermute | solution.py:187
  149.2 61.7 %collective-permute-start.33 = (bf16[384,1024]{1,0:T(8,128)(2,1)}, bf16[384,1024]{1,0:T(8,128)(2,1)}, u32[]{:S(2)}, u32[]{:S(2)}) collective-permute-start(bf16[384,1024]{1,0:T(8,128)(2,1)} %bitcast.123), channel_id=1, source_target_pairs={{0,2},{1,3},{2,0},{3,1},{4,6},{5,7},{6,4},{7,5},{8,10},{9,11},{10,... | collective-permute-start | bytes 2359304 | tf_op jit(solution)/shard_map/ppermute | solution.py:187
  151.0 60.0 %collective-permute-start.32 = (bf16[384,1024]{1,0:T(8,128)(2,1)}, bf16[384,1024]{1,0:T(8,128)(2,1)}, u32[]{:S(2)}, u32[]{:S(2)}) collective-permute-start(bf16[384,1024]{1,0:T(8,128)(2,1)} %bitcast.121), channel_id=1, source_target_pairs={{0,1},{1,0},{2,3},{3,2},{4,5},{5,4},{6,7},{7,6},{8,9},{9,8},{10,11... | collective-permute-start | bytes 2359304 | tf_op jit(solution)/shard_map/ppermute | solution.py:187
  151.8 32.6 %collective-permute-start.28 = (bf16[512,384]{1,0:T(8,128)(2,1)S(1)}, bf16[512,384]{1,0:T(8,128)(2,1)}, u32[]{:S(2)}, u32[]{:S(2)}) collective-permute-start(bf16[512,384]{1,0:T(8,128)(2,1)S(1)} %multiply_convert_fusion.3), channel_id=1, source_target_pairs={{0,1},{1,0},{2,3},{3,2},{4,5},{5,4},{6,7},{7,6},{8,9},{9,8},{10,11... | collective-permute-start | bytes 1179656 | tf_op jit(solution)/shard_map/ppermute | solution.py:187
  160.2 48.8 %collective-permute-start.44 = (bf16[512,384]{1,0:T(8,128)(2,1)S(1)}, bf16[512,384]{1,0:T(8,128)(2,1)}, u32[]{:S(2)}, u32[]{:S(2)}) collective-permute-start(bf16[512,384]{1,0:T(8,128)(2,1)S(1)} %get-tuple-element.105), channel_id=1, source_target_pairs={{0,2},{1,3},{2,0},{3,1},{4,6},{5,7},{6,4},{7,5},{8,10},{9,11},{10,... | collective-permute-start | bytes 1179656 | tf_op jit(solution)/shard_map/ppermute | solution.py:187
  167.0 46.9 %collective-permute-start.34 = (bf16[384,1024]{1,0:T(8,128)(2,1)}, bf16[384,1024]{1,0:T(8,128)(2,1)S(1)}, u32[]{:S(2)}, u32[]{:S(2)}) collective-permute-start(bf16[384,1024]{1,0:T(8,128)(2,1)} %bitcast.251), channel_id=1, source_target_pairs={{0,3},{1,2},{2,1},{3,0},{4,7},{5,6},{6,5},{7,4},{8,11},{9,10},{10,... | collective-permute-start | bytes 2359304 | tf_op jit(solution)/shard_map/ppermute | solution.py:187
  184.4 25.9 %collective-permute-start.43 = (bf16[512,384]{1,0:T(8,128)(2,1)S(1)}, bf16[512,384]{1,0:T(8,128)(2,1)S(1)}, u32[]{:S(2)}, u32[]{:S(2)}) collective-permute-start(bf16[512,384]{1,0:T(8,128)(2,1)S(1)} %get-tuple-element.105), channel_id=1, source_target_pairs={{0,1},{1,0},{2,3},{3,2},{4,5},{5,4},{6,7},{7,6},{8,9},{9,8},{10,11... | collective-permute-start | bytes 1179656 | tf_op jit(solution)/shard_map/ppermute | solution.py:187
  209.0 24.0 %collective-permute-start.31 = (bf16[512,1536]{1,0:T(8,128)(2,1)S(1)}, bf16[512,1536]{1,0:T(8,128)(2,1)S(1)}, u32[]{:S(2)}, u32[]{:S(2)}) collective-permute-start(bf16[512,1536]{1,0:T(8,128)(2,1)S(1)} %pad_maximum_fusion.3), channel_id=1, source_target_pairs={{0,4},{4,0},{1,5},{5,1},{2,6},{6,2},{3,7},{7,3},{8,12},{12,8},{9,1... | collective-permute-start | bytes 4718600 | tf_op jit(solution)/shard_map/ppermute | solution.py:187
  213.8 24.0 %collective-permute-start.35 = (bf16[384,512]{1,0:T(8,128)(2,1)S(1)}, bf16[384,512]{1,0:T(8,128)(2,1)S(1)}, u32[]{:S(2)}, u32[]{:S(2)}) collective-permute-start(bf16[384,512]{1,0:T(8,128)(2,1)S(1)} %copy-done.18), channel_id=1, source_target_pairs={{0,1},{1,0},{2,3},{3,2},{4,5},{5,4},{6,7},{7,6},{8,9},{9,8},{10,11... | collective-permute-start | bytes 1179656 | tf_op jit(solution)/shard_map/ppermute | solution.py:187
  214.5 23.4 %collective-permute-start.37 = (bf16[384,512]{1,0:T(8,128)(2,1)S(1)}, bf16[384,512]{1,0:T(8,128)(2,1)S(1)}, u32[]{:S(2)}, u32[]{:S(2)}) collective-permute-start(bf16[384,512]{1,0:T(8,128)(2,1)S(1)} %copy-done.17), channel_id=1, source_target_pairs={{0,3},{1,2},{2,1},{3,0},{4,7},{5,6},{6,5},{7,4},{8,11},{9,10},{10,... | collective-permute-start | bytes 1179656 | tf_op jit(solution)/shard_map/ppermute | solution.py:187
  250.1 63.5 %collective-permute-start.81 = (bf16[2,384,1024]{2,1,0:T(8,128)(2,1)S(1)}, bf16[2,384,1024]{2,1,0:T(8,128)(2,1)S(1)}, u32[]{:S(2)}, u32[]{:S(2)}) collective-permute-start(bf16[2,384,1024]{2,1,0:T(8,128)(2,1)S(1)} %pad_maximum_fusion.6), channel_id=1, source_target_pairs={{0,8},{8,0},{16,24},{24,16},{1,9},{9,1},{17,25},{25,17},{2,10},{10... | collective-permute-start | bytes 4718600 | tf_op jit(solution)/shard_map/ppermute | solution.py:187
  263.8 39.3 %collective-permute-start.87 = (bf16[1,384,512]{2,1,0:T(8,128)(2,1)S(1)}, bf16[1,384,512]{2,1,0:T(8,128)(2,1)S(1)}, u32[]{:S(2)}, u32[]{:S(2)}) collective-permute-start(bf16[1,384,512]{2,1,0:T(8,128)(2,1)S(1)} %fusion.69), channel_id=1, source_target_pairs={{0,16},{8,24},{16,0},{24,8},{1,17},{9,25},{17,1},{25,9},{2,18},{10... | collective-permute-start | bytes 1179656 | tf_op jit(solution)/shard_map/ppermute | solution.py:187
  270.1 47.4 %collective-permute-start.49 = (bf16[512,1536]{1,0:T(8,128)(2,1)S(1)}, bf16[512,1536]{1,0:T(8,128)(2,1)S(1)}, u32[]{:S(2)}, u32[]{:S(2)}) collective-permute-start(bf16[512,1536]{1,0:T(8,128)(2,1)S(1)} %slice.524), channel_id=1, source_target_pairs={{0,4},{4,0},{1,5},{5,1},{2,6},{6,2},{3,7},{7,3},{8,12},{12,8},{9,1... | collective-permute-start | bytes 4718600 | tf_op jit(solution)/shard_map/ppermute | solution.py:187
  314.0 47.3 %collective-permute-start.82 = (bf16[1,384,1024]{2,1,0:T(8,128)(2,1)S(1)}, bf16[1,384,1024]{2,1,0:T(8,128)(2,1)S(1)}, u32[]{:S(2)}, u32[]{:S(2)}) collective-permute-start(bf16[1,384,1024]{2,1,0:T(8,128)(2,1)S(1)} %fusion.56), channel_id=1, source_target_pairs={{0,16},{8,24},{16,0},{24,8},{1,17},{9,25},{17,1},{25,9},{2,18},{10... | collective-permute-start | bytes 2359304 | tf_op jit(solution)/shard_map/ppermute | solution.py:187
  362.8 23.0 %collective-permute-start.85 = (bf16[96,1024]{1,0:T(8,128)(2,1)}, bf16[96,1024]{1,0:T(8,128)(2,1)}, u32[]{:S(2)}, u32[]{:S(2)}) collective-permute-start(bf16[96,1024]{1,0:T(8,128)(2,1)} %get-tuple-element.90), channel_id=1, source_target_pairs={{0,3},{1,2},{2,1},{3,0},{4,7},{5,6},{6,5},{7,4},{8,11},{9,10},{10,... | collective-permute-start | bytes 589832 | tf_op jit(solution)/shard_map/ppermute | solution.py:187
  393.0 41.1 %collective-permute-start.79 = (bf16[1,96,768]{2,1,0:T(8,128)(2,1)}, bf16[1,96,768]{2,1,0:T(8,128)(2,1)}, u32[]{:S(2)}, u32[]{:S(2)}) collective-permute-start(bf16[1,96,768]{2,1,0:T(8,128)(2,1)} %fusion.77), channel_id=1, source_target_pairs={{0,16},{8,24},{16,0},{24,8},{1,17},{9,25},{17,1},{25,9},{2,18},{10... | collective-permute-start | bytes 442376 | tf_op jit(solution)/shard_map/ppermute | solution.py:187
  428.1 76.7 %collective-permute-start.68 = (bf16[2,384,1024]{2,1,0:T(8,128)(2,1)S(1)}, bf16[2,384,1024]{2,1,0:T(8,128)(2,1)}, u32[]{:S(2)}, u32[]{:S(2)}) collective-permute-start(bf16[2,384,1024]{2,1,0:T(8,128)(2,1)S(1)} %pad_maximum_fusion.5), channel_id=1, source_target_pairs={{0,8},{8,0},{16,24},{24,16},{1,9},{9,1},{17,25},{25,17},{2,10},{10... | collective-permute-start | bytes 4718600 | tf_op jit(solution)/shard_map/ppermute | solution.py:187
  434.1 40.6 %collective-permute-start.60 = (bf16[512,1536]{1,0:T(8,128)(2,1)S(1)}, bf16[512,1536]{1,0:T(8,128)(2,1)S(1)}, u32[]{:S(2)}, u32[]{:S(2)}) collective-permute-start(bf16[512,1536]{1,0:T(8,128)(2,1)S(1)} %slice.523), channel_id=1, source_target_pairs={{0,4},{4,0},{1,5},{5,1},{2,6},{6,2},{3,7},{7,3},{8,12},{12,8},{9,1... | collective-permute-start | bytes 4718600 | tf_op jit(solution)/shard_map/ppermute | solution.py:187
  438.8 24.3 %collective-permute-start.74 = (bf16[1,384,128]{1,2,0:T(8,128)(2,1)S(1)}, bf16[1,384,128]{1,2,0:T(8,128)(2,1)S(1)}, u32[]{:S(2)}, u32[]{:S(2)}) collective-permute-start(bf16[1,384,128]{1,2,0:T(8,128)(2,1)S(1)} %fusion.78), channel_id=1, source_target_pairs={{0,16},{8,24},{16,0},{24,8},{1,17},{9,25},{17,1},{25,9},{2,18},{10... | collective-permute-start | bytes 294920 | tf_op jit(solution)/shard_map/ppermute | solution.py:187
  469.0 35.0 %collective-permute-start.80 = (f32[96,768]{1,0:T(8,128)}, f32[96,768]{1,0:T(8,128)}, u32[]{:S(2)}, u32[]{:S(2)}) collective-permute-start(f32[96,768]{1,0:T(8,128)} %constant_dynamic-update-slice_fusion.15), channel_id=1, source_target_pairs={{0,0},{1,8},{2,16},{3,24},{8,1},{9,9},{10,17},{11,25},{16,2},{17,1... | collective-permute-start | bytes 884744 | tf_op jit(solution)/shard_map/ppermute | solution.py:480
  478.3 22.3 %collective-permute-start.63 = (bf16[512,384]{1,0:T(8,128)(2,1)S(1)}, bf16[512,384]{1,0:T(8,128)(2,1)S(1)}, u32[]{:S(2)}, u32[]{:S(2)}) collective-permute-start(bf16[512,384]{1,0:T(8,128)(2,1)S(1)} %get-tuple-element.63), channel_id=1, source_target_pairs={{0,3},{1,2},{2,1},{3,0},{4,7},{5,6},{6,5},{7,4},{8,11},{9,10},{10,... | collective-permute-start | bytes 1179656 | tf_op jit(solution)/shard_map/ppermute | solution.py:187
  506.6 42.2 %collective-permute-start.69 = (bf16[1,384,1024]{2,1,0:T(8,128)(2,1)S(1)}, bf16[1,384,1024]{2,1,0:T(8,128)(2,1)S(1)}, u32[]{:S(2)}, u32[]{:S(2)}) collective-permute-start(bf16[1,384,1024]{2,1,0:T(8,128)(2,1)S(1)} %fusion.55), channel_id=1, source_target_pairs={{0,16},{8,24},{16,0},{24,8},{1,17},{9,25},{17,1},{25,9},{2,18},{10... | collective-permute-start | bytes 2359304 | tf_op jit(solution)/shard_map/ppermute | solution.py:187
  515.4 31.1 %collective-permute-start.93 = (bf16[1,96,2]{1,2,0:T(2,128)(2,1)S(1)}, bf16[1,96,2]{1,2,0:T(2,128)(2,1)S(1)}, u32[]{:S(2)}, u32[]{:S(2)}) collective-permute-start(bf16[1,96,2]{1,2,0:T(2,128)(2,1)S(1)} %fusion.90), channel_id=1, source_target_pairs={{0,16},{8,24},{16,0},{24,8},{1,17},{9,25},{17,1},{25,9},{2,18},{10... | collective-permute-start | bytes 1160 | tf_op jit(solution)/shard_map/ppermute | solution.py:187
  (112 other events, 1404.5 us)

commit v2 on v1

v2 whole, which is shorter than its diff:
```python
import functools

import jax
import jax.numpy as jnp
from jax import lax
from jax.experimental import pallas as pl
from jax.experimental.pallas import tpu as pltpu
from jax.sharding import PartitionSpec as P

f32 = jnp.float32
bf16 = jnp.bfloat16

SEQ = 256
HD = 128


def dot_of(a, b, ca, cb):
    return lax.dot_general(a, b, (((ca,), (cb,)), ((), ())), preferred_element_type=f32)


def halves_of(a):
    high = a.astype(bf16)
    return high, (a - high.astype(f32)).astype(bf16)


def mul(a, b, ca=1, cb=0, passes=3):
    if passes == 1:
        return dot_of(a.astype(bf16), b.astype(bf16), ca, cb)
    if a.dtype == bf16:
        bh, bl = halves_of(b)
        return dot_of(a, bh, ca, cb) + dot_of(a, bl, ca, cb)
    if b.dtype == bf16:
        ah, al = halves_of(a)
        return dot_of(ah, b, ca, cb) + dot_of(al, b, ca, cb)
    ah, al = halves_of(a)
    bh, bl = halves_of(b)
    return dot_of(ah, bh, ca, cb) + (dot_of(ah, bl, ca, cb) + dot_of(al, bh, ca, cb))


def iotas():
    rows = lax.broadcasted_iota(jnp.int32, (SEQ, SEQ), 0)
    cols = lax.broadcasted_iota(jnp.int32, (SEQ, SEQ), 1)
    return rows, cols


def prepare(raw, logit_row, i, j):
    eye = i == j
    raw_f = raw.astype(f32)
    norm = lax.rsqrt(jnp.sum(raw_f * raw_f, axis=1, keepdims=True) + 1e-6)
    norm_row = jnp.sum(jnp.where(eye, norm, 0.0), axis=0, keepdims=True)
    beta_row = 2.0 / (1.0 + jnp.exp(-logit_row))
    beta = jnp.sum(jnp.where(eye, beta_row, 0.0), axis=1, keepdims=True)
    return raw_f, norm, norm_row, beta_row, beta


def inverses(lowers, i, j):
    eye = jnp.where(i == j, 1.0, 0.0)
    first = ((i >> 1) == (j >> 1)) & (i > j)
    inv = [eye - jnp.where(first, n, 0.0) for n in lowers]
    s = 1
    while (1 << s) < SEQ:
        mask = ((i >> (s + 1)) == (j >> (s + 1))) & ((i >> s) > (j >> s))
        mids = [mul(d, jnp.where(mask, n, 0.0)) for d, n in zip(inv, lowers)]
        inv = [d - mul(x, d) for d, x in zip(inv, mids)]
        s += 1
    return inv


def forward_kernel(count, len_ref, x_ref, l_ref, o_ref, inv_ref, carry_ref, prob_ref):
    base = pl.program_id(0) * count
    i, j = iotas()
    row = lax.broadcasted_iota(jnp.int32, (SEQ, 1), 0)
    xs = [x_ref[t] for t in range(count)]
    qs = [x[:, 0:HD] for x in xs]
    ks = [x[:, HD : 2 * HD] for x in xs]
    vs = [x[:, 2 * HD : 3 * HD] for x in xs]
    us = [x[:, 3 * HD : 4 * HD] for x in xs]
    pre = [prepare(us[t], l_ref[t], i, j) for t in range(count)]
    lowers = [
        p[4] * jnp.where(i > j, dot_of(u, u, 1, 1) * p[1] * p[2], 0.0) for u, p in zip(us, pre)
    ]
    inv = inverses(lowers, i, j)
    bs = [jnp.where(i > j, dot_of(u, k, 1, 1) * p[1], 0.0) for u, k, p in zip(us, ks, pre)]
    carries = [mul(d * p[3], b) for d, p, b in zip(inv, pre, bs)]
    as_ = [jnp.where(i >= j, dot_of(q, u, 1, 1) * p[2], 0.0) for q, u, p in zip(qs, us, pre)]
    scores = [
        (dot_of(q, k, 1, 1) - mul(a, c)) * (HD**-0.5) for q, k, a, c in zip(qs, ks, as_, carries)
    ]
    for t in range(count):
        length = len_ref[base + t]
        score = jnp.where((j <= i) & (j < length), scores[t], -1e30)
        weight = jnp.exp(score - jnp.max(score, axis=1, keepdims=True))
        prob = weight * (1.0 / jnp.sum(weight, axis=1, keepdims=True))
        out = jnp.where(row < length, mul(prob, vs[t], passes=1), 0.0)
        o_ref[t] = out.astype(bf16)
        inv_ref[t] = inv[t]
        carry_ref[t] = carries[t]
        prob_ref[t] = prob


def to_row(col, eye):
    return jnp.sum(jnp.where(eye, col, 0.0), axis=0, keepdims=True)


def backward_kernel(
    count,
    start,
    len_ref,
    x_ref,
    l_ref,
    inv_ref,
    carry_ref,
    prob_ref,
    do_ref,
    dx_ref,
    dl_ref,
    sum_ref,
):
    base = (pl.program_id(0) + start) * count
    i, j = iotas()
    row = lax.broadcasted_iota(jnp.int32, (SEQ, 1), 0)
    for t in range(count):
        x = x_ref[t]
        q, k = x[:, 0:HD], x[:, HD : 2 * HD]
        v, u = x[:, 2 * HD : 3 * HD], x[:, 3 * HD : 4 * HD]
        do = do_ref[0, t].astype(f32) + do_ref[1, t].astype(f32)
        do = (do + (do_ref[2, t].astype(f32) + do_ref[3, t].astype(f32))).astype(bf16)
        do = jnp.where(row < len_ref[base + t], do, jnp.zeros_like(do))
        inv, carry, prob = inv_ref[t], carry_ref[t], prob_ref[t]
        raw, norm, norm_row, beta_row, beta = prepare(u, l_ref[t], i, j)
        gram = jnp.where(i > j, dot_of(u, u, 1, 1) * norm * norm_row, 0.0)
        a = jnp.where(i >= j, dot_of(q, u, 1, 1) * norm_row, 0.0)
        b = jnp.where(i > j, dot_of(u, k, 1, 1) * norm, 0.0)
        m = inv * beta_row
        dv = mul(prob, do, 0, 0, passes=1)
        dprob = dot_of(do, v, 1, 1)
        ds = prob * (dprob - jnp.sum(dprob * prob, axis=1, keepdims=True)) * (HD**-0.5)
        da = jnp.where(i >= j, -mul(ds, carry, 1, 1), 0.0)
        dc = -mul(a, ds, 0, 0)
        dm = mul(dc, b, 1, 1)
        db = jnp.where(i > j, mul(m, dc, 0, 0), 0.0)
        dn = jnp.where(i > j, -mul(mul(inv, dm, 0, 0), m, 1, 1), 0.0)
        dgram = beta * dn
        dbeta = jnp.sum(dm * inv, axis=0, keepdims=True)
        dbeta_col = jnp.sum(dn * gram, axis=1, keepdims=True)
        dbeta = dbeta + jnp.sum(jnp.where(i == j, dbeta_col, 0.0), axis=0, keepdims=True)
        dq = mul(ds, k, passes=1) + mul(da * norm_row, u, passes=1)
        dk = mul(ds, q, 0, 0, passes=1) + mul(db * norm, u, 0, 0, passes=1)
        dw = mul(da, q, 0, 0, passes=1) + mul(db, k, passes=1)
        dw = dw + mul(dgram * norm_row, u, passes=1) + mul(dgram * norm, u, 0, 0, passes=1)
        du = norm * dw - (norm * norm * norm) * raw * jnp.sum(dw * raw, axis=1, keepdims=True)
        dx = jnp.concatenate([dq, dk, dv, du], axis=1)
        dl = dbeta * beta_row * (1.0 - 0.5 * beta_row)
        dx_ref[t] = dx.astype(bf16)
        dl_ref[t] = dl
        total = jnp.sum(dx * x.astype(f32), axis=1, keepdims=True)
        sum_ref[t] = to_row(total, i == j) + dl * l_ref[t]


def block_of(count, *shape):
    return pl.BlockSpec((count,) + shape, lambda g, lens: (g, 0, 0))


def attention_forward(lens, x, logits, count=3):
    pairs = x.shape[0]
    square = jax.ShapeDtypeStruct((pairs, SEQ, SEQ), f32)
    return pl.pallas_call(
        functools.partial(forward_kernel, count),
        out_shape=[jax.ShapeDtypeStruct((pairs, SEQ, HD), bf16), square, square, square],
        grid_spec=pltpu.PrefetchScalarGridSpec(
            num_scalar_prefetch=1,
            grid=(pairs // count,),
            in_specs=[block_of(count, SEQ, 4 * HD), block_of(count, 1, SEQ)],
            out_specs=[block_of(count, SEQ, HD)] + [block_of(count, SEQ, SEQ)] * 3,
        ),
        compiler_params=pltpu.CompilerParams(vmem_limit_bytes=48 << 20),
        cost_estimate=cost(pairs * 1600000000, pairs * 1100000),
    )(lens, x, logits)


def attention_backward(lens, x, logits, inv, carry, prob, do, start, pairs):
    line = jax.ShapeDtypeStruct((pairs, 1, SEQ), f32)

    def from_start(*dims):
        return pl.BlockSpec((1,) + dims, lambda g, lens: (g + start, 0, 0))

    return pl.pallas_call(
        functools.partial(backward_kernel, 1, start),
        out_shape=[jax.ShapeDtypeStruct((pairs, SEQ, 4 * HD), bf16), line, line],
        grid_spec=pltpu.PrefetchScalarGridSpec(
            num_scalar_prefetch=1,
            grid=(pairs,),
            in_specs=[from_start(SEQ, 4 * HD), from_start(1, SEQ)]
            + [from_start(SEQ, SEQ)] * 3
            + [pl.BlockSpec((4, 1, SEQ, HD), lambda g, lens: (0, g + start, 0, 0))],
            out_specs=[block_of(1, SEQ, 4 * HD)] + [block_of(1, 1, SEQ)] * 2,
        ),
        compiler_params=pltpu.CompilerParams(vmem_limit_bytes=48 << 20),
        cost_estimate=cost(pairs * 1400000000, pairs * 1400000),
    )(lens, x, logits, inv, carry, prob, do)


VMEM_LIMIT = 48 << 20
COST_SCALE = 0.001


def shape(*dims, dtype=bf16):
    return jax.ShapeDtypeStruct(dims, dtype)


def rows_block(size, cols):
    return pl.BlockSpec((size, cols), lambda g, *p: (g, 0))


def stack_block(n, size, cols):
    return pl.BlockSpec((n, size, cols), lambda g, *p: (0, g, 0))


def lead_block(size, cols):
    return pl.BlockSpec((1, size, cols), lambda g, *p: (g, 0, 0))


def whole(*dims):
    return pl.BlockSpec(dims, lambda g, *p: (0,) * len(dims))


def cost(flops, moved):
    scale = COST_SCALE
    return pl.CostEstimate(
        flops=int(flops * scale), bytes_accessed=int(moved * scale), transcendentals=0
    )


def project_kernel(n, x_ref, w_ref, misc_ref, a_ref, b_ref, l_ref, r_ref, xg_ref):
    i, j = iotas()
    squares = 0.0
    for k in range(n):
        xf = x_ref[k].astype(f32)
        squares = squares + jnp.sum(xf * xf, axis=1, keepdims=True)
    r = lax.rsqrt(squares * (1.0 / (n * x_ref.shape[2])) + 1e-6)
    acc = 0.0
    logit = 0.0
    for k in range(n):
        gain = misc_ref[k][6:7, :].astype(f32)
        normed = (x_ref[k].astype(f32) * r * gain).astype(bf16)
        xg_ref[k] = normed
        acc = acc + dot_of(normed, w_ref[k], 1, 0)
        logit = logit + dot_of(misc_ref[k], normed, 1, 1)
    out = acc.astype(bf16)
    a_ref[0] = out[:, : 4 * HD]
    b_ref[0] = out[:, 4 * HD :]
    l_ref[0] = logit
    r_ref[0] = to_row(r, i == j)


def project(x, w, misc):
    n, half, part = x.shape
    blocks = half // SEQ
    cols = w.shape[2]
    lines = misc.shape[1]
    return pl.pallas_call(
        functools.partial(project_kernel, n),
        out_shape=[
            shape(blocks, SEQ, 4 * HD),
            shape(blocks, SEQ, 4 * HD),
            shape(blocks, lines, SEQ, dtype=f32),
            shape(blocks, 1, SEQ, dtype=f32),
            shape(n, half, part),
        ],
        grid=(blocks,),
        in_specs=[stack_block(n, SEQ, part), whole(n, part, cols), whole(n, lines, part)],
        out_specs=[
            lead_block(SEQ, 4 * HD),
            lead_block(SEQ, 4 * HD),
            lead_block(lines, SEQ),
            lead_block(1, SEQ),
            stack_block(n, SEQ, part),
        ],
        compiler_params=pltpu.CompilerParams(vmem_limit_bytes=VMEM_LIMIT),
        cost_estimate=cost(2 * half * part * n * cols, 8000000),
    )(x, w, misc)


def ffn_kernel(
    n,
    len_ref,
    side_ref,
    h_ref,
    g_ref,
    wa_ref,
    wb_ref,
    misc_ref,
    n2_ref,
    m_ref,
    d_ref,
    dn_ref,
    sum_ref,
    r_ref,
):
    ff = m_ref.shape[2]
    i, j = iotas()
    row = lax.broadcasted_iota(jnp.int32, (SEQ, 1), 0)
    valid = row < len_ref[pl.program_id(0)]
    squares = 0.0
    for k in range(n):
        hf = h_ref[k].astype(f32)
        squares = squares + jnp.sum(hf * hf, axis=1, keepdims=True)
    r = lax.rsqrt(squares * (1.0 / (n * h_ref.shape[2])) + 1e-6)
    for k in range(n):
        gain = misc_ref[k][7:8, :].astype(f32)
        n2_ref[k] = (h_ref[k].astype(f32) * r * gain).astype(bf16)
    r_ref[...] = r
    both = []
    total = 0.0
    for c, w_ref in enumerate((wa_ref, wb_ref)):
        place = side_ref[0] ^ c
        gate_up = 0.0
        dm = 0.0
        for k in range(n):
            gate_up = gate_up + dot_of(n2_ref[k], w_ref[k, :, : 2 * ff], 1, 0)
            dm = dm + dot_of(g_ref[k], w_ref[k, :, 2 * ff :], 1, 0)
        gate = gate_up[:, :ff]
        up = gate_up[:, ff:]
        sig = 1.0 / (1.0 + jnp.exp(-gate))
        active = gate * sig
        m_ref[place] = jnp.where(valid, active * up, 0.0).astype(bf16)
        dm = jnp.where(valid, dm, 0.0)
        dgate = dm * up * sig * (1.0 + gate * (1.0 - sig))
        dup = dm * active
        total = total + jnp.sum(dgate * gate + dup * up, axis=1, keepdims=True)
        d = jnp.concatenate([dgate, dup], axis=1).astype(bf16)
        d_ref[place] = d
        both.append(d)
    sum_ref[0] = to_row(total, i == j)
    for k in range(n):
        dn = dot_of(both[0], wa_ref[k, :, : 2 * ff], 1, 1)
        dn = dn + dot_of(both[1], wb_ref[k, :, : 2 * ff], 1, 1)
        dn_ref[k] = dn.astype(dn_ref.dtype)


def feed_forward(lens, side, h, g, wa, wb, misc, out_type):
    n, half, part = h.shape
    blocks = half // SEQ
    cols = wa.shape[2]
    ff = cols // 3
    lines = misc.shape[1]
    return pl.pallas_call(
        functools.partial(ffn_kernel, n),
        out_shape=[
            shape(n, half, part),
            shape(2, half, ff),
            shape(2, half, 2 * ff),
            shape(n, half, part, dtype=out_type),
            shape(blocks, 1, SEQ, dtype=f32),
            shape(half, 1, dtype=f32),
        ],
        grid_spec=pltpu.PrefetchScalarGridSpec(
            num_scalar_prefetch=2,
            grid=(blocks,),
            in_specs=[stack_block(n, SEQ, part)] * 2
            + [whole(n, part, cols)] * 2
            + [whole(n, lines, part)],
            out_specs=[
                stack_block(n, SEQ, part),
                stack_block(2, SEQ, ff),
                stack_block(2, SEQ, 2 * ff),
                stack_block(n, SEQ, part),
                lead_block(1, SEQ),
                rows_block(SEQ, 1),
            ],
        ),
        compiler_params=pltpu.CompilerParams(vmem_limit_bytes=VMEM_LIMIT),
        cost_estimate=cost(2 * half * part * n * 10 * ff, 12000000),
    )(lens, side, h, g, wa, wb, misc)


def ffn_out_kernel(n, side_ref, one_ref, two_ref, wa_ref, wb_ref, own_ref, far_ref):
    ff = one_ref.shape[2]
    for m_ref, out_ref in ((one_ref, own_ref), (two_ref, far_ref)):
        first, second = m_ref[side_ref[0]], m_ref[side_ref[0] ^ 1]
        for k in range(n):
            total = dot_of(first, wa_ref[k, :, 2 * ff :], 1, 1)
            total = total + dot_of(second, wb_ref[k, :, 2 * ff :], 1, 1)
            out_ref[k] = total.astype(out_ref.dtype)


def feed_forward_out(side, own, far, wa, wb):
    _, half, ff = own.shape
    n, part, cols = wa.shape
    return pl.pallas_call(
        functools.partial(ffn_out_kernel, n),
        out_shape=[shape(n, half, part, dtype=f32), shape(n, half, part)],
        grid_spec=pltpu.PrefetchScalarGridSpec(
            num_scalar_prefetch=1,
            grid=(half // SEQ,),
            in_specs=[stack_block(2, SEQ, ff)] * 2 + [whole(n, part, cols)] * 2,
            out_specs=[stack_block(n, SEQ, part)] * 2,
        ),
        compiler_params=pltpu.CompilerParams(vmem_limit_bytes=VMEM_LIMIT),
        cost_estimate=cost(8 * half * part * n * ff, 12000000),
    )(side, own, far, wa, wb)


def back_kernel(n, flag_ref, a_ref, b_ref, l_ref, w_ref, misc_ref, out_ref):
    b = b_ref[0]
    b = jnp.where(flag_ref[0] > 0, b, jnp.zeros_like(b))
    d = jnp.concatenate([a_ref[0], b], axis=1)
    line = l_ref[0]
    for k in range(n):
        total = dot_of(d, w_ref[k], 1, 1) + dot_of(line, misc_ref[k], 0, 0)
        out_ref[k] = total.astype(out_ref.dtype)


def project_back(flag, a, start, b, lines, w, misc, out_type):
    n, part, cols = w.shape
    blocks = b.shape[0]
    rows = misc.shape[1]
    return pl.pallas_call(
        functools.partial(back_kernel, n),
        out_shape=shape(n, blocks * SEQ, part, dtype=out_type),
        grid_spec=pltpu.PrefetchScalarGridSpec(
            num_scalar_prefetch=1,
            grid=(blocks,),
            in_specs=[
                pl.BlockSpec((1, SEQ, 4 * HD), lambda g, *p: (g + start, 0, 0)),
                lead_block(SEQ, 4 * HD),
                lead_block(rows, SEQ),
            ]
            + [whole(n, part, cols), whole(n, rows, part)],
            out_specs=stack_block(n, SEQ, part),
        ),
        compiler_params=pltpu.CompilerParams(vmem_limit_bytes=VMEM_LIMIT),
        cost_estimate=cost(2 * blocks * SEQ * part * n * cols, 8000000),
    )(flag, a, b, lines, w, misc)


def weight_call(kernel, idx, picked, rest, cols, flops, flags=0):
    count = idx.shape[0] - flags
    n, half, part = picked[0].shape
    pick = pl.BlockSpec((1, half, part), lambda g, *p: (p[0][g], 0, 0))
    return pl.pallas_call(
        kernel,
        out_shape=shape(count, part, cols),
        grid_spec=pltpu.PrefetchScalarGridSpec(
            num_scalar_prefetch=1,
            grid=(count,),
            in_specs=[pick] * len(picked) + [whole(*x.shape) for x in rest],
            out_specs=lead_block(part, cols),
        ),
        compiler_params=pltpu.CompilerParams(vmem_limit_bytes=VMEM_LIMIT),
        cost_estimate=cost(flops * count, 6000000),
    )(idx, *picked, *rest)


def ffn_weight_kernel(c, idx_ref, n1, n2, g1, g2, d1, d2, m1, m2, out_ref):
    cols = d1.shape[2]
    total = dot_of(n1[0], d1[c], 0, 0) + dot_of(n2[0], d2[c], 0, 0)
    out_ref[0, :, :cols] = total.astype(bf16)
    total = dot_of(g1[0], m1[c], 0, 0) + dot_of(g2[0], m2[c], 0, 0)
    out_ref[0, :, cols:] = total.astype(bf16)


def own_weight_kernel(idx_ref, n1, n2, d, out_ref):
    total = dot_of(n1[0], d[0], 0, 0) + dot_of(n2[0], d[1], 0, 0)
    out_ref[0] = total.astype(bf16)


def shared_weight_kernel(idx_ref, n1, n2, d, l1, l2, out_ref):
    left = jnp.where(idx_ref[idx_ref.shape[0] - 1] == 0, n1[0], n2[0])
    cols = d.shape[1]
    out_ref[0, :, :cols] = dot_of(left, d[...], 0, 0).astype(bf16)
    lines = dot_of(n1[0], l1[...], 0, 1) + dot_of(n2[0], l2[...], 0, 1)
    out_ref[0, :, cols:] = lines.astype(bf16)


def own_head(k):
    return (3 * k + 1) // 2


def shared_head(q):
    return 1 + 3 * q


def head_cols(h):
    return slice(h * HD, (h + 1) * HD)


def mix_kernel(n, half, place_ref, w_ref, o_ref, own_ref, far_ref):
    for p, out_ref in enumerate((own_ref, far_ref)):
        second = place_ref[0] ^ p
        total = 0.0
        for k in range(n):
            ok = o_ref[k, p * half : (p + 1) * half, :]
            total = total + dot_of(ok, w_ref[:, head_cols(own_head(k))], 1, 1)
        for q in range(n // 2):
            one, two = o_ref[2 * q, 2 * half :, :], o_ref[2 * q + 1, 2 * half :, :]
            ob = jnp.where(second == 0, one, two)
            total = total + dot_of(ob, w_ref[:, head_cols(shared_head(q))], 1, 1)
        out_ref[...] = total


def attention_out(place, w_out, o, half):
    n = o.shape[0]
    part, cols = w_out.shape
    return pl.pallas_call(
        functools.partial(mix_kernel, n, half),
        out_shape=[shape(half, part, dtype=f32)] * 2,
        grid_spec=pltpu.PrefetchScalarGridSpec(
            num_scalar_prefetch=1,
            grid=(1,),
            in_specs=[whole(part, cols), whole(*o.shape)],
            out_specs=[whole(half, part)] * 2,
        ),
        compiler_params=pltpu.CompilerParams(vmem_limit_bytes=VMEM_LIMIT),
        cost_estimate=cost(4 * half * part * cols, 4000000),
    )(place, w_out, o)


def unmix_kernel(n, half, place_ref, w_ref, own_ref, far_ref, out_ref):
    place = place_ref[0]
    da = (own_ref[...], far_ref[...])
    for k in range(n):
        w = w_ref[:, head_cols(own_head(k))]
        for p in range(2):
            out_ref[k, p * half : (p + 1) * half, :] = dot_of(da[p], w, 1, 0).astype(bf16)
    for q in range(n // 2):
        w = w_ref[:, head_cols(shared_head(q))]
        both = [dot_of(d, w, 1, 0).astype(bf16) for d in da]
        out_ref[2 * q, 2 * half :, :] = jnp.where(place == 0, both[0], both[1])
        out_ref[2 * q + 1, 2 * half :, :] = jnp.where(place == 0, both[1], both[0])


def attention_out_back(place, w_out, own, far, n):
    half, part = own.shape
    cols = w_out.shape[1]
    return pl.pallas_call(
        functools.partial(unmix_kernel, n, half),
        out_shape=shape(n, 3 * half, HD),
        grid_spec=pltpu.PrefetchScalarGridSpec(
            num_scalar_prefetch=1,
            grid=(1,),
            in_specs=[whole(part, cols), whole(half, part), whole(half, part)],
            out_specs=whole(n, 3 * half, HD),
        ),
        compiler_params=pltpu.CompilerParams(vmem_limit_bytes=VMEM_LIMIT),
        cost_estimate=cost(4 * half * part * cols, 4000000),
    )(place, w_out, own, far)


def out_grad_kernel(n, half, place_ref, own_ref, far_ref, o_ref, out_ref):
    place = place_ref[0]
    da = (own_ref[...], far_ref[...])
    for k in range(n):
        total = dot_of(da[0], o_ref[k, :half, :], 0, 0)
        total = total + dot_of(da[1], o_ref[k, half : 2 * half, :], 0, 0)
        out_ref[:, head_cols(own_head(k))] = total.astype(bf16)
    for q in range(n // 2):
        one, two = o_ref[2 * q, 2 * half :, :], o_ref[2 * q + 1, 2 * half :, :]
        total = dot_of(da[0], jnp.where(place == 0, one, two), 0, 0)
        total = total + dot_of(da[1], jnp.where(place == 0, two, one), 0, 0)
        out_ref[:, head_cols(shared_head(q))] = total.astype(bf16)


def out_gradient(place, own, far, o, cols):
    n = o.shape[0]
    half, part = own.shape
    return pl.pallas_call(
        functools.partial(out_grad_kernel, n, half),
        out_shape=shape(part, cols),
        grid_spec=pltpu.PrefetchScalarGridSpec(
            num_scalar_prefetch=1,
            grid=(1,),
            in_specs=[whole(half, part), whole(half, part), whole(*o.shape)],
            out_specs=whole(part, cols),
        ),
        compiler_params=pltpu.CompilerParams(vmem_limit_bytes=VMEM_LIMIT),
        cost_estimate=cost(4 * half * part * cols, 4000000),
    )(place, own, far, o)


def swap(x, axis, size, k):
    return lax.ppermute(x, axis, [(n, n ^ k) for n in range(size)])


def shift_rows(x, start, size):
    return lax.dynamic_slice_in_dim(x, start, size, axis=0)


def exchange(x, axis):
    return lax.all_to_all(x, axis, split_axis=0, concat_axis=0, tiled=True)


def to_all(x, axis, n):
    return exchange(jnp.broadcast_to(x[None], (n,) + x.shape), axis)


def after(x, *others):
    return lax.optimization_barrier((x,) + others)[0]


def per_device(
    dp_size,
    wid_size,
    tokens,
    cotangent,
    lengths,
    w_project,
    w_beta,
    w_out,
    w_gate_up,
    w_down,
    gain_attn,
    gain_ffn,
):
    wid = lax.axis_index("wid")
    hid = lax.axis_index("hid")
    dp = lax.axis_index("dp")
    ws = range(wid_size)
    rows, part = tokens.shape
    half = rows // 2
    width = part * wid_size
    ff = w_down.shape[1] // wid_size
    heads = w_beta.shape[1]
    per_half = half // SEQ

    def hid_swap(x):
        return swap(x, "hid", 2, 1)

    half_b = (wid & 1) ^ hid
    my_head = own_head(wid)
    my_shared = shared_head(wid // 2)

    x_own = shift_rows(tokens, hid * half, half)
    g_own = shift_rows(cotangent, hid * half, half)

    spare = jnp.zeros((16 - heads - 3, part), bf16)
    length_line = jnp.broadcast_to(lengths.astype(bf16)[:, None], (1, part))
    misc_here = jnp.concatenate(
        [w_beta.T, gain_attn[None], gain_ffn[None], length_line, spare], axis=0
    )
    gathered = to_all(jnp.concatenate([x_own, misc_here], axis=0), "wid", wid_size)
    xs_own, misc = gathered[:, :half], gathered[:, half:]
    xs_far = hid_swap(xs_own)
    len_abs = misc[:, heads + 2, 0].astype(jnp.int32)

    def heads_for(w):
        a = w_project[:, :, head_cols(own_head(w))].reshape(part, 4 * HD)
        b = w_project[:, :, head_cols(shared_head(w // 2))].reshape(part, 4 * HD)
        return jnp.concatenate([a, b], axis=1)

    proj_w = exchange(jnp.stack([heads_for(w) for w in ws]), "wid")

    side = dp & 1
    ffh = ff // 2

    def ffn_for(w):
        at = w * ff + side * ffh
        cut = lax.dynamic_slice_in_dim(w_gate_up, at, ffh, axis=2).reshape(part, 2 * ffh)
        return jnp.concatenate([cut, lax.dynamic_slice_in_dim(w_down, at, ffh, axis=1)], axis=1)

    ffn_own = exchange(after(jnp.stack([ffn_for(w) for w in ws]), proj_w), "wid")
    ffn_other = swap(ffn_own, "dp", dp_size, 1)
    side = side.astype(jnp.int32)[None]

    def lens_of(place):
        return lax.dynamic_slice_in_dim(len_abs, place * per_half, per_half)

    lens_own, lens_far = lens_of(hid), lens_of(1 - hid)
    lens = jnp.concatenate([lens_own, lens_far, lens_of(wid & 1)])
    slot = jnp.arange(SEQ, dtype=jnp.int32)
    valid_half = (slot[None] < lens_own[:, None]).astype(f32).reshape(half, 1)

    a_own, b_own, l_own, r_own, n1_own = project(xs_own, proj_w, misc)
    a_far, b_far, l_far, r_far, n1_far = project(xs_far, proj_w, misc)

    def pick_b(own, far):
        return jnp.where(half_b == 0, own, far)

    pairs = jnp.concatenate([a_own, a_far, pick_b(b_own, b_far)], axis=0)

    def line_of(lines, h):
        return lax.dynamic_slice_in_dim(lines, h, 1, axis=1)

    logit_pairs = jnp.concatenate(
        [
            line_of(l_own, my_head),
            line_of(l_far, my_head),
            line_of(pick_b(l_own, l_far), my_shared),
        ],
        axis=0,
    )
    attended, inv, carry, prob = attention_forward(lens, pairs, logit_pairs)
    o_all = to_all(after(attended, ffn_own).reshape(-1, HD), "wid", wid_size)
    place = hid.astype(jnp.int32)[None]
    attn_own, attn_far = attention_out(place, w_out, o_all, half)
    hidden = x_own.astype(f32) + attn_own + hid_swap(attn_far)

    gain_one = gain_attn[None].astype(f32)
    gain_two = gain_ffn[None].astype(f32)
    hs_own = to_all(hidden.astype(bf16), "wid", wid_size)
    hs_far = hid_swap(hs_own)
    gs_own = exchange(
        after(jnp.broadcast_to(g_own[None], (wid_size,) + g_own.shape), hs_own, ffn_other), "wid"
    )
    gs_far = hid_swap(gs_own)
    n2_own, m_own, d_own, dn_own, s_own, r2_own = feed_forward(
        lens_own, side, hs_own, gs_own, ffn_own, ffn_other, misc, f32
    )
    n2_far, m_far, d_far, dn_far, s_far, r2_far = feed_forward(
        lens_far, side, hs_far, gs_far, ffn_own, ffn_other, misc, bf16
    )

    def partial(own, far):
        return (own + hid_swap(far).astype(f32)).astype(bf16)

    def line_sum(own, far, late):
        here = (own + hid_swap(far)).reshape(-1, 128)
        others = [swap(here, "wid", wid_size, k) for k in range(1, wid_size)]
        others = lax.optimization_barrier((*others, late))[:-1]
        total = here + sum(others)
        return total.reshape(-1, 1) * (1.0 / width)

    dn_here = partial(dn_own, dn_far)
    dn_got = exchange(dn_here, "wid")
    mean_two = line_sum(s_own, s_far, dn_got)
    grad_normed_two = jnp.sum(dn_got.astype(f32), axis=0)

    chunk = width // dp_size
    direct = dp_size == wid_size
    sub = chunk // wid_size

    def dp_pieces(make, odd_first):
        ts = range(1 if odd_first else 0, dp_size, 2)
        if direct:
            return make(jnp.stack([dp ^ t for t in ts]).astype(jnp.int32))
        full = make(jnp.arange(wid_size, dtype=jnp.int32)).reshape(width, -1)
        return jnp.stack([shift_rows(full, (dp ^ t) * chunk, chunk) for t in ts])

    def dp_send(held, k=2):
        return held[0::2], swap(held[1::2].astype(bf16), "dp", dp_size, k)

    def dp_take(keep, got, k=2):
        held = keep + got.astype(f32)
        while held.shape[0] > 1:
            k *= 2
            keep, got = dp_send(held, k)
            held = keep + got.astype(f32)
        return held[0]

    def dp_sum(pieces, *late):
        odd, even = jnp.stack(pieces[1::2]), jnp.stack(pieces[0::2])
        got = after(swap(odd.astype(bf16), "dp", dp_size, 1), *late)
        return dp_take(*dp_send(even.astype(f32) + got.astype(f32)))

    def to_rows(x):
        return exchange(x.astype(bf16).reshape(wid_size, sub, -1), "wid")

    d_then = after(d_own, dn_here)

    def ffn_weights(c, then):
        def make(idx):
            return weight_call(
                functools.partial(ffn_weight_kernel, c),
                idx,
                (n2_own, n2_far, gs_own, gs_far),
                (then, d_far, m_own, m_far),
                3 * ffh,
                12 * half * part * ffh,
            )

        return make

    odd_one = dp_pieces(ffn_weights(0, d_then), True)
    got_one = swap(odd_one, "dp", dp_size, 1)
    d_then = after(d_then, odd_one)
    odd_two = dp_pieces(ffn_weights(1, d_then), True)
    got_two = swap(odd_two, "dp", dp_size, 1)
    d_then = after(d_then, odd_two)
    even_one = dp_pieces(ffn_weights(0, d_then), False)
    even_two = dp_pieces(ffn_weights(1, d_then), False)

    grad_half = g_own.astype(f32) * valid_half
    grad_hidden = grad_half + r2_own * (
        grad_normed_two * gain_two - r2_own * hidden * mean_two
    )
    gain_two_part = jnp.sum(grad_normed_two * hidden * r2_own, axis=0)
    da_own = after(grad_hidden.astype(bf16), even_one, even_two)
    da_far = hid_swap(da_own)
    do_here = attention_out_back(place, w_out, da_own, da_far, wid_size)
    do_pieces = exchange(do_here, "wid")
    ffn_own_out, ffn_far_out = feed_forward_out(
        side, after(m_own, do_here, got_one), m_far, ffn_own, ffn_other
    )
    g_out = out_gradient(place, after(da_own, do_here, got_one), da_far, o_all, w_out.shape[1])
    do_got = do_pieces.reshape(wid_size, -1, SEQ, HD)
    got_one = after(got_one, do_got)
    held_one = even_one.astype(f32) + got_one.astype(f32)
    keep_one, next_one = dp_send(held_one)

    pairs_a, lines_a, sums_a = attention_backward(
        lens, pairs, logit_pairs, inv, carry, prob, after(do_got, held_one, ffn_far_out), 0, 2 * per_half
    )

    head_iota = lax.broadcasted_iota(jnp.int32, (1, 16, 1), 1)
    right_own = pairs_a.reshape(2, half, 4 * HD)

    def own_weights(idx):
        return weight_call(
            own_weight_kernel,
            idx,
            (n1_own, n1_far),
            (right_own,),
            4 * HD,
            4 * half * part * 4 * HD,
        )

    own_odd = dp_pieces(own_weights, True)
    own_got = swap(own_odd, "dp", dp_size, 1)
    pairs_b, lines_b, sums_b = attention_backward(
        lens, pairs, logit_pairs, inv, carry, prob, after(do_got, own_odd), 2 * per_half, per_half
    )

    def spread(a, b, at):
        own = a[at * per_half : (at + 1) * per_half]
        return own, jnp.where(half_b == at, b, 0.0)

    def lines_at(at):
        own, shared = spread(lines_a, lines_b, at)
        own = jnp.where(head_iota == my_head, own, 0.0)
        shared = jnp.where(head_iota == my_shared, shared, 0.0)
        return (own + shared).astype(bf16)

    def flat_lines(x):
        flat = jnp.swapaxes(x, 0, 1).reshape(16, half)
        return jnp.concatenate([flat, jnp.zeros((128 - 16, half), bf16)], axis=0)

    lines_own, lines_far = lines_at(0), lines_at(1)
    flat_own, flat_far = flat_lines(lines_own), flat_lines(lines_far)
    right_shared = after(pairs_b, next_one).reshape(half, 4 * HD)

    def shared_weights(idx):
        return weight_call(
            shared_weight_kernel,
            jnp.concatenate([idx, half_b.astype(jnp.int32)[None]]),
            (n1_own, n1_far),
            (right_shared, flat_own, flat_far),
            5 * HD,
            2 * half * part * 5 * HD,
            1,
        )

    shared_odd = dp_pieces(shared_weights, True)
    shared_got = swap(shared_odd, "dp", dp_size, 1)
    right_own = after(right_own, own_got)
    right_shared = after(right_shared, own_got)
    flags = [(half_b == p).astype(jnp.int32)[None] for p in range(2)]
    got_two = after(got_two, shared_odd)
    held_two = even_two.astype(f32) + got_two.astype(f32)
    keep_two, next_two = dp_send(held_two)
    back_b = after(pairs_b, shared_odd, held_two, own_got)
    dn1_far = project_back(flags[1], pairs_a, per_half, back_b, lines_far, proj_w, misc, bf16)
    own_even = dp_pieces(own_weights, False)
    keep_own, next_own = dp_send(own_even.astype(f32) + own_got.astype(f32))
    shared_even = dp_pieces(shared_weights, False)
    keep_shared, next_shared = dp_send(shared_even.astype(f32) + shared_got.astype(f32))
    back_b = after(back_b, next_two, keep_own, shared_got)
    dn1_own = project_back(flags[0], pairs_a, 0, back_b, lines_own, proj_w, misc, f32)
    dn1_here = after(partial(dn1_own, dn1_far), next_own, keep_shared)
    dn1_got = exchange(dn1_here, "wid")
    ffn_far_out = after(ffn_far_out, pairs_b)
    ffn_here = after(partial(ffn_own_out, ffn_far_out), dn1_got)
    ffn_back = exchange(ffn_here, "wid")
    next_shared = after(next_shared, dn1_got)
    sums = [sum(spread(sums_a, sums_b, p)) for p in range(2)]
    mean_one = line_sum(*sums, dn1_got)
    grad_normed_one = jnp.sum(dn1_got.astype(f32), axis=0)
    ffn = jnp.sum(ffn_back.astype(f32), axis=0)

    source = x_own.astype(f32)
    r1_half = r_own.reshape(half, 1)
    gain_one_part = jnp.sum(grad_normed_one * source * r1_half, axis=0)
    input_half = grad_hidden + r1_half * (
        grad_normed_one * gain_one - r1_half * source * mean_one
    )

    def whole_rows(x):
        other = hid_swap(x)
        return jnp.concatenate(
            [jnp.where(hid == 0, x, other), jnp.where(hid == 0, other, x)], axis=0
        )

    parts = [
        dp_take(keep_one, next_one),
        dp_take(keep_two, next_two),
        dp_take(keep_own, next_own),
        dp_take(keep_shared, next_shared),
    ]
    g_all = jnp.concatenate(parts, axis=1).astype(bf16)
    input_grad = whole_rows(after(input_half.astype(bf16), g_all))
    output = whole_rows(after(((hidden + ffn) * valid_half).astype(bf16), g_all))

    fine = part // dp_size
    to_place = [
        (c * wid_size + w, w * dp_size + c) for c in range(dp_size) for w in range(wid_size)
    ]

    def dp_fine(x, *late):
        return dp_sum([shift_rows(x, (dp ^ t) * fine, fine) for t in range(dp_size)], *late)

    out_out = lax.ppermute(dp_fine(g_out, g_all), ("dp", "wid"), to_place)
    gain_part = after(jnp.stack([gain_one_part, gain_two_part], axis=1), g_all)
    gain_part = gain_part + hid_swap(gain_part)
    gain_sum = lax.ppermute(dp_fine(gain_part), ("dp", "wid"), to_place)

    all_rows = to_rows(after(g_all, ffn_back))
    got = all_rows[:, :, : 3 * ff].reshape(wid_size, sub, 2, 3 * ffh)
    pieces = [got[w, :, c] for w in ws for c in range(2)]
    gate, up, down = (
        jnp.concatenate([p[:, k * ffh : (k + 1) * ffh] for p in pieces], axis=1) for k in range(3)
    )
    out_gate_up = jnp.stack([gate, up], axis=1).astype(f32)
    out_down = down.astype(f32)

    got = all_rows[:, :, 3 * ff :].astype(f32)
    a = [got[w, :, : 4 * HD] for w in ws]
    b = [got[w, :, 4 * HD : 8 * HD] for w in ws]
    proj_rows = [a[0], b[0] + b[1], a[1], a[2], b[2] + b[3], a[3]]
    out_project = jnp.concatenate([p.reshape(sub, 4, HD) for p in proj_rows], axis=2)
    out_beta = jnp.sum(got[:, :, 8 * HD : 8 * HD + heads], axis=0)


    return (
        output,
        input_grad,
        out_project,
        out_beta,
        out_out,
        out_gate_up,
        out_down,
        gain_sum[:, 0],
        gain_sum[:, 1],
    )


def solution(mesh):
    return jax.shard_map(
        functools.partial(per_device, mesh.shape["dp"], mesh.shape["wid"]),
        mesh=mesh,
        in_specs=(
            P("dp", "wid"),
            P("dp", "wid"),
            P(("dp", "wid")),
            P("wid", None, "hid"),
            P("wid", "hid"),
            P("wid", "hid"),
            P("wid", None, "hid"),
            P("wid", "hid"),
            P("wid"),
            P("wid"),
        ),
        out_specs=(
            P("dp", "wid"),
            P("dp", "wid"),
            P(("dp", "wid"), None, "hid"),
            P(("dp", "wid"), "hid"),
            P(("dp", "wid"), "hid"),
            P(("dp", "wid"), None, "hid"),
            P(("dp", "wid"), "hid"),
            P(("dp", "wid")),
            P(("dp", "wid")),
        ),
        check_vma=False,
    )
```

time: 580 us -> 542 us (0.934)
  Pallas kernels: 29.5 us -> 111 us
  matrix products: 44.1 us -> 0 us
  other arithmetic: 77.2 us -> 49.8 us
  starting transfers between devices: 111 us -> 83.6 us
  waiting for transfers between devices: 239 us -> 224 us
    ppermute x93 -> x32, waiting for transfers between devices: 239 us -> 108 us  [swap(): return lax.ppermute(x, axis, [(n, n ^ k) for n in range(size)])]
    all_to_all x0 -> x11, waiting for transfers between devices: none -> 117 us  [exchange(): return lax.all_to_all(x, axis, split_axis=0, concat_axis=0, tiled=True)]
    pallas_call x1 -> x20, Pallas kernels: 13.9 us -> 95.7 us  [the longest x8 22.2 us: weight_call(): pl.pallas_call(kernel, out_shape=shape(count, part, cols), grid_spec=pltp...]
    ppermute x93 -> x32, starting transfers between devices: 107 us -> 35 us  [swap(): return lax.ppermute(x, axis, [(n, n ^ k) for n in range(size)])]
    all_to_all x0 -> x11, starting transfers between devices: none -> 47.3 us  [exchange(): return lax.all_to_all(x, axis, split_axis=0, concat_axis=0, tiled=True)]
    dot_general x16 -> x0, matrix products: 44.1 us -> none  [dot_of(): lax.dot_general(a, b, (((ca,), (cb,)), ((), ())), preferred_element_type=...]
    select_n x5 -> x2, other arithmetic: 15.5 us -> 0.06 us  [the longest x1 0.06 us: pick_b(): return jnp.where(half_b == 0, own, far)]
    reduce_sum x4 -> x5, other arithmetic: 18.5 us -> 6.38 us  [the longest x1 1.8 us: per_device(): grad_normed_two = jnp.sum(dn_got.astype(f32), axis=0)]
  transfers between devices with their start and end apart: 95 -> 45, of which waited for: 35 -> 20; matrix products, arithmetic and copies ran while one was open for 29% -> 10% of each run, Pallas kernels for 2% -> 18%
where the time goes in v2:
time: 542 us; the launch traced here: 535 us
  waiting for transfers between devices  224 us (41%)
  Pallas kernels  111 us (20%)
  starting transfers between devices  83.6 us (15%)
  local copies, waits for them, and re-layouts  62.5 us (12%)
  other arithmetic  49.8 us (9%)
    all_to_all x11, waiting for transfers between devices, exchange(): return lax.all_to_all(x, axis, split_axis=0, concat_axis=0, tiled=True)  117 us
    ppermute x32, waiting for transfers between devices, swap(): return lax.ppermute(x, axis, [(n, n ^ k) for n in range(size)])  108 us
    all_to_all x11, starting transfers between devices, exchange(): return lax.all_to_all(x, axis, split_axis=0, concat_axis=0, tiled=True)  47.3 us
    unnamed x232, local copies, waits for them, and re-layouts  36.7 us
    ppermute x32, starting transfers between devices, swap(): return lax.ppermute(x, axis, [(n, n ^ k) for n in range(size)])  35 us
    pallas_call x8, Pallas kernels, weight_call(): pl.pallas_call(kernel, out_shape=shape(count, part, cols), grid_spec=pltp...  22.2 us
    pallas_call x2, Pallas kernels, feed_forward(): pl.pallas_call(functools.partial(ffn_kernel, n), out_shape=[shape(n, half...  22.1 us
    pallas_call x2, Pallas kernels, attention_backward(): pl.pallas_call(functools.partial(backward_kernel, 1, start), out_shape=[j...  16 us
  transfers between devices with their start and end apart: 45, of which 20 were waited for; matrix products, arithmetic and copies ran while one was open for 10% of the time, Pallas kernels for 18%

profile of v2, /device:TPU:0, one launch (start us, length us, event | category | flops | bytes accessed | tf_op | source)
XLA Modules:
  0.0 534.5 jit_solution(17832243254578710521)
XLA Ops:
  6.0 5.2 all-to-all-start
  16.3 14.7 %all-to-all-done = bf16[4,528,384]{2,1,0:T(8,128)(2,1)S(1)} async-done(((bf16[4,528,384]{2,1,0:T(8,128)(2,1)}), bf16[4,528,384]{2,1,0:T(8,128)(2,1)S(1)}, u32[]{:S(2)}, u32[]{:S(2)}) %all-to-all-start) | async-done | bytes 1622048 | tf_op jit(solution)/shard_map/all_to_all | solution.py:590
  43.6 28.0 %all-to-all-done.1.w_ref = bf16[4,384,1024]{2,1,0:T(8,128)(2,1)S(1)} async-done(((bf16[4,384,1024]{2,1,0:T(8,128)(2,1)}), bf16[4,384,1024]{2,1,0:T(8,128)(2,1)S(1)}, u32[]{:S(2)}, u32[]{:S(2)}) %all-to-all-start.1) | async-done | bytes 3145760 | tf_op jit(solution)/shard_map/all_to_all | solution.py:590
  73.3 4.1 all-to-all-start.2
  79.2 5.4 %shard_map.169 = (bf16[2,256,512]{2,1,0:T(8,128)(2,1)S(1)}, bf16[2,256,512]{2,1,0:T(8,128)(2,1)S(1)}, f32[2,16,256]{2,1,0:T(8,128)S(1)}, f32[2,1,256]{2,1,0:T(1,128)S(1)}, bf16[4,512,384]{2,1,0:T(8,128)(2,1)S(1)}) custom-call(bf16[4,512,384]{2,1,0:T(8,128)(2,1)} %slice.302.x_ref, bf16[4,384,1024]{2,1,0:T(8,128)(2,1)} %copy-done.51, ...), custom_call_target="tpu_custom_call" | custom-call | flops 1610612 | bytes 8000 | tf_op jit(solution)/shard_map/pallas_call | solution.py:261
  86.4 5.7 %shard_map.170 = (bf16[2,256,512]{2,1,0:T(8,128)(2,1)S(1)}, bf16[2,256,512]{2,1,0:T(8,128)(2,1)S(1)}, f32[2,16,256]{2,1,0:T(8,128)S(1)}, f32[2,1,256]{2,1,0:T(1,128)}, bf16[4,512,384]{2,1,0:T(8,128)(2,1)S(1)}) custom-call(bf16[4,512,384]{2,1,0:T(8,128)(2,1)} %collective-permute-done.x_ref, bf16[4,384,1024]{2,1,0:T(8,128)(2,1)} %copy-done.51, ...), custom_call_target="tpu_custom_call" | custom-call | flops 1610612 | bytes 8000 | tf_op jit(solution)/shard_map/pallas_call | solution.py:261
  94.7 15.0 %shard_map.171 = (bf16[6,256,128]{2,1,0:T(8,128)(2,1)S(1)}, f32[6,256,256]{2,1,0:T(8,128)S(1)}, f32[6,256,256]{2,1,0:T(8,128)S(1)}, f32[6,256,256]{2,1,0:T(8,128)S(1)}) custom-call(s32[6]{0:T(128)S(1)} %pad_add_fusion.len_ref, bf16[6,256,512]{2,1,0:T(8,128)(2,1)} %pad_maximum_fusion.3.x_ref, f32[6,1,256]{2,1,0:T(1,128)S(1)} %pad_maximum_fusion.11.l_ref), custom_call_target="tpu_custom_call" | custom-call | flops 9600000 | bytes 6600 | tf_op jit(solution)/shard_map/pallas_call | solution.py:167
  114.7 4.5 all-to-all-start.3
  120.9 17.1 %all-to-all-done.3.o_ref = bf16[4,1536,128]{2,1,0:T(8,128)(2,1)} async-done(((bf16[4,1536,128]{2,1,0:T(8,128)(2,1)}), bf16[4,1536,128]{2,1,0:T(8,128)(2,1)}, u32[]{:S(2)}, u32[]{:S(2)}) %all-to-all-start.3) | async-done | bytes 1572896 | tf_op jit(solution)/shard_map/all_to_all | solution.py:590
  145.5 4.4 all-to-all-start.4
  150.9 20.6 %collective-permute-done.2.wb_ref = bf16[4,384,768]{2,1,0:T(8,128)(2,1)} collective-permute-done((bf16[4,384,768]{2,1,0:T(8,128)(2,1)S(1)}, bf16[4,384,768]{2,1,0:T(8,128)(2,1)}, u32[]{:S(2)}, u32[]{:S(2)}) %collective-permute-start.2) | collective-permute-done | bytes 2359328 | tf_op jit(solution)/shard_map/ppermute | solution.py:582
  177.0 17.5 %all-to-all-done.5.g_ref.g1 = bf16[4,512,384]{2,1,0:T(8,128)(2,1)S(1)} async-done(((bf16[4,512,384]{2,1,0:T(8,128)(2,1)}), bf16[4,512,384]{2,1,0:T(8,128)(2,1)S(1)}, u32[]{:S(2)}, u32[]{:S(2)}) %all-to-all-start.5) | async-done | bytes 1572896 | tf_op jit(solution)/shard_map/all_to_all | solution.py:590
  199.1 10.9 %shard_map.174 = (bf16[4,512,384]{2,1,0:T(8,128)(2,1)S(1)}, bf16[2,512,256]{2,1,0:T(8,128)(2,1)S(1)}, bf16[2,512,512]{2,1,0:T(8,128)(2,1)S(1)}, bf16[4,512,384]{...) custom-call(s32[2]{0:T(128)S(1)} %get-tuple-element.244.len_ref, s32[1]{0:T(128)} %bitcast.12.side_ref, ...), custom_call_target="tpu_custom_call" | custom-call | flops 4026531 | bytes 12000 | tf_op jit(solution)/shard_map/pallas_call | solution.py:347
  211.3 11.2 %shard_map.173 = (bf16[4,512,384]{2,1,0:T(8,128)(2,1)S(1)}, bf16[2,512,256]{2,1,0:T(8,128)(2,1)S(1)}, bf16[2,512,512]{2,1,0:T(8,128)(2,1)S(1)}, f32[4,512,384]{2...) custom-call(s32[2]{0:T(128)S(1)} %get-tuple-element.242.len_ref, s32[1]{0:T(128)} %bitcast.12.side_ref, ...), custom_call_target="tpu_custom_call" | custom-call | flops 4026531 | bytes 12000 | tf_op jit(solution)/shard_map/pallas_call | solution.py:347
  227.7 4.5 all-to-all-start.6
  240.7 4.4 shard_map.175
  267.7 4.7 all-to-all-start.7
  275.9 15.9 %collective-permute-done.11 = bf16[2,384,768]{2,1,0:T(8,128)(2,1)} collective-permute-done((bf16[2,384,768]{2,1,0:T(8,128)(2,1)}, bf16[2,384,768]{2,1,0:T(8,128)(2,1)}, u32[]{:S(2)}, u32[]{:S(2)}) %collective-permute-start.11) | collective-permute-done | bytes 1179680 | tf_op jit(solution)/shard_map/ppermute | solution.py:582
  292.9 5.7 %shard_map.180 = (f32[4,512,384]{2,1,0:T(8,128)}, bf16[4,512,384]{2,1,0:T(8,128)(2,1)}) custom-call(s32[1]{0:T(128)} %bitcast.12.side_ref, bf16[2,512,256]{2,1,0:T(8,128)(2,1)S(1)} %copy-done.14, bf16[2,512,256]{2,1,0:T(8,128)(2,1)S(1)} %get-tuple-element.102.m2.two_ref, bf16[4,384,768]{2,1,0:T(8,128)(2,1)S(1)} %copy-done.1, ...), custom_call_target="tpu_custom_call" | custom-call | flops 1610612 | bytes 12000 | tf_op jit(solution)/shard_map/pallas_call | solution.py:390
  302.1 10.2 %shard_map.181 = (bf16[4,256,512]{2,1,0:T(8,128)(2,1)S(1)}, f32[4,1,256]{2,1,0:T(1,128)S(1)}, f32[4,1,256]{2,1,0:T(1,128)S(1)}) custom-call(s32[6]{0:T(128)S(1)} %pad_add_fusion.len_ref, bf16[6,256,512]{2,1,0:T(8,128)(2,1)S(1)} %copy-done.6, f32[6,1,256]{2,1,0:T(1,128)S(1)} %pad_maximum_fusion.11.l_ref, f32[6,256,256]{2,1,0:T(8,128)S(1)} %copy-done.19, ...), custom_call_target="tpu_custom_call" | custom-call | flops 5600000 | bytes 5600 | tf_op jit(solution)/shard_map/pallas_call | solution.py:187
  318.6 5.8 %shard_map.183 = (bf16[2,256,512]{2,1,0:T(8,128)(2,1)S(1)}, f32[2,1,256]{2,1,0:T(1,128)S(1)}, f32[2,1,256]{2,1,0:T(1,128)S(1)}) custom-call(s32[6]{0:T(128)S(1)} %pad_add_fusion.len_ref, bf16[6,256,512]{2,1,0:T(8,128)(2,1)S(1)} %copy-done.6, f32[6,1,256]{2,1,0:T(1,128)S(1)} %pad_maximum_fusion.11.l_ref, f32[6,256,256]{2,1,0:T(8,128)S(1)} %copy-done.19, ...), custom_call_target="tpu_custom_call" | custom-call | flops 2800000 | bytes 2800 | tf_op jit(solution)/shard_map/pallas_call | solution.py:187
  324.7 20.6 %collective-permute-done.13 = bf16[1,384,768]{2,1,0:T(8,128)(2,1)S(1)} collective-permute-done((bf16[1,384,768]{2,1,0:T(8,128)(2,1)S(1)}, bf16[1,384,768]{2,1,0:T(8,128)(2,1)S(1)}, u32[]{:S(2)}, u32[]{:S(2)}) %collective-permute-start.13) | collective-permute-done | bytes 589856 | tf_op jit(solution)/shard_map/ppermute | solution.py:582
  351.1 6.0 %shard_map.187 = bf16[4,512,384]{2,1,0:T(8,128)(2,1)} custom-call(s32[1]{0:T(128)} %bitcast.28.flag_ref, bf16[4,256,512]{2,1,0:T(8,128)(2,1)S(1)} %get-tuple-element.116.a_ref, bf16[2,256,512]{2,1,0:T(8,128)(2,1)S(1)} %get-tuple-element.126.b_ref, bf16[2,16,256]{2,1,0:T(8,128)(2,1)S(1)} %get-tuple-element.329.l_ref, bf16[4,384,1024]{2,1,0:T(8,128)(2,1)} %copy-done.51, ...), custom_call_target="tpu_custom_call" | custom-call | flops 1610612 | bytes 8000 | tf_op jit(solution)/shard_map/pallas_call | solution.py:418
  379.6 22.5 %collective-permute-done.16 = bf16[1,384,768]{2,1,0:T(8,128)(2,1)S(1)} collective-permute-done((bf16[1,384,768]{2,1,0:T(8,128)(2,1)S(1)}, bf16[1,384,768]{2,1,0:T(8,128)(2,1)S(1)}, u32[]{:S(2)}, u32[]{:S(2)}) %collective-permute-start.16) | collective-permute-done | bytes 589856 | tf_op jit(solution)/shard_map/ppermute | solution.py:582
  408.6 5.3 shard_map.186
  418.4 4.6 all-to-all-start.8
  430.9 11.4 %all-to-all-done.8 = bf16[4,512,384]{2,1,0:T(8,128)(2,1)} async-done(((bf16[4,512,384]{2,1,0:T(8,128)(2,1)}), bf16[4,512,384]{2,1,0:T(8,128)(2,1)}, u32[]{:S(2)}, u32[]{:S(2)}) %all-to-all-start.8) | async-done | bytes 1572896 | tf_op jit(solution)/shard_map/all_to_all | solution.py:590
  442.3 6.6 %collective-permute-done.20 = bf16[1,384,640]{2,1,0:T(8,128)(2,1)} collective-permute-done((bf16[1,384,640]{2,1,0:T(8,128)(2,1)S(1)}, bf16[1,384,640]{2,1,0:T(8,128)(2,1)}, u32[]{:S(2)}, u32[]{:S(2)}) %collective-permute-start.20) | collective-permute-done | bytes 491552 | tf_op jit(solution)/shard_map/ppermute | solution.py:582
  462.7 7.2 %collective-permute-done.31 = bf16[2,96,2]{1,2,0:T(2,128)(2,1)S(1)} collective-permute-done((bf16[2,96,2]{1,2,0:T(2,128)(2,1)S(1)}, bf16[2,96,2]{1,2,0:T(2,128)(2,1)S(1)}, u32[]{:S(2)}, u32[]{:S(2)}) %collective-permute-start.31) | collective-permute-done | bytes 800 | tf_op jit(solution)/shard_map/ppermute | solution.py:582
  470.3 4.1 collective-permute-done.32
  476.8 5.6 %collective-permute-start.28 = (bf16[1,96,768]{2,1,0:T(8,128)(2,1)}, bf16[1,96,768]{2,1,0:T(8,128)(2,1)}, u32[]{:S(2)}, u32[]{:S(2)}) collective-permute-start(bf16[1,96,768]{2,1,0:T(8,128)(2,1)} %slice.422), channel_id=1, source_target_pairs={{0,16},{8,24},{16,0},{24,8},{1,17},{9,25},{17,1},{25,9},{2,18},{10... | collective-permute-start | bytes 442376 | tf_op jit(solution)/shard_map/ppermute | solution.py:582
  495.0 28.2 %all-to-all-done.10 = bf16[4,96,2688]{2,1,0:T(8,128)(2,1)S(1)} async-done(((bf16[4,96,2688]{2,1,0:T(8,128)(2,1)}), bf16[4,96,2688]{2,1,0:T(8,128)(2,1)S(1)}, u32[]{:S(2)}, u32[]{:S(2)}) %all-to-all-start.10) | async-done | bytes 2064416 | tf_op jit(solution)/shard_map/all_to_all | solution.py:590
  (422 shorter events, 193.6 us)
Async XLA Ops:
  6.0 25.0 %all-to-all-start = ((bf16[4,528,384]{2,1,0:T(8,128)(2,1)}), bf16[4,528,384]{2,1,0:T(8,128)(2,1)S(1)}, u32[]{:S(2)}, u32[]{:S(2)}) async-start(bf16[4,528,384]{2,1,0:T(8,128)(2,1)} %broadcast_in_dim.158), calls=%async_computation | async-start | bytes 3244032 | tf_op jit(solution)/shard_map/all_to_all | solution.py:590
  32.3 39.3 %all-to-all-start.1 = ((bf16[4,384,1024]{2,1,0:T(8,128)(2,1)}), bf16[4,384,1024]{2,1,0:T(8,128)(2,1)S(1)}, u32[]{:S(2)}, u32[]{:S(2)}) async-start(bf16[4,384,1024]{2,1,0:T(8,128)(2,1)} %pad_maximum_fusion), calls=%async_computation.1 | async-start | bytes 6291456 | tf_op jit(solution)/shard_map/all_to_all | solution.py:590
  41.7 44.7 %collective-permute-start = (bf16[4,512,384]{2,1,0:T(8,128)(2,1)}, bf16[4,512,384]{2,1,0:T(8,128)(2,1)}, u32[]{:S(2)}, u32[]{:S(2)}) collective-permute-start(bf16[4,512,384]{2,1,0:T(8,128)(2,1)} %slice.302.x_ref), channel_id=1, source_target_pairs={{0,4},{4,0},{1,5},{5,1},{2,6},{6,2},{3,7},{7,3},{8,12},{12,8},{9,1... | collective-permute-start | bytes 4718600 | tf_op jit(solution)/shard_map/ppermute | solution.py:582
  73.3 39.9 %all-to-all-start.2 = ((bf16[4,384,768]{2,1,0:T(8,128)(2,1)}), bf16[4,384,768]{2,1,0:T(8,128)(2,1)S(1)}, u32[]{:S(2)}, u32[]{:S(2)}) async-start(bf16[4,384,768]{2,1,0:T(8,128)(2,1)} %pad_maximum_fusion.1), calls=%async_computation.2 | async-start | bytes 4718592 | tf_op jit(solution)/shard_map/all_to_all | solution.py:590
  114.7 23.3 %all-to-all-start.3 = ((bf16[4,1536,128]{2,1,0:T(8,128)(2,1)}), bf16[4,1536,128]{2,1,0:T(8,128)(2,1)}, u32[]{:S(2)}, u32[]{:S(2)}) async-start(bf16[4,1536,128]{2,1,0:T(8,128)(2,1)} %broadcast_in_dim.160), calls=%async_computation.3 | async-start | bytes 3145728 | tf_op jit(solution)/shard_map/all_to_all | solution.py:590
  119.2 52.4 %collective-permute-start.2 = (bf16[4,384,768]{2,1,0:T(8,128)(2,1)S(1)}, bf16[4,384,768]{2,1,0:T(8,128)(2,1)}, u32[]{:S(2)}, u32[]{:S(2)}) collective-permute-start(bf16[4,384,768]{2,1,0:T(8,128)(2,1)S(1)} %all-to-all-done.2.wa_ref), channel_id=1, source_target_pairs={{0,8},{8,0},{16,24},{24,16},{1,9},{9,1},{17,25},{25,17},{2,10},{10... | collective-permute-start | bytes 7077896 | tf_op jit(solution)/shard_map/ppermute | solution.py:582
  145.5 26.0 %all-to-all-start.4 = ((bf16[4,512,384]{2,1,0:T(8,128)(2,1)}), bf16[4,512,384]{2,1,0:T(8,128)(2,1)}, u32[]{:S(2)}, u32[]{:S(2)}) async-start(bf16[4,512,384]{2,1,0:T(8,128)(2,1)} %broadcast_in_dim.162), calls=%async_computation.4 | async-start | bytes 3145728 | tf_op jit(solution)/shard_map/all_to_all | solution.py:590
  172.8 21.6 %all-to-all-start.5 = ((bf16[4,512,384]{2,1,0:T(8,128)(2,1)}), bf16[4,512,384]{2,1,0:T(8,128)(2,1)S(1)}, u32[]{:S(2)}, u32[]{:S(2)}) async-start(bf16[4,512,384]{2,1,0:T(8,128)(2,1)} %broadcast_in_dim.163), calls=%async_computation.5 | async-start | bytes 3145728 | tf_op jit(solution)/shard_map/all_to_all | solution.py:590
  176.9 17.5 %collective-permute-start.3 = (bf16[4,512,384]{2,1,0:T(8,128)(2,1)}, bf16[4,512,384]{2,1,0:T(8,128)(2,1)S(1)}, u32[]{:S(2)}, u32[]{:S(2)}) collective-permute-start(bf16[4,512,384]{2,1,0:T(8,128)(2,1)} %all-to-all-done.4.h_ref), channel_id=1, source_target_pairs={{0,4},{4,0},{1,5},{5,1},{2,6},{6,2},{3,7},{7,3},{8,12},{12,8},{9,1... | collective-permute-start | bytes 4718600 | tf_op jit(solution)/shard_map/ppermute | solution.py:582
  211.1 13.1 %collective-permute-start.5 = (bf16[4,512,384]{2,1,0:T(8,128)(2,1)S(1)}, bf16[4,512,384]{2,1,0:T(8,128)(2,1)S(1)}, u32[]{:S(2)}, u32[]{:S(2)}) collective-permute-start(bf16[4,512,384]{2,1,0:T(8,128)(2,1)S(1)} %get-tuple-element.91), channel_id=1, source_target_pairs={{0,4},{4,0},{1,5},{5,1},{2,6},{6,2},{3,7},{7,3},{8,12},{12,8},{9,1... | collective-permute-start | bytes 4718600 | tf_op jit(solution)/shard_map/ppermute | solution.py:582
  227.7 31.2 %all-to-all-start.6 = ((bf16[4,512,384]{2,1,0:T(8,128)(2,1)}), bf16[4,512,384]{2,1,0:T(8,128)(2,1)}, u32[]{:S(2)}, u32[]{:S(2)}) async-start(bf16[4,512,384]{2,1,0:T(8,128)(2,1)} %add_convert_fusion.2), calls=%async_computation.6 | async-start | bytes 3145728 | tf_op jit(solution)/shard_map/all_to_all | solution.py:590
  233.5 25.4 %collective-permute-start.9 = (f32[4,128]{1,0:T(4,128)S(1)}, f32[4,128]{1,0:T(4,128)S(1)}, u32[]{:S(2)}, u32[]{:S(2)}) collective-permute-start(f32[4,128]{1,0:T(4,128)S(1)} %bitcast.182), channel_id=1, source_target_pairs={{0,3},{1,2},{2,1},{3,0},{4,7},{5,6},{6,5},{7,4},{8,11},{9,10},{10,... | collective-permute-start | bytes 6152 | tf_op jit(solution)/shard_map/ppermute | solution.py:582
  236.4 22.5 %collective-permute-start.8 = (f32[4,128]{1,0:T(4,128)S(1)}, f32[4,128]{1,0:T(4,128)S(1)}, u32[]{:S(2)}, u32[]{:S(2)}) collective-permute-start(f32[4,128]{1,0:T(4,128)S(1)} %bitcast.183), channel_id=1, source_target_pairs={{0,2},{1,3},{2,0},{3,1},{4,6},{5,7},{6,4},{7,5},{8,10},{9,11},{10,... | collective-permute-start | bytes 6152 | tf_op jit(solution)/shard_map/ppermute | solution.py:582
  236.9 22.0 %collective-permute-start.7 = (f32[4,128]{1,0:T(4,128)S(1)}, f32[4,128]{1,0:T(4,128)S(1)}, u32[]{:S(2)}, u32[]{:S(2)}) collective-permute-start(f32[4,128]{1,0:T(4,128)S(1)} %bitcast.184), channel_id=1, source_target_pairs={{0,1},{1,0},{2,3},{3,2},{4,5},{5,4},{6,7},{7,6},{8,9},{9,8},{10,11... | collective-permute-start | bytes 6152 | tf_op jit(solution)/shard_map/ppermute | solution.py:582
  262.7 29.2 %collective-permute-start.11 = (bf16[2,384,768]{2,1,0:T(8,128)(2,1)}, bf16[2,384,768]{2,1,0:T(8,128)(2,1)}, u32[]{:S(2)}, u32[]{:S(2)}) collective-permute-start(bf16[2,384,768]{2,1,0:T(8,128)(2,1)} %shard_map.175), channel_id=1, source_target_pairs={{0,8},{8,0},{16,24},{24,16},{1,9},{9,1},{17,25},{25,17},{2,10},{10... | collective-permute-start | bytes 3538952 | tf_op jit(solution)/shard_map/ppermute | solution.py:582
  267.7 30.9 %all-to-all-start.7 = ((bf16[4,1536,128]{2,1,0:T(8,128)(2,1)}), bf16[4,1536,128]{2,1,0:T(8,128)(2,1)}, u32[]{:S(2)}, u32[]{:S(2)}) async-start(bf16[4,1536,128]{2,1,0:T(8,128)(2,1)} %copy-done.17), calls=%async_computation.7 | async-start | bytes 3145728 | tf_op jit(solution)/shard_map/all_to_all | solution.py:590
  274.2 73.8 %collective-permute-start.14 = (bf16[2,384,768]{2,1,0:T(8,128)(2,1)}, bf16[2,384,768]{2,1,0:T(8,128)(2,1)}, u32[]{:S(2)}, u32[]{:S(2)}) collective-permute-start(bf16[2,384,768]{2,1,0:T(8,128)(2,1)} %copy-done.39), channel_id=1, source_target_pairs={{0,8},{8,0},{16,24},{24,16},{1,9},{9,1},{17,25},{25,17},{2,10},{10... | collective-permute-start | bytes 3538952 | tf_op jit(solution)/shard_map/ppermute | solution.py:582
  314.2 36.9 %collective-permute-start.15 = (bf16[2,384,512]{2,1,0:T(8,128)(2,1)S(1)}, bf16[2,384,512]{2,1,0:T(8,128)(2,1)S(1)}, u32[]{:S(2)}, u32[]{:S(2)}) collective-permute-start(bf16[2,384,512]{2,1,0:T(8,128)(2,1)S(1)} %shard_map.182), channel_id=1, source_target_pairs={{0,8},{8,0},{16,24},{24,16},{1,9},{9,1},{17,25},{25,17},{2,10},{10... | collective-permute-start | bytes 2359304 | tf_op jit(solution)/shard_map/ppermute | solution.py:582
  315.9 29.3 %collective-permute-start.13 = (bf16[1,384,768]{2,1,0:T(8,128)(2,1)S(1)}, bf16[1,384,768]{2,1,0:T(8,128)(2,1)S(1)}, u32[]{:S(2)}, u32[]{:S(2)}) collective-permute-start(bf16[1,384,768]{2,1,0:T(8,128)(2,1)S(1)} %slice.419), channel_id=1, source_target_pairs={{0,16},{8,24},{16,0},{24,8},{1,17},{9,25},{17,1},{25,9},{2,18},{10... | collective-permute-start | bytes 1769480 | tf_op jit(solution)/shard_map/ppermute | solution.py:582
  357.2 56.8 %collective-permute-start.18 = (bf16[4,512,384]{2,1,0:T(8,128)(2,1)}, bf16[4,512,384]{2,1,0:T(8,128)(2,1)}, u32[]{:S(2)}, u32[]{:S(2)}) collective-permute-start(bf16[4,512,384]{2,1,0:T(8,128)(2,1)} %shard_map.187), channel_id=1, source_target_pairs={{0,4},{4,0},{1,5},{5,1},{2,6},{6,2},{3,7},{7,3},{8,12},{12,8},{9,1... | collective-permute-start | bytes 4718600 | tf_op jit(solution)/shard_map/ppermute | solution.py:582
  363.7 43.0 %collective-permute-start.17 = (bf16[2,384,640]{2,1,0:T(8,128)(2,1)S(1)}, bf16[2,384,640]{2,1,0:T(8,128)(2,1)S(1)}, u32[]{:S(2)}, u32[]{:S(2)}) collective-permute-start(bf16[2,384,640]{2,1,0:T(8,128)(2,1)S(1)} %copy-done.41), channel_id=1, source_target_pairs={{0,8},{8,0},{16,24},{24,16},{1,9},{9,1},{17,25},{25,17},{2,10},{10... | collective-permute-start | bytes 2949128 | tf_op jit(solution)/shard_map/ppermute | solution.py:582
  368.4 59.5 %collective-permute-start.12 = (bf16[4,512,384]{2,1,0:T(8,128)(2,1)}, bf16[4,512,384]{2,1,0:T(8,128)(2,1)}, u32[]{:S(2)}, u32[]{:S(2)}) collective-permute-start(bf16[4,512,384]{2,1,0:T(8,128)(2,1)} %get-tuple-element.119), channel_id=1, source_target_pairs={{0,4},{4,0},{1,5},{5,1},{2,6},{6,2},{3,7},{7,3},{8,12},{12,8},{9,1... | collective-permute-start | bytes 4718600 | tf_op jit(solution)/shard_map/ppermute | solution.py:582
  370.0 32.1 %collective-permute-start.16 = (bf16[1,384,768]{2,1,0:T(8,128)(2,1)S(1)}, bf16[1,384,768]{2,1,0:T(8,128)(2,1)S(1)}, u32[]{:S(2)}, u32[]{:S(2)}) collective-permute-start(bf16[1,384,768]{2,1,0:T(8,128)(2,1)S(1)} %slice.418), channel_id=1, source_target_pairs={{0,16},{8,24},{16,0},{24,8},{1,17},{9,25},{17,1},{25,9},{2,18},{10... | collective-permute-start | bytes 1769480 | tf_op jit(solution)/shard_map/ppermute | solution.py:582
  372.8 45.6 %collective-permute-start.19 = (bf16[1,384,512]{2,1,0:T(8,128)(2,1)S(1)}, bf16[1,384,512]{2,1,0:T(8,128)(2,1)}, u32[]{:S(2)}, u32[]{:S(2)}) collective-permute-start(bf16[1,384,512]{2,1,0:T(8,128)(2,1)S(1)} %slice.421), channel_id=1, source_target_pairs={{0,16},{8,24},{16,0},{24,8},{1,17},{9,25},{17,1},{25,9},{2,18},{10... | collective-permute-start | bytes 1179656 | tf_op jit(solution)/shard_map/ppermute | solution.py:582
  402.1 28.8 %collective-permute-start.25 = (f32[4,128]{1,0:T(4,128)}, f32[4,128]{1,0:T(4,128)}, u32[]{:S(2)}, u32[]{:S(2)}) collective-permute-start(f32[4,128]{1,0:T(4,128)} %bitcast.34), channel_id=1, source_target_pairs={{0,3},{1,2},{2,1},{3,0},{4,7},{5,6},{6,5},{7,4},{8,11},{9,10},{10,... | collective-permute-start | bytes 6152 | tf_op jit(solution)/shard_map/ppermute | solution.py:582
  406.7 24.2 %collective-permute-start.24 = (f32[4,128]{1,0:T(4,128)}, f32[4,128]{1,0:T(4,128)}, u32[]{:S(2)}, u32[]{:S(2)}) collective-permute-start(f32[4,128]{1,0:T(4,128)} %bitcast.34), channel_id=1, source_target_pairs={{0,2},{1,3},{2,0},{3,1},{4,6},{5,7},{6,4},{7,5},{8,10},{9,11},{10,... | collective-permute-start | bytes 6152 | tf_op jit(solution)/shard_map/ppermute | solution.py:582
  414.0 16.9 %collective-permute-start.23 = (f32[4,128]{1,0:T(4,128)}, f32[4,128]{1,0:T(4,128)S(1)}, u32[]{:S(2)}, u32[]{:S(2)}) collective-permute-start(f32[4,128]{1,0:T(4,128)} %bitcast.34), channel_id=1, source_target_pairs={{0,1},{1,0},{2,3},{3,2},{4,5},{5,4},{6,7},{7,6},{8,9},{9,8},{10,11... | collective-permute-start | bytes 6152 | tf_op jit(solution)/shard_map/ppermute | solution.py:582
  418.4 23.8 %all-to-all-start.8 = ((bf16[4,512,384]{2,1,0:T(8,128)(2,1)}), bf16[4,512,384]{2,1,0:T(8,128)(2,1)}, u32[]{:S(2)}, u32[]{:S(2)}) async-start(bf16[4,512,384]{2,1,0:T(8,128)(2,1)} %add_convert_fusion), calls=%async_computation.8 | async-start | bytes 3145728 | tf_op jit(solution)/shard_map/all_to_all | solution.py:590
  424.8 24.0 %collective-permute-start.20 = (bf16[1,384,640]{2,1,0:T(8,128)(2,1)S(1)}, bf16[1,384,640]{2,1,0:T(8,128)(2,1)}, u32[]{:S(2)}, u32[]{:S(2)}) collective-permute-start(bf16[1,384,640]{2,1,0:T(8,128)(2,1)S(1)} %slice.420), channel_id=1, source_target_pairs={{0,16},{8,24},{16,0},{24,8},{1,17},{9,25},{17,1},{25,9},{2,18},{10... | collective-permute-start | bytes 1474568 | tf_op jit(solution)/shard_map/ppermute | solution.py:582
  453.7 28.8 %all-to-all-start.9 = ((bf16[4,512,384]{2,1,0:T(8,128)(2,1)}), bf16[4,512,384]{2,1,0:T(8,128)(2,1)S(1)}, u32[]{:S(2)}, u32[]{:S(2)}) async-start(bf16[4,512,384]{2,1,0:T(8,128)(2,1)} %add_convert_fusion.1), calls=%async_computation.9 | async-start | bytes 3145728 | tf_op jit(solution)/shard_map/all_to_all | solution.py:590
  474.5 12.8 %collective-permute-start.33 = (f32[96,2]{0,1:T(2,128)S(1)}, f32[96,2]{0,1:T(2,128)S(1)}, u32[]{:S(2)}, u32[]{:S(2)}) collective-permute-start(f32[96,2]{0,1:T(2,128)S(1)} %fusion.30), channel_id=1, source_target_pairs={{0,0},{1,8},{2,16},{3,24},{8,1},{9,9},{10,17},{11,25},{16,2},{17,1... | collective-permute-start | bytes 2312 | tf_op jit(solution)/shard_map/ppermute | solution.py:913
  483.6 39.6 %all-to-all-start.10 = ((bf16[4,96,2688]{2,1,0:T(8,128)(2,1)}), bf16[4,96,2688]{2,1,0:T(8,128)(2,1)S(1)}, u32[]{:S(2)}, u32[]{:S(2)}) async-start(bf16[4,96,2688]{2,1,0:T(8,128)(2,1)} %bitcast.36), calls=%async_computation.10 | async-start | bytes 4128768 | tf_op jit(solution)/shard_map/all_to_all | solution.py:590
  (112 other events, 739.7 us)

commit v3 on v2

--- a/solution.py
+++ b/solution.py
@@ -434,17 +434,26 @@
     )(flag, a, b, lines, w, misc)
 
 
-def weight_call(kernel, idx, picked, rest, cols, flops, flags=0):
+def picked_block(half, part):
+    return pl.BlockSpec((1, half, part), lambda g, *p: (p[0][g], 0, 0))
+
+
+def weight_kernel(terms, *refs):
+    out_ref = refs[-1]
+    for at, total in terms(*refs[:-1]):
+        out_ref[0, :, at : at + total.shape[1]] = total.astype(bf16)
+
+
+def weight_call(terms, idx, picked, rest, cols, flops, flags=0):
     count = idx.shape[0] - flags
     n, half, part = picked[0].shape
-    pick = pl.BlockSpec((1, half, part), lambda g, *p: (p[0][g], 0, 0))
-    return pl.pallas_call(
-        kernel,
+    return pl.pallas_call(
+        functools.partial(weight_kernel, terms),
         out_shape=shape(count, part, cols),
         grid_spec=pltpu.PrefetchScalarGridSpec(
             num_scalar_prefetch=1,
             grid=(count,),
-            in_specs=[pick] * len(picked) + [whole(*x.shape) for x in rest],
+            in_specs=[picked_block(half, part)] * len(picked) + [whole(*x.shape) for x in rest],
             out_specs=lead_block(part, cols),
         ),
         compiler_params=pltpu.CompilerParams(vmem_limit_bytes=VMEM_LIMIT),
@@ -452,25 +461,57 @@
     )(idx, *picked, *rest)
 
 
-def ffn_weight_kernel(c, idx_ref, n1, n2, g1, g2, d1, d2, m1, m2, out_ref):
-    cols = d1.shape[2]
-    total = dot_of(n1[0], d1[c], 0, 0) + dot_of(n2[0], d2[c], 0, 0)
-    out_ref[0, :, :cols] = total.astype(bf16)
-    total = dot_of(g1[0], m1[c], 0, 0) + dot_of(g2[0], m2[c], 0, 0)
-    out_ref[0, :, cols:] = total.astype(bf16)
-
-
-def own_weight_kernel(idx_ref, n1, n2, d, out_ref):
-    total = dot_of(n1[0], d[0], 0, 0) + dot_of(n2[0], d[1], 0, 0)
-    out_ref[0] = total.astype(bf16)
-
-
-def shared_weight_kernel(idx_ref, n1, n2, d, l1, l2, out_ref):
+def weight_add_kernel(terms, *refs):
+    got_ref, keep_ref, send_ref = refs[-3:]
+    step = pl.program_id(0)
+    for at, total in terms(*refs[:-3]):
+        cols = slice(at, at + total.shape[1])
+        total = total + got_ref[0, :, cols].astype(f32)
+
+        @pl.when(step == 0)
+        def _():
+            keep_ref[0, :, cols] = total
+
+        @pl.when(step != 0)
+        def _():
+            send_ref[0, :, cols] = total.astype(bf16)
+
+
+def weight_add(terms, idx, picked, rest, got, cols, flops):
+    n, half, part = picked[0].shape
+    return pl.pallas_call(
+        functools.partial(weight_add_kernel, terms),
+        out_shape=[shape(1, part, cols, dtype=f32), shape(1, part, cols)],
+        grid_spec=pltpu.PrefetchScalarGridSpec(
+            num_scalar_prefetch=1,
+            grid=(2,),
+            in_specs=[picked_block(half, part)] * len(picked)
+            + [whole(*x.shape) for x in rest]
+            + [lead_block(part, cols)],
+            out_specs=[whole(1, part, cols)] * 2,
+        ),
+        compiler_params=pltpu.CompilerParams(vmem_limit_bytes=VMEM_LIMIT),
+        cost_estimate=cost(flops * 2, 6000000),
+    )(idx, *picked, *rest, got)
+
+
+def gate_up_terms(c, idx_ref, n1, n2, d1, d2):
+    yield 0, dot_of(n1[0], d1[c], 0, 0) + dot_of(n2[0], d2[c], 0, 0)
+
+
+def down_terms(idx_ref, g1, g2, m1, m2):
+    for c in range(2):
+        yield c * m1.shape[2], dot_of(g1[0], m1[c], 0, 0) + dot_of(g2[0], m2[c], 0, 0)
+
+
+def own_terms(idx_ref, n1, n2, d):
+    yield 0, dot_of(n1[0], d[0], 0, 0) + dot_of(n2[0], d[1], 0, 0)
+
+
+def shared_terms(idx_ref, n1, n2, d, l1, l2):
     left = jnp.where(idx_ref[idx_ref.shape[0] - 1] == 0, n1[0], n2[0])
-    cols = d.shape[1]
-    out_ref[0, :, :cols] = dot_of(left, d[...], 0, 0).astype(bf16)
-    lines = dot_of(n1[0], l1[...], 0, 1) + dot_of(n2[0], l2[...], 0, 1)
-    out_ref[0, :, cols:] = lines.astype(bf16)
+    yield 0, dot_of(left, d[...], 0, 0)
+    yield d.shape[1], dot_of(n1[0], l1[...], 0, 1) + dot_of(n2[0], l2[...], 0, 1)
 
 
 def own_head(k):
@@ -648,8 +689,6 @@
         b = w_project[:, :, head_cols(shared_head(w // 2))].reshape(part, 4 * HD)
         return jnp.concatenate([a, b], axis=1)
 
-    proj_w = exchange(jnp.stack([heads_for(w) for w in ws]), "wid")
-
     side = dp & 1
     ffh = ff // 2
 
@@ -658,7 +697,8 @@
         cut = lax.dynamic_slice_in_dim(w_gate_up, at, ffh, axis=2).reshape(part, 2 * ffh)
         return jnp.concatenate([cut, lax.dynamic_slice_in_dim(w_down, at, ffh, axis=1)], axis=1)
 
-    ffn_own = exchange(after(jnp.stack([ffn_for(w) for w in ws]), proj_w), "wid")
+    ffn_own = exchange(after(jnp.stack([ffn_for(w) for w in ws]), gathered), "wid")
+    proj_w = exchange(after(jnp.stack([heads_for(w) for w in ws]), ffn_own), "wid")
     ffn_other = swap(ffn_own, "dp", dp_size, 1)
     side = side.astype(jnp.int32)[None]
 
@@ -689,8 +729,11 @@
         ],
         axis=0,
     )
-    attended, inv, carry, prob = attention_forward(lens, pairs, logit_pairs)
-    o_all = to_all(after(attended, ffn_own).reshape(-1, HD), "wid", wid_size)
+    gs_own = exchange(
+        after(jnp.broadcast_to(g_own[None], (wid_size,) + g_own.shape), proj_w), "wid"
+    )
+    attended, inv, carry, prob = attention_forward(lens, after(pairs, ffn_other), logit_pairs)
+    o_all = to_all(after(attended, gs_own).reshape(-1, HD), "wid", wid_size)
     place = hid.astype(jnp.int32)[None]
     attn_own, attn_far = attention_out(place, w_out, o_all, half)
     hidden = x_own.astype(f32) + attn_own + hid_swap(attn_far)
@@ -699,9 +742,6 @@
     gain_two = gain_ffn[None].astype(f32)
     hs_own = to_all(hidden.astype(bf16), "wid", wid_size)
     hs_far = hid_swap(hs_own)
-    gs_own = exchange(
-        after(jnp.broadcast_to(g_own[None], (wid_size,) + g_own.shape), hs_own, ffn_other), "wid"
-    )
     gs_far = hid_swap(gs_own)
     n2_own, m_own, d_own, dn_own, s_own, r2_own = feed_forward(
         lens_own, side, hs_own, gs_own, ffn_own, ffn_other, misc, f32
@@ -729,12 +769,28 @@
     direct = dp_size == wid_size
     sub = chunk // wid_size
 
-    def dp_pieces(make, odd_first):
-        ts = range(1 if odd_first else 0, dp_size, 2)
+    def dp_pieces(terms, picked, rest, cols, flags, ts):
         if direct:
-            return make(jnp.stack([dp ^ t for t in ts]).astype(jnp.int32))
-        full = make(jnp.arange(wid_size, dtype=jnp.int32)).reshape(width, -1)
+            idx = jnp.stack([dp ^ t for t in ts]).astype(jnp.int32)
+            idx = jnp.concatenate([idx, *flags])
+            return weight_call(terms, idx, picked, rest, cols, 2 * half * part * cols, len(flags))
+        idx = jnp.concatenate([jnp.arange(wid_size, dtype=jnp.int32), *flags])
+        full = weight_call(terms, idx, picked, rest, cols, 2 * half * part * cols, len(flags))
+        full = full.reshape(width, -1)
         return jnp.stack([shift_rows(full, (dp ^ t) * chunk, chunk) for t in ts])
+
+    def dp_odd(terms, picked, rest, cols, flags=()):
+        return dp_pieces(terms, picked, rest, cols, flags, range(1, dp_size, 2))
+
+    def dp_even(terms, picked, rest, cols, got, flags=()):
+        if direct and dp_size == 4:
+            idx = jnp.stack([dp, dp ^ 2]).astype(jnp.int32)
+            idx = jnp.concatenate([idx, *flags])
+            flops = 2 * half * part * cols
+            keep, send = weight_add(terms, idx, picked, rest, got, cols, flops)
+            return keep, swap(send, "dp", dp_size, 2)
+        here = dp_pieces(terms, picked, rest, cols, flags, range(0, dp_size, 2))
+        return dp_send(here.astype(f32) + got.astype(f32))
 
     def dp_send(held, k=2):
         return held[0::2], swap(held[1::2].astype(bf16), "dp", dp_size, k)
@@ -755,69 +811,47 @@
     def to_rows(x):
         return exchange(x.astype(bf16).reshape(wid_size, sub, -1), "wid")
 
-    d_then = after(d_own, dn_here)
-
-    def ffn_weights(c, then):
-        def make(idx):
-            return weight_call(
-                functools.partial(ffn_weight_kernel, c),
-                idx,
-                (n2_own, n2_far, gs_own, gs_far),
-                (then, d_far, m_own, m_far),
-                3 * ffh,
-                12 * half * part * ffh,
-            )
-
-        return make
-
-    odd_one = dp_pieces(ffn_weights(0, d_then), True)
-    got_one = swap(odd_one, "dp", dp_size, 1)
-    d_then = after(d_then, odd_one)
-    odd_two = dp_pieces(ffn_weights(1, d_then), True)
-    got_two = swap(odd_two, "dp", dp_size, 1)
-    d_then = after(d_then, odd_two)
-    even_one = dp_pieces(ffn_weights(0, d_then), False)
-    even_two = dp_pieces(ffn_weights(1, d_then), False)
+    gate_up = [functools.partial(gate_up_terms, c) for c in range(2)]
+    n2_both, gs_both = (n2_own, n2_far), (gs_own, gs_far)
+    odd = [dp_odd(gate_up[0], n2_both, (after(d_own, dn_here), d_far), ff)]
+    odd.append(dp_odd(gate_up[1], n2_both, (after(d_own, odd[0]), d_far), ff))
+    odd.append(dp_odd(down_terms, gs_both, (after(m_own, odd[1]), m_far), ff))
+    got_odd = [swap(x, "dp", dp_size, 1) for x in odd]
 
     grad_half = g_own.astype(f32) * valid_half
     grad_hidden = grad_half + r2_own * (
         grad_normed_two * gain_two - r2_own * hidden * mean_two
     )
     gain_two_part = jnp.sum(grad_normed_two * hidden * r2_own, axis=0)
-    da_own = after(grad_hidden.astype(bf16), even_one, even_two)
+    da_own = after(grad_hidden.astype(bf16), odd[2])
     da_far = hid_swap(da_own)
-    do_here = attention_out_back(place, w_out, da_own, da_far, wid_size)
+    keep_0, next_0 = dp_even(gate_up[0], n2_both, (after(d_own, odd[2]), d_far), ff, got_odd[0])
+    do_here = attention_out_back(place, w_out, after(da_own, keep_0), da_far, wid_size)
     do_pieces = exchange(do_here, "wid")
     ffn_own_out, ffn_far_out = feed_forward_out(
-        side, after(m_own, do_here, got_one), m_far, ffn_own, ffn_other
-    )
-    g_out = out_gradient(place, after(da_own, do_here, got_one), da_far, o_all, w_out.shape[1])
+        side, after(m_own, do_here), m_far, ffn_own, ffn_other
+    )
+    g_out = out_gradient(place, after(da_own, ffn_far_out), da_far, o_all, w_out.shape[1])
     do_got = do_pieces.reshape(wid_size, -1, SEQ, HD)
-    got_one = after(got_one, do_got)
-    held_one = even_one.astype(f32) + got_one.astype(f32)
-    keep_one, next_one = dp_send(held_one)
 
     pairs_a, lines_a, sums_a = attention_backward(
-        lens, pairs, logit_pairs, inv, carry, prob, after(do_got, held_one, ffn_far_out), 0, 2 * per_half
+        lens, pairs, logit_pairs, inv, carry, prob, after(do_got, ffn_far_out, g_out), 0, 2 * per_half
     )
 
     head_iota = lax.broadcasted_iota(jnp.int32, (1, 16, 1), 1)
+    m_then = after(m_own, pairs_a)
+    keep_2, next_2 = dp_even(down_terms, gs_both, (m_then, m_far), ff, got_odd[2])
     right_own = pairs_a.reshape(2, half, 4 * HD)
-
-    def own_weights(idx):
-        return weight_call(
-            own_weight_kernel,
-            idx,
-            (n1_own, n1_far),
-            (right_own,),
-            4 * HD,
-            4 * half * part * 4 * HD,
-        )
-
-    own_odd = dp_pieces(own_weights, True)
+    ffn_here = after(partial(ffn_own_out, after(ffn_far_out, do_got)), pairs_a)
+    ffn_back = exchange(ffn_here, "wid")
+
+    n1_both = (n1_own, n1_far)
+    own_odd = dp_odd(own_terms, n1_both, (right_own,), 4 * HD)
     own_got = swap(own_odd, "dp", dp_size, 1)
+    d_then = after(d_own, own_odd)
+    keep_1, next_1 = dp_even(gate_up[1], n2_both, (d_then, d_far), ff, got_odd[1])
     pairs_b, lines_b, sums_b = attention_backward(
-        lens, pairs, logit_pairs, inv, carry, prob, after(do_got, own_odd), 2 * per_half, per_half
+        lens, pairs, logit_pairs, inv, carry, prob, after(do_got, own_odd, keep_1, next_0), 2 * per_half, per_half
     )
 
     def spread(a, b, at):
@@ -836,41 +870,38 @@
 
     lines_own, lines_far = lines_at(0), lines_at(1)
     flat_own, flat_far = flat_lines(lines_own), flat_lines(lines_far)
-    right_shared = after(pairs_b, next_one).reshape(half, 4 * HD)
-
-    def shared_weights(idx):
-        return weight_call(
-            shared_weight_kernel,
-            jnp.concatenate([idx, half_b.astype(jnp.int32)[None]]),
-            (n1_own, n1_far),
-            (right_shared, flat_own, flat_far),
-            5 * HD,
-            2 * half * part * 5 * HD,
-            1,
-        )
-
-    shared_odd = dp_pieces(shared_weights, True)
+    right_shared = after(pairs_b, keep_2, next_1).reshape(half, 4 * HD)
+
+    flat_both = (flat_own, flat_far)
+    half_flag = (half_b.astype(jnp.int32)[None],)
+    shared_odd = dp_odd(shared_terms, n1_both, (right_shared, *flat_both), 5 * HD, half_flag)
     shared_got = swap(shared_odd, "dp", dp_size, 1)
-    right_own = after(right_own, own_got)
-    right_shared = after(right_shared, own_got)
+    fine = part // dp_size
+    to_place = [
+        (c * wid_size + w, w * dp_size + c) for c in range(dp_size) for w in range(wid_size)
+    ]
+
+    def dp_fine(x, *late):
+        return dp_sum([shift_rows(x, (dp ^ t) * fine, fine) for t in range(dp_size)], *late)
+
+    out_pieces = [shift_rows(g_out, (dp ^ t) * fine, fine) for t in range(dp_size)]
+    out_got = swap(jnp.stack(out_pieces[1::2]), "dp", dp_size, 1)
     flags = [(half_b == p).astype(jnp.int32)[None] for p in range(2)]
-    got_two = after(got_two, shared_odd)
-    held_two = even_two.astype(f32) + got_two.astype(f32)
-    keep_two, next_two = dp_send(held_two)
-    back_b = after(pairs_b, shared_odd, held_two, own_got)
+    back_b = after(pairs_b, shared_odd, own_got, ffn_back)
     dn1_far = project_back(flags[1], pairs_a, per_half, back_b, lines_far, proj_w, misc, bf16)
-    own_even = dp_pieces(own_weights, False)
-    keep_own, next_own = dp_send(own_even.astype(f32) + own_got.astype(f32))
-    shared_even = dp_pieces(shared_weights, False)
-    keep_shared, next_shared = dp_send(shared_even.astype(f32) + shared_got.astype(f32))
-    back_b = after(back_b, next_two, keep_own, shared_got)
+    right_own = after(right_own, dn1_far, own_got)
+    keep_own, next_own = dp_even(own_terms, n1_both, (right_own,), 4 * HD, own_got)
+    back_b = after(back_b, keep_own)
     dn1_own = project_back(flags[0], pairs_a, 0, back_b, lines_own, proj_w, misc, f32)
-    dn1_here = after(partial(dn1_own, dn1_far), next_own, keep_shared)
+    dn1_here = partial(dn1_own, dn1_far)
     dn1_got = exchange(dn1_here, "wid")
-    ffn_far_out = after(ffn_far_out, pairs_b)
-    ffn_here = after(partial(ffn_own_out, ffn_far_out), dn1_got)
-    ffn_back = exchange(ffn_here, "wid")
-    next_shared = after(next_shared, dn1_got)
+    right_shared = after(right_shared, dn1_here, shared_got)
+    right_shared = after(right_shared, next_own)
+    keep_shared, next_shared = dp_even(
+        shared_terms, n1_both, (right_shared, *flat_both), 5 * HD, shared_got, half_flag
+    )
+    next_own, next_shared = lax.optimization_barrier((next_own, next_shared, dn1_got))[:2]
+    next_2 = after(next_2, dn1_got)
     sums = [sum(spread(sums_a, sums_b, p)) for p in range(2)]
     mean_one = line_sum(*sums, dn1_got)
     grad_normed_one = jnp.sum(dn1_got.astype(f32), axis=0)
@@ -889,39 +920,32 @@
             [jnp.where(hid == 0, x, other), jnp.where(hid == 0, other, x)], axis=0
         )
 
-    parts = [
-        dp_take(keep_one, next_one),
-        dp_take(keep_two, next_two),
-        dp_take(keep_own, next_own),
-        dp_take(keep_shared, next_shared),
-    ]
-    g_all = jnp.concatenate(parts, axis=1).astype(bf16)
-    input_grad = whole_rows(after(input_half.astype(bf16), g_all))
-    output = whole_rows(after(((hidden + ffn) * valid_half).astype(bf16), g_all))
-
-    fine = part // dp_size
-    to_place = [
-        (c * wid_size + w, w * dp_size + c) for c in range(dp_size) for w in range(wid_size)
-    ]
-
-    def dp_fine(x, *late):
-        return dp_sum([shift_rows(x, (dp ^ t) * fine, fine) for t in range(dp_size)], *late)
-
-    out_out = lax.ppermute(dp_fine(g_out, g_all), ("dp", "wid"), to_place)
-    gain_part = after(jnp.stack([gain_one_part, gain_two_part], axis=1), g_all)
+    ffn_sums = [dp_take(keep_0, next_0), dp_take(keep_1, next_1), dp_take(keep_2, next_2)]
+    ffn_sums = after(jnp.concatenate(ffn_sums, axis=1).astype(bf16), dn1_got)
+    ffn_rows = to_rows(ffn_sums)
+    input_grad = whole_rows(after(input_half.astype(bf16), ffn_sums))
+    output = whole_rows(after(((hidden + ffn) * valid_half).astype(bf16), ffn_sums))
+
+    proj_sums = [dp_take(keep_own, next_own), dp_take(keep_shared, next_shared)]
+    proj_sums = jnp.concatenate(proj_sums, axis=1).astype(bf16)
+    out_even = jnp.stack(out_pieces[0::2]).astype(f32)
+    out_got = after(out_got, dn1_got)
+    out_sum = dp_take(*dp_send(out_even + out_got.astype(f32))).astype(bf16)
+    out_sum = after(out_sum, proj_sums, ffn_rows)
+    out_out = lax.ppermute(out_sum, ("dp", "wid"), to_place).astype(f32)
+    gain_part = after(jnp.stack([gain_one_part, gain_two_part], axis=1), proj_sums, ffn_rows)
     gain_part = gain_part + hid_swap(gain_part)
     gain_sum = lax.ppermute(dp_fine(gain_part), ("dp", "wid"), to_place)
 
-    all_rows = to_rows(after(g_all, ffn_back))
-    got = all_rows[:, :, : 3 * ff].reshape(wid_size, sub, 2, 3 * ffh)
-    pieces = [got[w, :, c] for w in ws for c in range(2)]
-    gate, up, down = (
-        jnp.concatenate([p[:, k * ffh : (k + 1) * ffh] for p in pieces], axis=1) for k in range(3)
-    )
+    got = ffn_rows[:, :, : 2 * ff].reshape(wid_size, sub, 2, 2, ffh)
+    gate, up = (
+        jnp.concatenate([got[w, :, c, k] for w in ws for c in range(2)], axis=1) for k in range(2)
+    )
+    down = jnp.concatenate([ffn_rows[w, :, 2 * ff :] for w in ws], axis=1)
     out_gate_up = jnp.stack([gate, up], axis=1).astype(f32)
     out_down = down.astype(f32)
 
-    got = all_rows[:, :, 3 * ff :].astype(f32)
+    got = to_rows(after(proj_sums, ffn_rows)).astype(f32)
     a = [got[w, :, : 4 * HD] for w in ws]
     b = [got[w, :, 4 * HD : 8 * HD] for w in ws]
     proj_rows = [a[0], b[0] + b[1], a[1], a[2], b[2] + b[3], a[3]]

time: 542 us -> 522 us (0.963)
  waiting for transfers between devices: 224 us -> 183 us
  blocking collectives: 0 us -> 22.8 us
  other arithmetic: 49.8 us -> 39.8 us
    all_to_all x0 -> x1, blocking collectives: none -> 22.8 us  [exchange(): return lax.all_to_all(x, axis, split_axis=0, concat_axis=0, tiled=True)]
    ppermute x32 -> x34, waiting for transfers between devices: 108 us -> 85 us  [swap(): return lax.ppermute(x, axis, [(n, n ^ k) for n in range(size)])]
    all_to_all x11, waiting for transfers between devices: 117 us -> 98.4 us  [exchange(): return lax.all_to_all(x, axis, split_axis=0, concat_axis=0, tiled=True)]
    pallas_call x8 -> x10, Pallas kernels: 22.2 us -> 29.5 us  [the longest x5 18 us: weight_add(): pl.pallas_call(functools.partial(weight_add_kernel, terms), out_shape=[sh...]
    unnamed x232 -> x218, local copies, waits for them, and re-layouts: 36.7 us -> 43.1 us
    ppermute x32 -> x34, starting transfers between devices: 35 us -> 34.8 us  [swap(): return lax.ppermute(x, axis, [(n, n ^ k) for n in range(size)])]
  transfers between devices with their start and end apart: 45 -> 47, of which waited for: 20 -> 17; matrix products, arithmetic and copies ran while one was open for 10% -> 11% of each run, Pallas kernels for 18% -> 18%
where the time goes in v3:
time: 522 us; the launch traced here: 515 us
  waiting for transfers between devices  183 us (35%)
  Pallas kernels  114 us (22%)
  starting transfers between devices  84.7 us (16%)
  local copies, waits for them, and re-layouts  67.2 us (13%)
  other arithmetic  39.8 us (8%)
  blocking collectives  22.8 us (4%)
    all_to_all x11, waiting for transfers between devices, exchange(): return lax.all_to_all(x, axis, split_axis=0, concat_axis=0, tiled=True)  98.4 us
    ppermute x34, waiting for transfers between devices, swap(): return lax.ppermute(x, axis, [(n, n ^ k) for n in range(size)])  85 us
    all_to_all x11, starting transfers between devices, exchange(): return lax.all_to_all(x, axis, split_axis=0, concat_axis=0, tiled=True)  48.6 us
    unnamed x218, local copies, waits for them, and re-layouts  43.1 us
    ppermute x34, starting transfers between devices, swap(): return lax.ppermute(x, axis, [(n, n ^ k) for n in range(size)])  34.8 us
    all_to_all x1, blocking collectives, exchange(): return lax.all_to_all(x, axis, split_axis=0, concat_axis=0, tiled=True)  22.8 us
    pallas_call x2, Pallas kernels, feed_forward(): pl.pallas_call(functools.partial(ffn_kernel, n), out_shape=[shape(n, half...  22 us
    pallas_call x5, Pallas kernels, weight_add(): pl.pallas_call(functools.partial(weight_add_kernel, terms), out_shape=[sh...  18 us
  transfers between devices with their start and end apart: 47, of which 17 were waited for; matrix products, arithmetic and copies ran while one was open for 11% of the time, Pallas kernels for 18%

profile of v3, /device:TPU:0, one launch (start us, length us, event | category | flops | bytes accessed | tf_op | source)
XLA Modules:
  0.0 515.1 jit_solution(15328492809165047021)
XLA Ops:
  6.0 5.2 %all-to-all-start = ((bf16[4,528,384]{2,1,0:T(8,128)(2,1)}), bf16[4,528,384]{2,1,0:T(8,128)(2,1)S(1)}, u32[]{:S(2)}, u32[]{:S(2)}) async-start(bf16[4,528,384]{2,1,0:T(8,128)(2,1)} %broadcast_in_dim.157), calls=%async_computation | async-start | bytes 3244032 | tf_op jit(solution)/shard_map/all_to_all | solution.py:631
  17.1 13.9 %all-to-all-done = bf16[4,528,384]{2,1,0:T(8,128)(2,1)S(1)} async-done(((bf16[4,528,384]{2,1,0:T(8,128)(2,1)}), bf16[4,528,384]{2,1,0:T(8,128)(2,1)S(1)}, u32[]{:S(2)}, u32[]{:S(2)}) %all-to-all-start) | async-done | bytes 1622048 | tf_op jit(solution)/shard_map/all_to_all | solution.py:631
  40.9 22.1 %all-to-all-done.1.wa_ref = bf16[4,384,768]{2,1,0:T(8,128)(2,1)S(1)} async-done(((bf16[4,384,768]{2,1,0:T(8,128)(2,1)}), bf16[4,384,768]{2,1,0:T(8,128)(2,1)S(1)}, u32[]{:S(2)}, u32[]{:S(2)}) %all-to-all-start.1) | async-done | bytes 2359328 | tf_op jit(solution)/shard_map/all_to_all | solution.py:631
  63.0 4.6 all-to-all-start.2
  72.2 31.2 %all-to-all-done.2.w_ref = bf16[4,384,1024]{2,1,0:T(8,128)(2,1)} async-done(((bf16[4,384,1024]{2,1,0:T(8,128)(2,1)}), bf16[4,384,1024]{2,1,0:T(8,128)(2,1)}, u32[]{:S(2)}, u32[]{:S(2)}) %all-to-all-start.2) | async-done | bytes 3145760 | tf_op jit(solution)/shard_map/all_to_all | solution.py:631
  104.6 4.6 all-to-all-start.3
  111.0 5.4 %shard_map.169 = (bf16[2,256,512]{2,1,0:T(8,128)(2,1)S(1)}, bf16[2,256,512]{2,1,0:T(8,128)(2,1)S(1)}, f32[2,16,256]{2,1,0:T(8,128)S(1)}, f32[2,1,256]{2,1,0:T(1,128)S(1)}, bf16[4,512,384]{2,1,0:T(8,128)(2,1)S(1)}) custom-call(bf16[4,512,384]{2,1,0:T(8,128)(2,1)} %slice.206.x_ref, bf16[4,384,1024]{2,1,0:T(8,128)(2,1)} %all-to-all-done.2.w_ref, ...), custom_call_target="tpu_custom_call" | custom-call | flops 1610612 | bytes 8000 | tf_op jit(solution)/shard_map/pallas_call | solution.py:261
  117.7 5.7 %shard_map.170 = (bf16[2,256,512]{2,1,0:T(8,128)(2,1)S(1)}, bf16[2,256,512]{2,1,0:T(8,128)(2,1)S(1)}, f32[2,16,256]{2,1,0:T(8,128)S(1)}, f32[2,1,256]{2,1,0:T(1,128)}, bf16[4,512,384]{2,1,0:T(8,128)(2,1)S(1)}) custom-call(bf16[4,512,384]{2,1,0:T(8,128)(2,1)} %collective-permute-done.x_ref, bf16[4,384,1024]{2,1,0:T(8,128)(2,1)} %all-to-all-done.2.w_ref, ...), custom_call_target="tpu_custom_call" | custom-call | flops 1610612 | bytes 8000 | tf_op jit(solution)/shard_map/pallas_call | solution.py:261
  125.1 15.0 %shard_map.171 = (bf16[6,256,128]{2,1,0:T(8,128)(2,1)S(1)}, f32[6,256,256]{2,1,0:T(8,128)S(1)}, f32[6,256,256]{2,1,0:T(8,128)S(1)}, f32[6,256,256]{2,1,0:T(8,128)S(1)}) custom-call(s32[6]{0:T(128)S(1)} %pad_add_fusion.len_ref, bf16[6,256,512]{2,1,0:T(8,128)(2,1)} %pad_maximum_fusion.2.x_ref, f32[6,1,256]{2,1,0:T(1,128)S(1)} %pad_maximum_fusion.12.l_ref), custom_call_target="tpu_custom_call" | custom-call | flops 9600000 | bytes 6600 | tf_op jit(solution)/shard_map/pallas_call | solution.py:167
  143.9 22.8 %all_to_all.60.o_ref = bf16[4,1536,128]{2,1,0:T(8,128)(2,1)S(1)} all-to-all(bf16[4,1536,128]{2,1,0:T(8,128)(2,1)S(1)} %broadcast_in_dim.160), channel_id=1, replica_groups=mesh['dp'=4,'hid'=2,'wid'=4] {'wid'}, dimensions={0} | all-to-all | bytes 3145728 | tf_op jit(solution)/shard_map/all_to_all | solution.py:631
  177.0 19.6 %all-to-all-done.5.h_ref = bf16[4,512,384]{2,1,0:T(8,128)(2,1)S(1)} async-done(((bf16[4,512,384]{2,1,0:T(8,128)(2,1)}), bf16[4,512,384]{2,1,0:T(8,128)(2,1)S(1)}, u32[]{:S(2)}, u32[]{:S(2)}) %all-to-all-start.5) | async-done | bytes 1572896 | tf_op jit(solution)/shard_map/all_to_all | solution.py:631
  201.2 10.9 %shard_map.174 = (bf16[4,512,384]{2,1,0:T(8,128)(2,1)S(1)}, bf16[2,512,256]{2,1,0:T(8,128)(2,1)S(1)}, bf16[2,512,512]{2,1,0:T(8,128)(2,1)S(1)}, bf16[4,512,384]{...) custom-call(s32[2]{0:T(128)S(1)} %get-tuple-element.280.len_ref, s32[1]{0:T(128)} %bitcast.12.side_ref, ...), custom_call_target="tpu_custom_call" | custom-call | flops 4026531 | bytes 12000 | tf_op jit(solution)/shard_map/pallas_call | solution.py:347
  213.0 11.2 %shard_map.173 = (bf16[4,512,384]{2,1,0:T(8,128)(2,1)S(1)}, bf16[2,512,256]{2,1,0:T(8,128)(2,1)S(1)}, bf16[2,512,512]{2,1,0:T(8,128)(2,1)S(1)}, f32[4,512,384]{2...) custom-call(s32[2]{0:T(128)S(1)} %get-tuple-element.278.len_ref, s32[1]{0:T(128)} %bitcast.12.side_ref, ...), custom_call_target="tpu_custom_call" | custom-call | flops 4026531 | bytes 12000 | tf_op jit(solution)/shard_map/pallas_call | solution.py:347
  230.0 4.5 all-to-all-start.6
  274.9 4.6 all-to-all-start.7
  279.6 5.5 %shard_map.180 = (f32[4,512,384]{2,1,0:T(8,128)}, bf16[4,512,384]{2,1,0:T(8,128)(2,1)S(1)}) custom-call(s32[1]{0:T(128)} %bitcast.12.side_ref, bf16[2,512,256]{2,1,0:T(8,128)(2,1)S(1)} %copy-done.48, bf16[2,512,256]{2,1,0:T(8,128)(2,1)S(1)} %copy-done.44, bf16[4,384,768]{2,1,0:T(8,128)(2,1)S(1)} %copy-done.1, bf16[4,384,768]{2,1,0:T(8,128)(2,1)} %collective-permute-done.1.wb_ref), custom_call_target="tpu_custom_call" | custom-call | flops 1610612 | bytes 12000 | tf_op jit(solution)/shard_map/pallas_call | solution.py:390
  286.3 11.7 %all-to-all-done.7 = bf16[4,1536,128]{2,1,0:T(8,128)(2,1)} async-done(((bf16[4,1536,128]{2,1,0:T(8,128)(2,1)}), bf16[4,1536,128]{2,1,0:T(8,128)(2,1)}, u32[]{:S(2)}, u32[]{:S(2)}) %all-to-all-start.7) | async-done | bytes 1572896 | tf_op jit(solution)/shard_map/all_to_all | solution.py:631
  308.5 10.2 %shard_map.182 = (bf16[4,256,512]{2,1,0:T(8,128)(2,1)S(1)}, f32[4,1,256]{2,1,0:T(1,128)S(1)}, f32[4,1,256]{2,1,0:T(1,128)S(1)}) custom-call(s32[6]{0:T(128)S(1)} %pad_add_fusion.len_ref, bf16[6,256,512]{2,1,0:T(8,128)(2,1)S(1)} %copy-done.6, f32[6,1,256]{2,1,0:T(1,128)S(1)} %pad_maximum_fusion.12.l_ref, f32[6,256,256]{2,1,0:T(8,128)S(1)} %copy-done.36, ...), custom_call_target="tpu_custom_call" | custom-call | flops 5600000 | bytes 5600 | tf_op jit(solution)/shard_map/pallas_call | solution.py:187
  320.3 4.8 all-to-all-start.8
  332.6 11.3 %collective-permute-done.14.refs_5_ = bf16[2,384,512]{2,1,0:T(8,128)(2,1)} collective-permute-done((bf16[2,384,512]{2,1,0:T(8,128)(2,1)}, bf16[2,384,512]{2,1,0:T(8,128)(2,1)}, u32[]{:S(2)}, u32[]{:S(2)}) %collective-permute-start.14) | collective-permute-done | bytes 786464 | tf_op jit(solution)/shard_map/ppermute | solution.py:623
  348.0 5.2 %shard_map.185 = (f32[1,384,512]{2,1,0:T(8,128)S(1)}, bf16[1,384,512]{2,1,0:T(8,128)(2,1)}) custom-call(s32[2]{0:T(128)S(1)} %pad_add_fusion.2.refs_0_, bf16[4,512,384]{2,1,0:T(8,128)(2,1)} %all-to-all-done.3.g_ref.refs_1_, bf16[4,512,384]{2,1,0:T(8,128)(2,1)S(1)} %copy-done.25, bf16[2,512,256]{2,1,0:T(8,128)(2,1)S(1)} %copy-done.49, ...), custom_call_target="tpu_custom_call" | custom-call | flops 402653 | bytes 6000 | tf_op jit(solution)/shard_map/pallas_call | solution.py:482
  353.2 5.8 %shard_map.186 = (bf16[2,256,512]{2,1,0:T(8,128)(2,1)S(1)}, f32[2,1,256]{2,1,0:T(1,128)S(1)}, f32[2,1,256]{2,1,0:T(1,128)S(1)}) custom-call(s32[6]{0:T(128)S(1)} %pad_add_fusion.len_ref, bf16[6,256,512]{2,1,0:T(8,128)(2,1)S(1)} %copy-done.7, f32[6,1,256]{2,1,0:T(1,128)S(1)} %pad_maximum_fusion.12.l_ref, f32[6,256,256]{2,1,0:T(8,128)S(1)} %copy-done.37, ...), custom_call_target="tpu_custom_call" | custom-call | flops 2800000 | bytes 2800 | tf_op jit(solution)/shard_map/pallas_call | solution.py:187
  359.2 8.7 %collective-permute-done.15 = bf16[1,384,512]{2,1,0:T(8,128)(2,1)} collective-permute-done((bf16[1,384,512]{2,1,0:T(8,128)(2,1)S(1)}, bf16[1,384,512]{2,1,0:T(8,128)(2,1)}, u32[]{:S(2)}, u32[]{:S(2)}) %collective-permute-start.15) | collective-permute-done | bytes 393248 | tf_op jit(solution)/shard_map/ppermute | solution.py:623
  373.7 5.8 %shard_map.188 = bf16[4,512,384]{2,1,0:T(8,128)(2,1)} custom-call(s32[1]{0:T(128)} %bitcast.30.flag_ref, bf16[4,256,512]{2,1,0:T(8,128)(2,1)S(1)} %copy-done.13, bf16[2,256,512]{2,1,0:T(8,128)(2,1)S(1)} %copy-done.29, bf16[2,16,256]{2,1,0:T(8,128)(2,1)S(1)} %get-tuple-element.354.l_ref, bf16[4,384,1024]{2,1,0:T(8,128)(2,1)} %all-to-all-done.2.w_ref, ...), custom_call_target="tpu_custom_call" | custom-call | flops 1610612 | bytes 8000 | tf_op jit(solution)/shard_map/pallas_call | solution.py:418
  390.8 5.1 shard_map.190
  398.8 4.5 all-to-all-start.9
  413.1 6.8 %collective-permute-done.27.refs_6_ = bf16[2,384,640]{2,1,0:T(8,128)(2,1)} collective-permute-done((bf16[2,384,640]{2,1,0:T(8,128)(2,1)}, bf16[2,384,640]{2,1,0:T(8,128)(2,1)}, u32[]{:S(2)}, u32[]{:S(2)}) %collective-permute-start.27) | collective-permute-done | bytes 983072 | tf_op jit(solution)/shard_map/ppermute | solution.py:623
  420.9 20.6 %collective-permute-done.26 = bf16[1,384,512]{2,1,0:T(8,128)(2,1)S(1)} collective-permute-done((bf16[1,384,512]{2,1,0:T(8,128)(2,1)}, bf16[1,384,512]{2,1,0:T(8,128)(2,1)S(1)}, u32[]{:S(2)}, u32[]{:S(2)}) %collective-permute-start.26) | collective-permute-done | bytes 393248 | tf_op jit(solution)/shard_map/ppermute | solution.py:623
  451.8 4.6 all-to-all-start.10
  459.5 15.9 %collective-permute-done.28 = bf16[1,384,640]{2,1,0:T(8,128)(2,1)} collective-permute-done((bf16[1,384,640]{2,1,0:T(8,128)(2,1)}, bf16[1,384,640]{2,1,0:T(8,128)(2,1)}, u32[]{:S(2)}, u32[]{:S(2)}) %collective-permute-start.28) | collective-permute-done | bytes 491552 | tf_op jit(solution)/shard_map/ppermute | solution.py:623
  491.7 4.3 collective-permute-start.33
  496.1 6.2 %collective-permute-done.33 = bf16[2,96,2]{1,2,0:T(2,128)(2,1)S(1)} collective-permute-done((bf16[2,96,2]{1,2,0:T(2,128)(2,1)S(1)}, bf16[2,96,2]{1,2,0:T(2,128)(2,1)S(1)}, u32[]{:S(2)}, u32[]{:S(2)}) %collective-permute-start.33) | collective-permute-done | bytes 800 | tf_op jit(solution)/shard_map/ppermute | solution.py:623
  (413 shorter events, 194.0 us)
Async XLA Ops:
  6.0 25.0 %all-to-all-start = ((bf16[4,528,384]{2,1,0:T(8,128)(2,1)}), bf16[4,528,384]{2,1,0:T(8,128)(2,1)S(1)}, u32[]{:S(2)}, u32[]{:S(2)}) async-start(bf16[4,528,384]{2,1,0:T(8,128)(2,1)} %broadcast_in_dim.157), calls=%async_computation | async-start | bytes 3244032 | tf_op jit(solution)/shard_map/all_to_all | solution.py:631
  32.2 30.8 %all-to-all-start.1 = ((bf16[4,384,768]{2,1,0:T(8,128)(2,1)}), bf16[4,384,768]{2,1,0:T(8,128)(2,1)S(1)}, u32[]{:S(2)}, u32[]{:S(2)}) async-start(bf16[4,384,768]{2,1,0:T(8,128)(2,1)} %pad_maximum_fusion.1), calls=%async_computation.1 | async-start | bytes 4718592 | tf_op jit(solution)/shard_map/all_to_all | solution.py:631
  63.0 40.3 %all-to-all-start.2 = ((bf16[4,384,1024]{2,1,0:T(8,128)(2,1)}), bf16[4,384,1024]{2,1,0:T(8,128)(2,1)}, u32[]{:S(2)}, u32[]{:S(2)}) async-start(bf16[4,384,1024]{2,1,0:T(8,128)(2,1)} %pad_maximum_fusion), calls=%async_computation.2 | async-start | bytes 6291456 | tf_op jit(solution)/shard_map/all_to_all | solution.py:631
  67.7 57.5 %collective-permute-start.1 = (bf16[4,384,768]{2,1,0:T(8,128)(2,1)S(1)}, bf16[4,384,768]{2,1,0:T(8,128)(2,1)}, u32[]{:S(2)}, u32[]{:S(2)}) collective-permute-start(bf16[4,384,768]{2,1,0:T(8,128)(2,1)S(1)} %all-to-all-done.1.wa_ref), channel_id=1, source_target_pairs={{0,8},{8,0},{16,24},{24,16},{1,9},{9,1},{17,25},{25,17},{2,10},{10... | collective-permute-start | bytes 7077896 | tf_op jit(solution)/shard_map/ppermute | solution.py:623
  72.1 45.6 %collective-permute-start = (bf16[4,512,384]{2,1,0:T(8,128)(2,1)}, bf16[4,512,384]{2,1,0:T(8,128)(2,1)}, u32[]{:S(2)}, u32[]{:S(2)}) collective-permute-start(bf16[4,512,384]{2,1,0:T(8,128)(2,1)} %slice.206.x_ref), channel_id=1, source_target_pairs={{0,4},{4,0},{1,5},{5,1},{2,6},{6,2},{3,7},{7,3},{8,12},{12,8},{9,1... | collective-permute-start | bytes 4718600 | tf_op jit(solution)/shard_map/ppermute | solution.py:623
  104.6 39.0 %all-to-all-start.3 = ((bf16[4,512,384]{2,1,0:T(8,128)(2,1)}), bf16[4,512,384]{2,1,0:T(8,128)(2,1)}, u32[]{:S(2)}, u32[]{:S(2)}) async-start(bf16[4,512,384]{2,1,0:T(8,128)(2,1)} %broadcast_in_dim.158), calls=%async_computation.3 | async-start | bytes 3145728 | tf_op jit(solution)/shard_map/all_to_all | solution.py:631
  172.7 23.8 %all-to-all-start.5 = ((bf16[4,512,384]{2,1,0:T(8,128)(2,1)}), bf16[4,512,384]{2,1,0:T(8,128)(2,1)S(1)}, u32[]{:S(2)}, u32[]{:S(2)}) async-start(bf16[4,512,384]{2,1,0:T(8,128)(2,1)} %broadcast_in_dim.162), calls=%async_computation.5 | async-start | bytes 3145728 | tf_op jit(solution)/shard_map/all_to_all | solution.py:631
  176.8 21.0 %collective-permute-start.4 = (bf16[4,512,384]{2,1,0:T(8,128)(2,1)}, bf16[4,512,384]{2,1,0:T(8,128)(2,1)S(1)}, u32[]{:S(2)}, u32[]{:S(2)}) collective-permute-start(bf16[4,512,384]{2,1,0:T(8,128)(2,1)} %all-to-all-done.3.g_ref.refs_1_), channel_id=1, source_target_pairs={{0,4},{4,0},{1,5},{5,1},{2,6},{6,2},{3,7},{7,3},{8,12},{12,8},{9,1... | collective-permute-start | bytes 4718600 | tf_op jit(solution)/shard_map/ppermute | solution.py:623
  230.0 25.4 %all-to-all-start.6 = ((bf16[4,512,384]{2,1,0:T(8,128)(2,1)}), bf16[4,512,384]{2,1,0:T(8,128)(2,1)}, u32[]{:S(2)}, u32[]{:S(2)}) async-start(bf16[4,512,384]{2,1,0:T(8,128)(2,1)} %add_convert_fusion.2), calls=%async_computation.6 | async-start | bytes 3145728 | tf_op jit(solution)/shard_map/all_to_all | solution.py:631
  235.7 19.7 %collective-permute-start.9 = (f32[4,128]{1,0:T(4,128)S(1)}, f32[4,128]{1,0:T(4,128)S(1)}, u32[]{:S(2)}, u32[]{:S(2)}) collective-permute-start(f32[4,128]{1,0:T(4,128)S(1)} %bitcast.198), channel_id=1, source_target_pairs={{0,3},{1,2},{2,1},{3,0},{4,7},{5,6},{6,5},{7,4},{8,11},{9,10},{10,... | collective-permute-start | bytes 6152 | tf_op jit(solution)/shard_map/ppermute | solution.py:623
  244.4 19.3 %collective-permute-start.10 = (bf16[2,384,512]{2,1,0:T(8,128)(2,1)}, bf16[2,384,512]{2,1,0:T(8,128)(2,1)}, u32[]{:S(2)}, u32[]{:S(2)}) collective-permute-start(bf16[2,384,512]{2,1,0:T(8,128)(2,1)} %shard_map.175), channel_id=1, source_target_pairs={{0,8},{8,0},{16,24},{24,16},{1,9},{9,1},{17,25},{25,17},{2,10},{10... | collective-permute-start | bytes 2359304 | tf_op jit(solution)/shard_map/ppermute | solution.py:623
  274.9 23.1 %all-to-all-start.7 = ((bf16[4,1536,128]{2,1,0:T(8,128)(2,1)}), bf16[4,1536,128]{2,1,0:T(8,128)(2,1)}, u32[]{:S(2)}, u32[]{:S(2)}) async-start(bf16[4,1536,128]{2,1,0:T(8,128)(2,1)} %copy-done.32), calls=%async_computation.7 | async-start | bytes 3145728 | tf_op jit(solution)/shard_map/all_to_all | solution.py:631
  298.0 20.8 %collective-permute-start.12 = (bf16[4,512,384]{2,1,0:T(8,128)(2,1)}, bf16[4,512,384]{2,1,0:T(8,128)(2,1)S(1)}, u32[]{:S(2)}, u32[]{:S(2)}) collective-permute-start(bf16[4,512,384]{2,1,0:T(8,128)(2,1)} %copy-done.69), channel_id=1, source_target_pairs={{0,4},{4,0},{1,5},{5,1},{2,6},{6,2},{3,7},{7,3},{8,12},{12,8},{9,1... | collective-permute-start | bytes 4718600 | tf_op jit(solution)/shard_map/ppermute | solution.py:623
  298.0 50.0 %collective-permute-start.16 = (bf16[2,384,512]{2,1,0:T(8,128)(2,1)}, bf16[2,384,512]{2,1,0:T(8,128)(2,1)}, u32[]{:S(2)}, u32[]{:S(2)}) collective-permute-start(bf16[2,384,512]{2,1,0:T(8,128)(2,1)} %copy-done.61), channel_id=1, source_target_pairs={{0,8},{8,0},{16,24},{24,16},{1,9},{9,1},{17,25},{25,17},{2,10},{10... | collective-permute-start | bytes 2359304 | tf_op jit(solution)/shard_map/ppermute | solution.py:623
  299.6 44.3 %collective-permute-start.14 = (bf16[2,384,512]{2,1,0:T(8,128)(2,1)}, bf16[2,384,512]{2,1,0:T(8,128)(2,1)}, u32[]{:S(2)}, u32[]{:S(2)}) collective-permute-start(bf16[2,384,512]{2,1,0:T(8,128)(2,1)} %copy-done.62), channel_id=1, source_target_pairs={{0,8},{8,0},{16,24},{24,16},{1,9},{9,1},{17,25},{25,17},{2,10},{10... | collective-permute-start | bytes 2359304 | tf_op jit(solution)/shard_map/ppermute | solution.py:623
  320.3 51.2 %all-to-all-start.8 = ((bf16[4,512,384]{2,1,0:T(8,128)(2,1)}), bf16[4,512,384]{2,1,0:T(8,128)(2,1)}, u32[]{:S(2)}, u32[]{:S(2)}) async-start(bf16[4,512,384]{2,1,0:T(8,128)(2,1)} %add_convert_fusion.1), calls=%async_computation.8 | async-start | bytes 3145728 | tf_op jit(solution)/shard_map/all_to_all | solution.py:631
  325.1 28.1 %collective-permute-start.13 = (bf16[1,384,512]{2,1,0:T(8,128)(2,1)}, bf16[1,384,512]{2,1,0:T(8,128)(2,1)}, u32[]{:S(2)}, u32[]{:S(2)}) collective-permute-start(bf16[1,384,512]{2,1,0:T(8,128)(2,1)} %copy-done.70), channel_id=1, source_target_pairs={{0,16},{8,24},{16,0},{24,8},{1,17},{9,25},{17,1},{25,9},{2,18},{10... | collective-permute-start | bytes 1179656 | tf_op jit(solution)/shard_map/ppermute | solution.py:623
  330.9 39.6 %collective-permute-start.18 = (bf16[2,384,512]{2,1,0:T(8,128)(2,1)S(1)}, bf16[2,384,512]{2,1,0:T(8,128)(2,1)S(1)}, u32[]{:S(2)}, u32[]{:S(2)}) collective-permute-start(bf16[2,384,512]{2,1,0:T(8,128)(2,1)S(1)} %shard_map.183), channel_id=1, source_target_pairs={{0,8},{8,0},{16,24},{24,16},{1,9},{9,1},{17,25},{25,17},{2,10},{10... | collective-permute-start | bytes 2359304 | tf_op jit(solution)/shard_map/ppermute | solution.py:623
  347.9 20.1 %collective-permute-start.15 = (bf16[1,384,512]{2,1,0:T(8,128)(2,1)S(1)}, bf16[1,384,512]{2,1,0:T(8,128)(2,1)}, u32[]{:S(2)}, u32[]{:S(2)}) collective-permute-start(bf16[1,384,512]{2,1,0:T(8,128)(2,1)S(1)} %get-tuple-element.145), channel_id=1, source_target_pairs={{0,16},{8,24},{16,0},{24,8},{1,17},{9,25},{17,1},{25,9},{2,18},{10... | collective-permute-start | bytes 1179656 | tf_op jit(solution)/shard_map/ppermute | solution.py:623
  383.7 36.2 %collective-permute-start.27 = (bf16[2,384,640]{2,1,0:T(8,128)(2,1)}, bf16[2,384,640]{2,1,0:T(8,128)(2,1)}, u32[]{:S(2)}, u32[]{:S(2)}) collective-permute-start(bf16[2,384,640]{2,1,0:T(8,128)(2,1)} %shard_map.187), channel_id=1, source_target_pairs={{0,8},{8,0},{16,24},{24,16},{1,9},{9,1},{17,25},{25,17},{2,10},{10... | collective-permute-start | bytes 2949128 | tf_op jit(solution)/shard_map/ppermute | solution.py:623
  398.8 50.5 %all-to-all-start.9 = ((bf16[4,512,384]{2,1,0:T(8,128)(2,1)}), bf16[4,512,384]{2,1,0:T(8,128)(2,1)}, u32[]{:S(2)}, u32[]{:S(2)}) async-start(bf16[4,512,384]{2,1,0:T(8,128)(2,1)} %add_convert_fusion), calls=%async_computation.9 | async-start | bytes 3145728 | tf_op jit(solution)/shard_map/all_to_all | solution.py:631
  403.6 45.0 %collective-permute-start.29 = (bf16[2,96,768]{2,1,0:T(8,128)(2,1)S(1)}, bf16[2,96,768]{2,1,0:T(8,128)(2,1)S(1)}, u32[]{:S(2)}, u32[]{:S(2)}) collective-permute-start(bf16[2,96,768]{2,1,0:T(8,128)(2,1)S(1)} %pad_maximum_fusion.11), channel_id=1, source_target_pairs={{0,8},{8,0},{16,24},{24,16},{1,9},{9,1},{17,25},{25,17},{2,10},{10... | collective-permute-start | bytes 884744 | tf_op jit(solution)/shard_map/ppermute | solution.py:623
  404.0 45.3 %collective-permute-start.17 = (bf16[1,384,512]{2,1,0:T(8,128)(2,1)}, bf16[1,384,512]{2,1,0:T(8,128)(2,1)}, u32[]{:S(2)}, u32[]{:S(2)}) collective-permute-start(bf16[1,384,512]{2,1,0:T(8,128)(2,1)} %get-tuple-element.148), channel_id=1, source_target_pairs={{0,16},{8,24},{16,0},{24,8},{1,17},{9,25},{17,1},{25,9},{2,18},{10... | collective-permute-start | bytes 1179656 | tf_op jit(solution)/shard_map/ppermute | solution.py:623
  405.6 43.7 %collective-permute-start.24 = (f32[4,128]{1,0:T(4,128)S(1)}, f32[4,128]{1,0:T(4,128)S(1)}, u32[]{:S(2)}, u32[]{:S(2)}) collective-permute-start(f32[4,128]{1,0:T(4,128)S(1)} %bitcast.194), channel_id=1, source_target_pairs={{0,3},{1,2},{2,1},{3,0},{4,7},{5,6},{6,5},{7,4},{8,11},{9,10},{10,... | collective-permute-start | bytes 6152 | tf_op jit(solution)/shard_map/ppermute | solution.py:623
  408.3 33.2 %collective-permute-start.26 = (bf16[1,384,512]{2,1,0:T(8,128)(2,1)}, bf16[1,384,512]{2,1,0:T(8,128)(2,1)S(1)}, u32[]{:S(2)}, u32[]{:S(2)}) collective-permute-start(bf16[1,384,512]{2,1,0:T(8,128)(2,1)} %get-tuple-element.168), channel_id=1, source_target_pairs={{0,16},{8,24},{16,0},{24,8},{1,17},{9,25},{17,1},{25,9},{2,18},{10... | collective-permute-start | bytes 1179656 | tf_op jit(solution)/shard_map/ppermute | solution.py:623
  419.9 29.4 %collective-permute-start.23 = (f32[4,128]{1,0:T(4,128)S(1)}, f32[4,128]{1,0:T(4,128)S(1)}, u32[]{:S(2)}, u32[]{:S(2)}) collective-permute-start(f32[4,128]{1,0:T(4,128)S(1)} %bitcast.195), channel_id=1, source_target_pairs={{0,2},{1,3},{2,0},{3,1},{4,6},{5,7},{6,4},{7,5},{8,10},{9,11},{10,... | collective-permute-start | bytes 6152 | tf_op jit(solution)/shard_map/ppermute | solution.py:623
  449.3 26.1 %collective-permute-start.28 = (bf16[1,384,640]{2,1,0:T(8,128)(2,1)}, bf16[1,384,640]{2,1,0:T(8,128)(2,1)}, u32[]{:S(2)}, u32[]{:S(2)}) collective-permute-start(bf16[1,384,640]{2,1,0:T(8,128)(2,1)} %get-tuple-element.171), channel_id=1, source_target_pairs={{0,16},{8,24},{16,0},{24,8},{1,17},{9,25},{17,1},{25,9},{2,18},{10... | collective-permute-start | bytes 1474568 | tf_op jit(solution)/shard_map/ppermute | solution.py:623
  451.8 31.4 %all-to-all-start.10 = ((bf16[4,96,1536]{2,1,0:T(8,128)(2,1)}), bf16[4,96,1536]{2,1,0:T(8,128)(2,1)}, u32[]{:S(2)}, u32[]{:S(2)}) async-start(bf16[4,96,1536]{2,1,0:T(8,128)(2,1)} %bitcast.169), calls=%async_computation.10 | async-start | bytes 2359296 | tf_op jit(solution)/shard_map/all_to_all | solution.py:631
  456.6 23.5 %collective-permute-start.30 = (bf16[1,96,768]{2,1,0:T(8,128)(2,1)S(1)}, bf16[1,96,768]{2,1,0:T(8,128)(2,1)S(1)}, u32[]{:S(2)}, u32[]{:S(2)}) collective-permute-start(bf16[1,96,768]{2,1,0:T(8,128)(2,1)S(1)} %slice.266), channel_id=1, source_target_pairs={{0,16},{8,24},{16,0},{24,8},{1,17},{9,25},{17,1},{25,9},{2,18},{10... | collective-permute-start | bytes 442376 | tf_op jit(solution)/shard_map/ppermute | solution.py:623
  459.5 20.6 %collective-permute-start.20 = (bf16[512,384]{1,0:T(8,128)(2,1)}, bf16[512,384]{1,0:T(8,128)(2,1)S(1)}, u32[]{:S(2)}, u32[]{:S(2)}) collective-permute-start(bf16[512,384]{1,0:T(8,128)(2,1)} %multiply_convert_fusion), channel_id=1, source_target_pairs={{0,4},{4,0},{1,5},{5,1},{2,6},{6,2},{3,7},{7,3},{8,12},{12,8},{9,1... | collective-permute-start | bytes 1179656 | tf_op jit(solution)/shard_map/ppermute | solution.py:623
  483.2 28.9 %all-to-all-start.11 = ((bf16[4,96,1152]{2,1,0:T(8,128)(2,1)}), bf16[4,96,1152]{2,1,0:T(8,128)(2,1)S(1)}, u32[]{:S(2)}, u32[]{:S(2)}) async-start(bf16[4,96,1152]{2,1,0:T(8,128)(2,1)} %bitcast.38), calls=%async_computation.11 | async-start | bytes 1769472 | tf_op jit(solution)/shard_map/all_to_all | solution.py:631
  486.7 24.7 %collective-permute-start.31 = (bf16[96,768]{1,0:T(8,128)(2,1)S(1)}, bf16[96,768]{1,0:T(8,128)(2,1)S(1)}, u32[]{:S(2)}, u32[]{:S(2)}) collective-permute-start(bf16[96,768]{1,0:T(8,128)(2,1)S(1)} %fusion.18), channel_id=1, source_target_pairs={{0,0},{1,8},{2,16},{3,24},{8,1},{9,9},{10,17},{11,25},{16,2},{17,1... | collective-permute-start | bytes 442376 | tf_op jit(solution)/shard_map/ppermute | solution.py:935
  (108 other events, 704.7 us)

commit v4 on v3

--- a/solution.py
+++ b/solution.py
@@ -896,7 +896,6 @@
     dn1_here = partial(dn1_own, dn1_far)
     dn1_got = exchange(dn1_here, "wid")
     right_shared = after(right_shared, dn1_here, shared_got)
-    right_shared = after(right_shared, next_own)
     keep_shared, next_shared = dp_even(
         shared_terms, n1_both, (right_shared, *flat_both), 5 * HD, shared_got, half_flag
     )

time: 522 us -> 517 us (level)
    unnamed x218 -> x216, local copies, waits for them, and re-layouts: 43.1 us -> 43.8 us
where the time goes in v4:
time: 517 us; the launch traced here: 510 us
  waiting for transfers between devices  179 us (35%)
  Pallas kernels  114 us (22%)
  starting transfers between devices  82.6 us (16%)
  local copies, waits for them, and re-layouts  67.9 us (13%)
  other arithmetic  40.8 us (8%)
  blocking collectives  22.8 us (4%)
    all_to_all x11, waiting for transfers between devices, exchange(): return lax.all_to_all(x, axis, split_axis=0, concat_axis=0, tiled=True)  98.4 us
    ppermute x34, waiting for transfers between devices, swap(): return lax.ppermute(x, axis, [(n, n ^ k) for n in range(size)])  81 us
    all_to_all x11, starting transfers between devices, exchange(): return lax.all_to_all(x, axis, split_axis=0, concat_axis=0, tiled=True)  48.6 us
    unnamed x216, local copies, waits for them, and re-layouts  43.8 us
    ppermute x34, starting transfers between devices, swap(): return lax.ppermute(x, axis, [(n, n ^ k) for n in range(size)])  32.7 us
    all_to_all x1, blocking collectives, exchange(): return lax.all_to_all(x, axis, split_axis=0, concat_axis=0, tiled=True)  22.8 us
    pallas_call x2, Pallas kernels, feed_forward(): pl.pallas_call(functools.partial(ffn_kernel, n), out_shape=[shape(n, half...  22 us
    pallas_call x5, Pallas kernels, weight_add(): pl.pallas_call(functools.partial(weight_add_kernel, terms), out_shape=[sh...  17.3 us
  transfers between devices with their start and end apart: 47, of which 17 were waited for; matrix products, arithmetic and copies ran while one was open for 11% of the time, Pallas kernels for 18%

profile of v4, /device:TPU:0, one launch (start us, length us, event | category | flops | bytes accessed | tf_op | source)
XLA Modules:
  0.0 510.1 jit_solution(548594145113001073)
XLA Ops:
  6.1 5.2 %all-to-all-start = ((bf16[4,528,384]{2,1,0:T(8,128)(2,1)}), bf16[4,528,384]{2,1,0:T(8,128)(2,1)S(1)}, u32[]{:S(2)}, u32[]{:S(2)}) async-start(bf16[4,528,384]{2,1,0:T(8,128)(2,1)} %broadcast_in_dim.157), calls=%async_computation | async-start | bytes 3244032 | tf_op jit(solution)/shard_map/all_to_all | solution.py:631
  17.1 13.9 %all-to-all-done = bf16[4,528,384]{2,1,0:T(8,128)(2,1)S(1)} async-done(((bf16[4,528,384]{2,1,0:T(8,128)(2,1)}), bf16[4,528,384]{2,1,0:T(8,128)(2,1)S(1)}, u32[]{:S(2)}, u32[]{:S(2)}) %all-to-all-start) | async-done | bytes 1622048 | tf_op jit(solution)/shard_map/all_to_all | solution.py:631
  40.9 22.1 %all-to-all-done.1.wa_ref = bf16[4,384,768]{2,1,0:T(8,128)(2,1)S(1)} async-done(((bf16[4,384,768]{2,1,0:T(8,128)(2,1)}), bf16[4,384,768]{2,1,0:T(8,128)(2,1)S(1)}, u32[]{:S(2)}, u32[]{:S(2)}) %all-to-all-start.1) | async-done | bytes 2359328 | tf_op jit(solution)/shard_map/all_to_all | solution.py:631
  63.0 4.6 all-to-all-start.2
  72.2 31.2 %all-to-all-done.2.w_ref = bf16[4,384,1024]{2,1,0:T(8,128)(2,1)} async-done(((bf16[4,384,1024]{2,1,0:T(8,128)(2,1)}), bf16[4,384,1024]{2,1,0:T(8,128)(2,1)}, u32[]{:S(2)}, u32[]{:S(2)}) %all-to-all-start.2) | async-done | bytes 3145760 | tf_op jit(solution)/shard_map/all_to_all | solution.py:631
  104.6 4.6 all-to-all-start.3
  111.0 5.4 %shard_map.169 = (bf16[2,256,512]{2,1,0:T(8,128)(2,1)S(1)}, bf16[2,256,512]{2,1,0:T(8,128)(2,1)S(1)}, f32[2,16,256]{2,1,0:T(8,128)S(1)}, f32[2,1,256]{2,1,0:T(1,128)S(1)}, bf16[4,512,384]{2,1,0:T(8,128)(2,1)S(1)}) custom-call(bf16[4,512,384]{2,1,0:T(8,128)(2,1)} %slice.206.x_ref, bf16[4,384,1024]{2,1,0:T(8,128)(2,1)} %all-to-all-done.2.w_ref, ...), custom_call_target="tpu_custom_call" | custom-call | flops 1610612 | bytes 8000 | tf_op jit(solution)/shard_map/pallas_call | solution.py:261
  117.7 5.7 %shard_map.170 = (bf16[2,256,512]{2,1,0:T(8,128)(2,1)S(1)}, bf16[2,256,512]{2,1,0:T(8,128)(2,1)S(1)}, f32[2,16,256]{2,1,0:T(8,128)S(1)}, f32[2,1,256]{2,1,0:T(1,128)}, bf16[4,512,384]{2,1,0:T(8,128)(2,1)S(1)}) custom-call(bf16[4,512,384]{2,1,0:T(8,128)(2,1)} %collective-permute-done.x_ref, bf16[4,384,1024]{2,1,0:T(8,128)(2,1)} %all-to-all-done.2.w_ref, ...), custom_call_target="tpu_custom_call" | custom-call | flops 1610612 | bytes 8000 | tf_op jit(solution)/shard_map/pallas_call | solution.py:261
  125.1 15.0 %shard_map.171 = (bf16[6,256,128]{2,1,0:T(8,128)(2,1)S(1)}, f32[6,256,256]{2,1,0:T(8,128)S(1)}, f32[6,256,256]{2,1,0:T(8,128)S(1)}, f32[6,256,256]{2,1,0:T(8,128)S(1)}) custom-call(s32[6]{0:T(128)S(1)} %pad_add_fusion.len_ref, bf16[6,256,512]{2,1,0:T(8,128)(2,1)} %pad_maximum_fusion.2.x_ref, f32[6,1,256]{2,1,0:T(1,128)S(1)} %pad_maximum_fusion.12.l_ref), custom_call_target="tpu_custom_call" | custom-call | flops 9600000 | bytes 6600 | tf_op jit(solution)/shard_map/pallas_call | solution.py:167
  143.9 22.8 %all_to_all.60.o_ref = bf16[4,1536,128]{2,1,0:T(8,128)(2,1)S(1)} all-to-all(bf16[4,1536,128]{2,1,0:T(8,128)(2,1)S(1)} %broadcast_in_dim.160), channel_id=1, replica_groups=mesh['dp'=4,'hid'=2,'wid'=4] {'wid'}, dimensions={0} | all-to-all | bytes 3145728 | tf_op jit(solution)/shard_map/all_to_all | solution.py:631
  177.0 19.6 %all-to-all-done.5.h_ref = bf16[4,512,384]{2,1,0:T(8,128)(2,1)S(1)} async-done(((bf16[4,512,384]{2,1,0:T(8,128)(2,1)}), bf16[4,512,384]{2,1,0:T(8,128)(2,1)S(1)}, u32[]{:S(2)}, u32[]{:S(2)}) %all-to-all-start.5) | async-done | bytes 1572896 | tf_op jit(solution)/shard_map/all_to_all | solution.py:631
  201.2 10.9 %shard_map.174 = (bf16[4,512,384]{2,1,0:T(8,128)(2,1)S(1)}, bf16[2,512,256]{2,1,0:T(8,128)(2,1)S(1)}, bf16[2,512,512]{2,1,0:T(8,128)(2,1)S(1)}, bf16[4,512,384]{...) custom-call(s32[2]{0:T(128)S(1)} %get-tuple-element.278.len_ref, s32[1]{0:T(128)} %bitcast.12.side_ref, ...), custom_call_target="tpu_custom_call" | custom-call | flops 4026531 | bytes 12000 | tf_op jit(solution)/shard_map/pallas_call | solution.py:347
  213.0 11.2 %shard_map.173 = (bf16[4,512,384]{2,1,0:T(8,128)(2,1)S(1)}, bf16[2,512,256]{2,1,0:T(8,128)(2,1)S(1)}, bf16[2,512,512]{2,1,0:T(8,128)(2,1)S(1)}, f32[4,512,384]{2...) custom-call(s32[2]{0:T(128)S(1)} %get-tuple-element.276.len_ref, s32[1]{0:T(128)} %bitcast.12.side_ref, ...), custom_call_target="tpu_custom_call" | custom-call | flops 4026531 | bytes 12000 | tf_op jit(solution)/shard_map/pallas_call | solution.py:347
  230.0 4.5 all-to-all-start.6
  274.9 4.6 all-to-all-start.7
  279.6 5.5 %shard_map.180 = (f32[4,512,384]{2,1,0:T(8,128)}, bf16[4,512,384]{2,1,0:T(8,128)(2,1)S(1)}) custom-call(s32[1]{0:T(128)} %bitcast.12.side_ref, bf16[2,512,256]{2,1,0:T(8,128)(2,1)S(1)} %copy-done.48, bf16[2,512,256]{2,1,0:T(8,128)(2,1)S(1)} %copy-done.44, bf16[4,384,768]{2,1,0:T(8,128)(2,1)S(1)} %copy-done.1, bf16[4,384,768]{2,1,0:T(8,128)(2,1)} %collective-permute-done.1.wb_ref), custom_call_target="tpu_custom_call" | custom-call | flops 1610612 | bytes 12000 | tf_op jit(solution)/shard_map/pallas_call | solution.py:390
  286.3 11.7 %all-to-all-done.7 = bf16[4,1536,128]{2,1,0:T(8,128)(2,1)} async-done(((bf16[4,1536,128]{2,1,0:T(8,128)(2,1)}), bf16[4,1536,128]{2,1,0:T(8,128)(2,1)}, u32[]{:S(2)}, u32[]{:S(2)}) %all-to-all-start.7) | async-done | bytes 1572896 | tf_op jit(solution)/shard_map/all_to_all | solution.py:631
  308.5 10.2 %shard_map.182 = (bf16[4,256,512]{2,1,0:T(8,128)(2,1)S(1)}, f32[4,1,256]{2,1,0:T(1,128)S(1)}, f32[4,1,256]{2,1,0:T(1,128)S(1)}) custom-call(s32[6]{0:T(128)S(1)} %pad_add_fusion.len_ref, bf16[6,256,512]{2,1,0:T(8,128)(2,1)S(1)} %copy-done.6, f32[6,1,256]{2,1,0:T(1,128)S(1)} %pad_maximum_fusion.12.l_ref, f32[6,256,256]{2,1,0:T(8,128)S(1)} %copy-done.36, ...), custom_call_target="tpu_custom_call" | custom-call | flops 5600000 | bytes 5600 | tf_op jit(solution)/shard_map/pallas_call | solution.py:187
  320.2 4.8 all-to-all-start.8
  332.6 11.3 %collective-permute-done.14.refs_5_ = bf16[2,384,512]{2,1,0:T(8,128)(2,1)} collective-permute-done((bf16[2,384,512]{2,1,0:T(8,128)(2,1)}, bf16[2,384,512]{2,1,0:T(8,128)(2,1)}, u32[]{:S(2)}, u32[]{:S(2)}) %collective-permute-start.14) | collective-permute-done | bytes 786464 | tf_op jit(solution)/shard_map/ppermute | solution.py:623
  348.0 5.2 %shard_map.185 = (f32[1,384,512]{2,1,0:T(8,128)S(1)}, bf16[1,384,512]{2,1,0:T(8,128)(2,1)}) custom-call(s32[2]{0:T(128)S(1)} %pad_add_fusion.2.refs_0_, bf16[4,512,384]{2,1,0:T(8,128)(2,1)} %all-to-all-done.3.g_ref.refs_1_, bf16[4,512,384]{2,1,0:T(8,128)(2,1)S(1)} %copy-done.25, bf16[2,512,256]{2,1,0:T(8,128)(2,1)S(1)} %copy-done.49, ...), custom_call_target="tpu_custom_call" | custom-call | flops 402653 | bytes 6000 | tf_op jit(solution)/shard_map/pallas_call | solution.py:482
  353.2 5.8 %shard_map.186 = (bf16[2,256,512]{2,1,0:T(8,128)(2,1)S(1)}, f32[2,1,256]{2,1,0:T(1,128)S(1)}, f32[2,1,256]{2,1,0:T(1,128)S(1)}) custom-call(s32[6]{0:T(128)S(1)} %pad_add_fusion.len_ref, bf16[6,256,512]{2,1,0:T(8,128)(2,1)S(1)} %copy-done.7, f32[6,1,256]{2,1,0:T(1,128)S(1)} %pad_maximum_fusion.12.l_ref, f32[6,256,256]{2,1,0:T(8,128)S(1)} %copy-done.37, ...), custom_call_target="tpu_custom_call" | custom-call | flops 2800000 | bytes 2800 | tf_op jit(solution)/shard_map/pallas_call | solution.py:187
  359.2 8.7 %collective-permute-done.15 = bf16[1,384,512]{2,1,0:T(8,128)(2,1)} collective-permute-done((bf16[1,384,512]{2,1,0:T(8,128)(2,1)S(1)}, bf16[1,384,512]{2,1,0:T(8,128)(2,1)}, u32[]{:S(2)}, u32[]{:S(2)}) %collective-permute-start.15) | collective-permute-done | bytes 393248 | tf_op jit(solution)/shard_map/ppermute | solution.py:623
  373.7 5.8 %shard_map.188 = bf16[4,512,384]{2,1,0:T(8,128)(2,1)} custom-call(s32[1]{0:T(128)} %bitcast.30.flag_ref, bf16[4,256,512]{2,1,0:T(8,128)(2,1)S(1)} %copy-done.13, bf16[2,256,512]{2,1,0:T(8,128)(2,1)S(1)} %copy-done.29, bf16[2,16,256]{2,1,0:T(8,128)(2,1)S(1)} %get-tuple-element.352.l_ref, bf16[4,384,1024]{2,1,0:T(8,128)(2,1)} %all-to-all-done.2.w_ref, ...), custom_call_target="tpu_custom_call" | custom-call | flops 1610612 | bytes 8000 | tf_op jit(solution)/shard_map/pallas_call | solution.py:418
  390.8 5.1 shard_map.190
  398.8 4.5 all-to-all-start.9
  412.4 6.2 %collective-permute-done.27.refs_6_ = bf16[2,384,640]{2,1,0:T(8,128)(2,1)} collective-permute-done((bf16[2,384,640]{2,1,0:T(8,128)(2,1)}, bf16[2,384,640]{2,1,0:T(8,128)(2,1)}, u32[]{:S(2)}, u32[]{:S(2)}) %collective-permute-start.27) | collective-permute-done | bytes 983072 | tf_op jit(solution)/shard_map/ppermute | solution.py:623
  431.5 4.6 all-to-all-start.10
  436.4 22.5 %collective-permute-done.26 = bf16[1,384,512]{2,1,0:T(8,128)(2,1)} collective-permute-done((bf16[1,384,512]{2,1,0:T(8,128)(2,1)}, bf16[1,384,512]{2,1,0:T(8,128)(2,1)}, u32[]{:S(2)}, u32[]{:S(2)}) %collective-permute-start.26) | collective-permute-done | bytes 393248 | tf_op jit(solution)/shard_map/ppermute | solution.py:623
  458.9 10.5 %collective-permute-done.28 = bf16[1,384,640]{2,1,0:T(8,128)(2,1)} collective-permute-done((bf16[1,384,640]{2,1,0:T(8,128)(2,1)}, bf16[1,384,640]{2,1,0:T(8,128)(2,1)}, u32[]{:S(2)}, u32[]{:S(2)}) %collective-permute-start.28) | collective-permute-done | bytes 491552 | tf_op jit(solution)/shard_map/ppermute | solution.py:623
  486.7 4.3 collective-permute-start.33
  491.1 6.2 %collective-permute-done.33 = bf16[2,96,2]{1,2,0:T(2,128)(2,1)S(1)} collective-permute-done((bf16[2,96,2]{1,2,0:T(2,128)(2,1)S(1)}, bf16[2,96,2]{1,2,0:T(2,128)(2,1)S(1)}, u32[]{:S(2)}, u32[]{:S(2)}) %collective-permute-start.33) | collective-permute-done | bytes 800 | tf_op jit(solution)/shard_map/ppermute | solution.py:623
  (411 shorter events, 192.9 us)
Async XLA Ops:
  6.1 25.0 %all-to-all-start = ((bf16[4,528,384]{2,1,0:T(8,128)(2,1)}), bf16[4,528,384]{2,1,0:T(8,128)(2,1)S(1)}, u32[]{:S(2)}, u32[]{:S(2)}) async-start(bf16[4,528,384]{2,1,0:T(8,128)(2,1)} %broadcast_in_dim.157), calls=%async_computation | async-start | bytes 3244032 | tf_op jit(solution)/shard_map/all_to_all | solution.py:631
  32.2 30.8 %all-to-all-start.1 = ((bf16[4,384,768]{2,1,0:T(8,128)(2,1)}), bf16[4,384,768]{2,1,0:T(8,128)(2,1)S(1)}, u32[]{:S(2)}, u32[]{:S(2)}) async-start(bf16[4,384,768]{2,1,0:T(8,128)(2,1)} %pad_maximum_fusion.1), calls=%async_computation.1 | async-start | bytes 4718592 | tf_op jit(solution)/shard_map/all_to_all | solution.py:631
  63.0 40.3 %all-to-all-start.2 = ((bf16[4,384,1024]{2,1,0:T(8,128)(2,1)}), bf16[4,384,1024]{2,1,0:T(8,128)(2,1)}, u32[]{:S(2)}, u32[]{:S(2)}) async-start(bf16[4,384,1024]{2,1,0:T(8,128)(2,1)} %pad_maximum_fusion), calls=%async_computation.2 | async-start | bytes 6291456 | tf_op jit(solution)/shard_map/all_to_all | solution.py:631
  67.7 57.4 %collective-permute-start.1 = (bf16[4,384,768]{2,1,0:T(8,128)(2,1)S(1)}, bf16[4,384,768]{2,1,0:T(8,128)(2,1)}, u32[]{:S(2)}, u32[]{:S(2)}) collective-permute-start(bf16[4,384,768]{2,1,0:T(8,128)(2,1)S(1)} %all-to-all-done.1.wa_ref), channel_id=1, source_target_pairs={{0,8},{8,0},{16,24},{24,16},{1,9},{9,1},{17,25},{25,17},{2,10},{10... | collective-permute-start | bytes 7077896 | tf_op jit(solution)/shard_map/ppermute | solution.py:623
  72.1 45.5 %collective-permute-start = (bf16[4,512,384]{2,1,0:T(8,128)(2,1)}, bf16[4,512,384]{2,1,0:T(8,128)(2,1)}, u32[]{:S(2)}, u32[]{:S(2)}) collective-permute-start(bf16[4,512,384]{2,1,0:T(8,128)(2,1)} %slice.206.x_ref), channel_id=1, source_target_pairs={{0,4},{4,0},{1,5},{5,1},{2,6},{6,2},{3,7},{7,3},{8,12},{12,8},{9,1... | collective-permute-start | bytes 4718600 | tf_op jit(solution)/shard_map/ppermute | solution.py:623
  104.6 39.0 %all-to-all-start.3 = ((bf16[4,512,384]{2,1,0:T(8,128)(2,1)}), bf16[4,512,384]{2,1,0:T(8,128)(2,1)}, u32[]{:S(2)}, u32[]{:S(2)}) async-start(bf16[4,512,384]{2,1,0:T(8,128)(2,1)} %broadcast_in_dim.158), calls=%async_computation.3 | async-start | bytes 3145728 | tf_op jit(solution)/shard_map/all_to_all | solution.py:631
  172.7 23.8 %all-to-all-start.5 = ((bf16[4,512,384]{2,1,0:T(8,128)(2,1)}), bf16[4,512,384]{2,1,0:T(8,128)(2,1)S(1)}, u32[]{:S(2)}, u32[]{:S(2)}) async-start(bf16[4,512,384]{2,1,0:T(8,128)(2,1)} %broadcast_in_dim.162), calls=%async_computation.5 | async-start | bytes 3145728 | tf_op jit(solution)/shard_map/all_to_all | solution.py:631
  176.8 21.0 %collective-permute-start.4 = (bf16[4,512,384]{2,1,0:T(8,128)(2,1)}, bf16[4,512,384]{2,1,0:T(8,128)(2,1)S(1)}, u32[]{:S(2)}, u32[]{:S(2)}) collective-permute-start(bf16[4,512,384]{2,1,0:T(8,128)(2,1)} %all-to-all-done.3.g_ref.refs_1_), channel_id=1, source_target_pairs={{0,4},{4,0},{1,5},{5,1},{2,6},{6,2},{3,7},{7,3},{8,12},{12,8},{9,1... | collective-permute-start | bytes 4718600 | tf_op jit(solution)/shard_map/ppermute | solution.py:623
  230.0 25.4 %all-to-all-start.6 = ((bf16[4,512,384]{2,1,0:T(8,128)(2,1)}), bf16[4,512,384]{2,1,0:T(8,128)(2,1)}, u32[]{:S(2)}, u32[]{:S(2)}) async-start(bf16[4,512,384]{2,1,0:T(8,128)(2,1)} %add_convert_fusion.2), calls=%async_computation.6 | async-start | bytes 3145728 | tf_op jit(solution)/shard_map/all_to_all | solution.py:631
  235.7 19.7 %collective-permute-start.9 = (f32[4,128]{1,0:T(4,128)S(1)}, f32[4,128]{1,0:T(4,128)S(1)}, u32[]{:S(2)}, u32[]{:S(2)}) collective-permute-start(f32[4,128]{1,0:T(4,128)S(1)} %bitcast.198), channel_id=1, source_target_pairs={{0,3},{1,2},{2,1},{3,0},{4,7},{5,6},{6,5},{7,4},{8,11},{9,10},{10,... | collective-permute-start | bytes 6152 | tf_op jit(solution)/shard_map/ppermute | solution.py:623
  244.4 19.3 %collective-permute-start.10 = (bf16[2,384,512]{2,1,0:T(8,128)(2,1)}, bf16[2,384,512]{2,1,0:T(8,128)(2,1)}, u32[]{:S(2)}, u32[]{:S(2)}) collective-permute-start(bf16[2,384,512]{2,1,0:T(8,128)(2,1)} %shard_map.175), channel_id=1, source_target_pairs={{0,8},{8,0},{16,24},{24,16},{1,9},{9,1},{17,25},{25,17},{2,10},{10... | collective-permute-start | bytes 2359304 | tf_op jit(solution)/shard_map/ppermute | solution.py:623
  274.9 23.1 %all-to-all-start.7 = ((bf16[4,1536,128]{2,1,0:T(8,128)(2,1)}), bf16[4,1536,128]{2,1,0:T(8,128)(2,1)}, u32[]{:S(2)}, u32[]{:S(2)}) async-start(bf16[4,1536,128]{2,1,0:T(8,128)(2,1)} %copy-done.32), calls=%async_computation.7 | async-start | bytes 3145728 | tf_op jit(solution)/shard_map/all_to_all | solution.py:631
  298.0 20.8 %collective-permute-start.12 = (bf16[4,512,384]{2,1,0:T(8,128)(2,1)}, bf16[4,512,384]{2,1,0:T(8,128)(2,1)S(1)}, u32[]{:S(2)}, u32[]{:S(2)}) collective-permute-start(bf16[4,512,384]{2,1,0:T(8,128)(2,1)} %copy-done.69), channel_id=1, source_target_pairs={{0,4},{4,0},{1,5},{5,1},{2,6},{6,2},{3,7},{7,3},{8,12},{12,8},{9,1... | collective-permute-start | bytes 4718600 | tf_op jit(solution)/shard_map/ppermute | solution.py:623
  298.0 50.0 %collective-permute-start.16 = (bf16[2,384,512]{2,1,0:T(8,128)(2,1)}, bf16[2,384,512]{2,1,0:T(8,128)(2,1)}, u32[]{:S(2)}, u32[]{:S(2)}) collective-permute-start(bf16[2,384,512]{2,1,0:T(8,128)(2,1)} %copy-done.61), channel_id=1, source_target_pairs={{0,8},{8,0},{16,24},{24,16},{1,9},{9,1},{17,25},{25,17},{2,10},{10... | collective-permute-start | bytes 2359304 | tf_op jit(solution)/shard_map/ppermute | solution.py:623
  299.6 44.3 %collective-permute-start.14 = (bf16[2,384,512]{2,1,0:T(8,128)(2,1)}, bf16[2,384,512]{2,1,0:T(8,128)(2,1)}, u32[]{:S(2)}, u32[]{:S(2)}) collective-permute-start(bf16[2,384,512]{2,1,0:T(8,128)(2,1)} %copy-done.62), channel_id=1, source_target_pairs={{0,8},{8,0},{16,24},{24,16},{1,9},{9,1},{17,25},{25,17},{2,10},{10... | collective-permute-start | bytes 2359304 | tf_op jit(solution)/shard_map/ppermute | solution.py:623
  320.2 51.2 %all-to-all-start.8 = ((bf16[4,512,384]{2,1,0:T(8,128)(2,1)}), bf16[4,512,384]{2,1,0:T(8,128)(2,1)}, u32[]{:S(2)}, u32[]{:S(2)}) async-start(bf16[4,512,384]{2,1,0:T(8,128)(2,1)} %add_convert_fusion.1), calls=%async_computation.8 | async-start | bytes 3145728 | tf_op jit(solution)/shard_map/all_to_all | solution.py:631
  325.1 28.1 %collective-permute-start.13 = (bf16[1,384,512]{2,1,0:T(8,128)(2,1)}, bf16[1,384,512]{2,1,0:T(8,128)(2,1)}, u32[]{:S(2)}, u32[]{:S(2)}) collective-permute-start(bf16[1,384,512]{2,1,0:T(8,128)(2,1)} %copy-done.71), channel_id=1, source_target_pairs={{0,16},{8,24},{16,0},{24,8},{1,17},{9,25},{17,1},{25,9},{2,18},{10... | collective-permute-start | bytes 1179656 | tf_op jit(solution)/shard_map/ppermute | solution.py:623
  330.9 39.6 %collective-permute-start.18 = (bf16[2,384,512]{2,1,0:T(8,128)(2,1)S(1)}, bf16[2,384,512]{2,1,0:T(8,128)(2,1)S(1)}, u32[]{:S(2)}, u32[]{:S(2)}) collective-permute-start(bf16[2,384,512]{2,1,0:T(8,128)(2,1)S(1)} %shard_map.183), channel_id=1, source_target_pairs={{0,8},{8,0},{16,24},{24,16},{1,9},{9,1},{17,25},{25,17},{2,10},{10... | collective-permute-start | bytes 2359304 | tf_op jit(solution)/shard_map/ppermute | solution.py:623
  347.9 20.1 %collective-permute-start.15 = (bf16[1,384,512]{2,1,0:T(8,128)(2,1)S(1)}, bf16[1,384,512]{2,1,0:T(8,128)(2,1)}, u32[]{:S(2)}, u32[]{:S(2)}) collective-permute-start(bf16[1,384,512]{2,1,0:T(8,128)(2,1)S(1)} %get-tuple-element.144), channel_id=1, source_target_pairs={{0,16},{8,24},{16,0},{24,8},{1,17},{9,25},{17,1},{25,9},{2,18},{10... | collective-permute-start | bytes 1179656 | tf_op jit(solution)/shard_map/ppermute | solution.py:623
  383.7 35.0 %collective-permute-start.27 = (bf16[2,384,640]{2,1,0:T(8,128)(2,1)}, bf16[2,384,640]{2,1,0:T(8,128)(2,1)}, u32[]{:S(2)}, u32[]{:S(2)}) collective-permute-start(bf16[2,384,640]{2,1,0:T(8,128)(2,1)} %shard_map.187), channel_id=1, source_target_pairs={{0,8},{8,0},{16,24},{24,16},{1,9},{9,1},{17,25},{25,17},{2,10},{10... | collective-permute-start | bytes 2949128 | tf_op jit(solution)/shard_map/ppermute | solution.py:623
  398.8 27.2 %all-to-all-start.9 = ((bf16[4,512,384]{2,1,0:T(8,128)(2,1)}), bf16[4,512,384]{2,1,0:T(8,128)(2,1)}, u32[]{:S(2)}, u32[]{:S(2)}) async-start(bf16[4,512,384]{2,1,0:T(8,128)(2,1)} %add_convert_fusion), calls=%async_computation.9 | async-start | bytes 3145728 | tf_op jit(solution)/shard_map/all_to_all | solution.py:631
  403.6 21.7 %collective-permute-start.29 = (bf16[2,96,768]{2,1,0:T(8,128)(2,1)S(1)}, bf16[2,96,768]{2,1,0:T(8,128)(2,1)S(1)}, u32[]{:S(2)}, u32[]{:S(2)}) collective-permute-start(bf16[2,96,768]{2,1,0:T(8,128)(2,1)S(1)} %pad_maximum_fusion.11), channel_id=1, source_target_pairs={{0,8},{8,0},{16,24},{24,16},{1,9},{9,1},{17,25},{25,17},{2,10},{10... | collective-permute-start | bytes 884744 | tf_op jit(solution)/shard_map/ppermute | solution.py:623
  404.0 25.0 %collective-permute-start.17 = (bf16[1,384,512]{2,1,0:T(8,128)(2,1)}, bf16[1,384,512]{2,1,0:T(8,128)(2,1)}, u32[]{:S(2)}, u32[]{:S(2)}) collective-permute-start(bf16[1,384,512]{2,1,0:T(8,128)(2,1)} %get-tuple-element.147), channel_id=1, source_target_pairs={{0,16},{8,24},{16,0},{24,8},{1,17},{9,25},{17,1},{25,9},{2,18},{10... | collective-permute-start | bytes 1179656 | tf_op jit(solution)/shard_map/ppermute | solution.py:623
  405.6 20.4 %collective-permute-start.24 = (f32[4,128]{1,0:T(4,128)S(1)}, f32[4,128]{1,0:T(4,128)S(1)}, u32[]{:S(2)}, u32[]{:S(2)}) collective-permute-start(f32[4,128]{1,0:T(4,128)S(1)} %bitcast.194), channel_id=1, source_target_pairs={{0,3},{1,2},{2,1},{3,0},{4,7},{5,6},{6,5},{7,4},{8,11},{9,10},{10,... | collective-permute-start | bytes 6152 | tf_op jit(solution)/shard_map/ppermute | solution.py:623
  408.3 20.7 %collective-permute-start.23 = (f32[4,128]{1,0:T(4,128)S(1)}, f32[4,128]{1,0:T(4,128)S(1)}, u32[]{:S(2)}, u32[]{:S(2)}) collective-permute-start(f32[4,128]{1,0:T(4,128)S(1)} %bitcast.195), channel_id=1, source_target_pairs={{0,2},{1,3},{2,0},{3,1},{4,6},{5,7},{6,4},{7,5},{8,10},{9,11},{10,... | collective-permute-start | bytes 6152 | tf_op jit(solution)/shard_map/ppermute | solution.py:623
  426.0 32.8 %collective-permute-start.26 = (bf16[1,384,512]{2,1,0:T(8,128)(2,1)}, bf16[1,384,512]{2,1,0:T(8,128)(2,1)}, u32[]{:S(2)}, u32[]{:S(2)}) collective-permute-start(bf16[1,384,512]{2,1,0:T(8,128)(2,1)} %get-tuple-element.167), channel_id=1, source_target_pairs={{0,16},{8,24},{16,0},{24,8},{1,17},{9,25},{17,1},{25,9},{2,18},{10... | collective-permute-start | bytes 1179656 | tf_op jit(solution)/shard_map/ppermute | solution.py:623
  426.0 43.4 %collective-permute-start.28 = (bf16[1,384,640]{2,1,0:T(8,128)(2,1)}, bf16[1,384,640]{2,1,0:T(8,128)(2,1)}, u32[]{:S(2)}, u32[]{:S(2)}) collective-permute-start(bf16[1,384,640]{2,1,0:T(8,128)(2,1)} %copy-done.70), channel_id=1, source_target_pairs={{0,16},{8,24},{16,0},{24,8},{1,17},{9,25},{17,1},{25,9},{2,18},{10... | collective-permute-start | bytes 1474568 | tf_op jit(solution)/shard_map/ppermute | solution.py:623
  431.5 46.7 %all-to-all-start.10 = ((bf16[4,96,1536]{2,1,0:T(8,128)(2,1)}), bf16[4,96,1536]{2,1,0:T(8,128)(2,1)}, u32[]{:S(2)}, u32[]{:S(2)}) async-start(bf16[4,96,1536]{2,1,0:T(8,128)(2,1)} %bitcast.169), calls=%async_computation.10 | async-start | bytes 2359296 | tf_op jit(solution)/shard_map/all_to_all | solution.py:631
  436.2 38.8 %collective-permute-start.30 = (bf16[1,96,768]{2,1,0:T(8,128)(2,1)S(1)}, bf16[1,96,768]{2,1,0:T(8,128)(2,1)S(1)}, u32[]{:S(2)}, u32[]{:S(2)}) collective-permute-start(bf16[1,96,768]{2,1,0:T(8,128)(2,1)S(1)} %slice.266), channel_id=1, source_target_pairs={{0,16},{8,24},{16,0},{24,8},{1,17},{9,25},{17,1},{25,9},{2,18},{10... | collective-permute-start | bytes 442376 | tf_op jit(solution)/shard_map/ppermute | solution.py:623
  436.3 38.7 %collective-permute-start.20 = (bf16[512,384]{1,0:T(8,128)(2,1)}, bf16[512,384]{1,0:T(8,128)(2,1)S(1)}, u32[]{:S(2)}, u32[]{:S(2)}) collective-permute-start(bf16[512,384]{1,0:T(8,128)(2,1)} %multiply_convert_fusion), channel_id=1, source_target_pairs={{0,4},{4,0},{1,5},{5,1},{2,6},{6,2},{3,7},{7,3},{8,12},{12,8},{9,1... | collective-permute-start | bytes 1179656 | tf_op jit(solution)/shard_map/ppermute | solution.py:623
  478.2 28.9 %all-to-all-start.11 = ((bf16[4,96,1152]{2,1,0:T(8,128)(2,1)}), bf16[4,96,1152]{2,1,0:T(8,128)(2,1)S(1)}, u32[]{:S(2)}, u32[]{:S(2)}) async-start(bf16[4,96,1152]{2,1,0:T(8,128)(2,1)} %bitcast.38), calls=%async_computation.11 | async-start | bytes 1769472 | tf_op jit(solution)/shard_map/all_to_all | solution.py:631
  481.7 24.7 %collective-permute-start.31 = (bf16[96,768]{1,0:T(8,128)(2,1)S(1)}, bf16[96,768]{1,0:T(8,128)(2,1)S(1)}, u32[]{:S(2)}, u32[]{:S(2)}) collective-permute-start(bf16[96,768]{1,0:T(8,128)(2,1)S(1)} %fusion.18), channel_id=1, source_target_pairs={{0,0},{1,8},{2,16},{3,24},{8,1},{9,9},{10,17},{11,25},{16,2},{17,1... | collective-permute-start | bytes 442376 | tf_op jit(solution)/shard_map/ppermute | solution.py:934
  (107 other events, 658.6 us)

commit v5 on v3

--- a/solution.py
+++ b/solution.py
@@ -891,7 +891,7 @@
     dn1_far = project_back(flags[1], pairs_a, per_half, back_b, lines_far, proj_w, misc, bf16)
     right_own = after(right_own, dn1_far, own_got)
     keep_own, next_own = dp_even(own_terms, n1_both, (right_own,), 4 * HD, own_got)
-    back_b = after(back_b, keep_own)
+    back_b = after(back_b, keep_own, next_2)
     dn1_own = project_back(flags[0], pairs_a, 0, back_b, lines_own, proj_w, misc, f32)
     dn1_here = partial(dn1_own, dn1_far)
     dn1_got = exchange(dn1_here, "wid")
@@ -901,7 +901,6 @@
         shared_terms, n1_both, (right_shared, *flat_both), 5 * HD, shared_got, half_flag
     )
     next_own, next_shared = lax.optimization_barrier((next_own, next_shared, dn1_got))[:2]
-    next_2 = after(next_2, dn1_got)
     sums = [sum(spread(sums_a, sums_b, p)) for p in range(2)]
     mean_one = line_sum(*sums, dn1_got)
     grad_normed_one = jnp.sum(dn1_got.astype(f32), axis=0)

time: 522 us -> 521 us (level)
    unnamed x218 -> x224, local copies, waits for them, and re-layouts: 43.1 us -> 45.3 us
  transfers between devices with their start and end apart: 47 -> 47, of which waited for: 17 -> 18; matrix products, arithmetic and copies ran while one was open for 11% -> 11% of each run, Pallas kernels for 18% -> 18%
where the time goes in v5:
time: 521 us; the launch traced here: 512 us
  waiting for transfers between devices  182 us (35%)
  Pallas kernels  113 us (22%)
  starting transfers between devices  82.8 us (16%)
  local copies, waits for them, and re-layouts  69 us (13%)
  other arithmetic  40 us (8%)
  blocking collectives  22.8 us (4%)
    all_to_all x11, waiting for transfers between devices, exchange(): return lax.all_to_all(x, axis, split_axis=0, concat_axis=0, tiled=True)  98.4 us
    ppermute x34, waiting for transfers between devices, swap(): return lax.ppermute(x, axis, [(n, n ^ k) for n in range(size)])  83.4 us
    all_to_all x11, starting transfers between devices, exchange(): return lax.all_to_all(x, axis, split_axis=0, concat_axis=0, tiled=True)  47.9 us
    unnamed x224, local copies, waits for them, and re-layouts  45.3 us
    ppermute x34, starting transfers between devices, swap(): return lax.ppermute(x, axis, [(n, n ^ k) for n in range(size)])  32.6 us
    all_to_all x1, blocking collectives, exchange(): return lax.all_to_all(x, axis, split_axis=0, concat_axis=0, tiled=True)  22.8 us
    pallas_call x2, Pallas kernels, feed_forward(): pl.pallas_call(functools.partial(ffn_kernel, n), out_shape=[shape(n, half...  22 us
    pallas_call x5, Pallas kernels, weight_add(): pl.pallas_call(functools.partial(weight_add_kernel, terms), out_shape=[sh...  16.4 us
  transfers between devices with their start and end apart: 47, of which 18 were waited for; matrix products, arithmetic and copies ran while one was open for 11% of the time, Pallas kernels for 18%

profile of v5, /device:TPU:0, one launch (start us, length us, event | category | flops | bytes accessed | tf_op | source)
XLA Modules:
  0.0 512.0 jit_solution(16057581700857648298)
XLA Ops:
  6.1 5.2 %all-to-all-start = ((bf16[4,528,384]{2,1,0:T(8,128)(2,1)}), bf16[4,528,384]{2,1,0:T(8,128)(2,1)S(1)}, u32[]{:S(2)}, u32[]{:S(2)}) async-start(bf16[4,528,384]{2,1,0:T(8,128)(2,1)} %broadcast_in_dim.157), calls=%async_computation | async-start | bytes 3244032 | tf_op jit(solution)/shard_map/all_to_all | solution.py:631
  17.2 13.9 %all-to-all-done = bf16[4,528,384]{2,1,0:T(8,128)(2,1)S(1)} async-done(((bf16[4,528,384]{2,1,0:T(8,128)(2,1)}), bf16[4,528,384]{2,1,0:T(8,128)(2,1)S(1)}, u32[]{:S(2)}, u32[]{:S(2)}) %all-to-all-start) | async-done | bytes 1622048 | tf_op jit(solution)/shard_map/all_to_all | solution.py:631
  40.9 22.1 %all-to-all-done.1.wa_ref = bf16[4,384,768]{2,1,0:T(8,128)(2,1)S(1)} async-done(((bf16[4,384,768]{2,1,0:T(8,128)(2,1)}), bf16[4,384,768]{2,1,0:T(8,128)(2,1)S(1)}, u32[]{:S(2)}, u32[]{:S(2)}) %all-to-all-start.1) | async-done | bytes 2359328 | tf_op jit(solution)/shard_map/all_to_all | solution.py:631
  63.0 4.6 all-to-all-start.2
  72.2 31.2 %all-to-all-done.2.w_ref = bf16[4,384,1024]{2,1,0:T(8,128)(2,1)} async-done(((bf16[4,384,1024]{2,1,0:T(8,128)(2,1)}), bf16[4,384,1024]{2,1,0:T(8,128)(2,1)}, u32[]{:S(2)}, u32[]{:S(2)}) %all-to-all-start.2) | async-done | bytes 3145760 | tf_op jit(solution)/shard_map/all_to_all | solution.py:631
  104.6 4.5 all-to-all-start.3
  110.9 5.4 %shard_map.169 = (bf16[2,256,512]{2,1,0:T(8,128)(2,1)S(1)}, bf16[2,256,512]{2,1,0:T(8,128)(2,1)S(1)}, f32[2,16,256]{2,1,0:T(8,128)S(1)}, f32[2,1,256]{2,1,0:T(1,128)S(1)}, bf16[4,512,384]{2,1,0:T(8,128)(2,1)S(1)}) custom-call(bf16[4,512,384]{2,1,0:T(8,128)(2,1)} %slice.206.x_ref, bf16[4,384,1024]{2,1,0:T(8,128)(2,1)} %all-to-all-done.2.w_ref, ...), custom_call_target="tpu_custom_call" | custom-call | flops 1610612 | bytes 8000 | tf_op jit(solution)/shard_map/pallas_call | solution.py:261
  117.6 5.7 %shard_map.170 = (bf16[2,256,512]{2,1,0:T(8,128)(2,1)S(1)}, bf16[2,256,512]{2,1,0:T(8,128)(2,1)S(1)}, f32[2,16,256]{2,1,0:T(8,128)S(1)}, f32[2,1,256]{2,1,0:T(1,128)}, bf16[4,512,384]{2,1,0:T(8,128)(2,1)S(1)}) custom-call(bf16[4,512,384]{2,1,0:T(8,128)(2,1)} %collective-permute-done.x_ref, bf16[4,384,1024]{2,1,0:T(8,128)(2,1)} %all-to-all-done.2.w_ref, ...), custom_call_target="tpu_custom_call" | custom-call | flops 1610612 | bytes 8000 | tf_op jit(solution)/shard_map/pallas_call | solution.py:261
  125.0 15.0 %shard_map.171 = (bf16[6,256,128]{2,1,0:T(8,128)(2,1)S(1)}, f32[6,256,256]{2,1,0:T(8,128)S(1)}, f32[6,256,256]{2,1,0:T(8,128)S(1)}, f32[6,256,256]{2,1,0:T(8,128)S(1)}) custom-call(s32[6]{0:T(128)S(1)} %pad_add_fusion.len_ref, bf16[6,256,512]{2,1,0:T(8,128)(2,1)} %pad_maximum_fusion.2.x_ref, f32[6,1,256]{2,1,0:T(1,128)S(1)} %pad_maximum_fusion.12.l_ref), custom_call_target="tpu_custom_call" | custom-call | flops 9600000 | bytes 6600 | tf_op jit(solution)/shard_map/pallas_call | solution.py:167
  143.8 22.8 %all_to_all.60.o_ref = bf16[4,1536,128]{2,1,0:T(8,128)(2,1)S(1)} all-to-all(bf16[4,1536,128]{2,1,0:T(8,128)(2,1)S(1)} %broadcast_in_dim.160), channel_id=1, replica_groups=mesh['dp'=4,'hid'=2,'wid'=4] {'wid'}, dimensions={0} | all-to-all | bytes 3145728 | tf_op jit(solution)/shard_map/all_to_all | solution.py:631
  176.8 19.6 %all-to-all-done.5.h_ref = bf16[4,512,384]{2,1,0:T(8,128)(2,1)S(1)} async-done(((bf16[4,512,384]{2,1,0:T(8,128)(2,1)}), bf16[4,512,384]{2,1,0:T(8,128)(2,1)S(1)}, u32[]{:S(2)}, u32[]{:S(2)}) %all-to-all-start.5) | async-done | bytes 1572896 | tf_op jit(solution)/shard_map/all_to_all | solution.py:631
  200.9 10.9 %shard_map.174 = (bf16[4,512,384]{2,1,0:T(8,128)(2,1)S(1)}, bf16[2,512,256]{2,1,0:T(8,128)(2,1)S(1)}, bf16[2,512,512]{2,1,0:T(8,128)(2,1)S(1)}, bf16[4,512,384]{...) custom-call(s32[2]{0:T(128)S(1)} %get-tuple-element.278.len_ref, s32[1]{0:T(128)} %bitcast.12.side_ref, ...), custom_call_target="tpu_custom_call" | custom-call | flops 4026531 | bytes 12000 | tf_op jit(solution)/shard_map/pallas_call | solution.py:347
  212.7 11.1 %shard_map.173 = (bf16[4,512,384]{2,1,0:T(8,128)(2,1)S(1)}, bf16[2,512,256]{2,1,0:T(8,128)(2,1)S(1)}, bf16[2,512,512]{2,1,0:T(8,128)(2,1)S(1)}, f32[4,512,384]{2...) custom-call(s32[2]{0:T(128)S(1)} %get-tuple-element.276.len_ref, s32[1]{0:T(128)} %bitcast.12.side_ref, ...), custom_call_target="tpu_custom_call" | custom-call | flops 4026531 | bytes 12000 | tf_op jit(solution)/shard_map/pallas_call | solution.py:347
  225.6 4.1 add_convert_fusion.2
  229.7 4.5 all-to-all-start.6
  274.7 4.6 all-to-all-start.7
  279.3 5.5 %shard_map.180 = (f32[4,512,384]{2,1,0:T(8,128)}, bf16[4,512,384]{2,1,0:T(8,128)(2,1)S(1)}) custom-call(s32[1]{0:T(128)} %bitcast.12.side_ref, bf16[2,512,256]{2,1,0:T(8,128)(2,1)S(1)} %copy-done.48, bf16[2,512,256]{2,1,0:T(8,128)(2,1)S(1)} %copy-done.44, bf16[4,384,768]{2,1,0:T(8,128)(2,1)S(1)} %copy-done.1, bf16[4,384,768]{2,1,0:T(8,128)(2,1)} %collective-permute-done.1.wb_ref), custom_call_target="tpu_custom_call" | custom-call | flops 1610612 | bytes 12000 | tf_op jit(solution)/shard_map/pallas_call | solution.py:390
  286.0 11.7 %all-to-all-done.7 = bf16[4,1536,128]{2,1,0:T(8,128)(2,1)} async-done(((bf16[4,1536,128]{2,1,0:T(8,128)(2,1)}), bf16[4,1536,128]{2,1,0:T(8,128)(2,1)}, u32[]{:S(2)}, u32[]{:S(2)}) %all-to-all-start.7) | async-done | bytes 1572896 | tf_op jit(solution)/shard_map/all_to_all | solution.py:631
  308.2 10.2 %shard_map.182 = (bf16[4,256,512]{2,1,0:T(8,128)(2,1)S(1)}, f32[4,1,256]{2,1,0:T(1,128)S(1)}, f32[4,1,256]{2,1,0:T(1,128)S(1)}) custom-call(s32[6]{0:T(128)S(1)} %pad_add_fusion.len_ref, bf16[6,256,512]{2,1,0:T(8,128)(2,1)S(1)} %copy-done.6, f32[6,1,256]{2,1,0:T(1,128)S(1)} %pad_maximum_fusion.12.l_ref, f32[6,256,256]{2,1,0:T(8,128)S(1)} %copy-done.36, ...), custom_call_target="tpu_custom_call" | custom-call | flops 5600000 | bytes 5600 | tf_op jit(solution)/shard_map/pallas_call | solution.py:187
  319.9 4.8 all-to-all-start.8
  332.3 11.4 %collective-permute-done.14.refs_5_ = bf16[2,384,512]{2,1,0:T(8,128)(2,1)} collective-permute-done((bf16[2,384,512]{2,1,0:T(8,128)(2,1)}, bf16[2,384,512]{2,1,0:T(8,128)(2,1)}, u32[]{:S(2)}, u32[]{:S(2)}) %collective-permute-start.14) | collective-permute-done | bytes 786464 | tf_op jit(solution)/shard_map/ppermute | solution.py:623
  347.8 4.4 shard_map.185
  352.3 5.8 %shard_map.186 = (bf16[2,256,512]{2,1,0:T(8,128)(2,1)S(1)}, f32[2,1,256]{2,1,0:T(1,128)S(1)}, f32[2,1,256]{2,1,0:T(1,128)S(1)}) custom-call(s32[6]{0:T(128)S(1)} %pad_add_fusion.len_ref, bf16[6,256,512]{2,1,0:T(8,128)(2,1)S(1)} %copy-done.7, f32[6,1,256]{2,1,0:T(1,128)S(1)} %pad_maximum_fusion.12.l_ref, f32[6,256,256]{2,1,0:T(8,128)S(1)} %copy-done.37, ...), custom_call_target="tpu_custom_call" | custom-call | flops 2800000 | bytes 2800 | tf_op jit(solution)/shard_map/pallas_call | solution.py:187
  358.3 9.3 %collective-permute-done.15 = bf16[1,384,512]{2,1,0:T(8,128)(2,1)} collective-permute-done((bf16[1,384,512]{2,1,0:T(8,128)(2,1)S(1)}, bf16[1,384,512]{2,1,0:T(8,128)(2,1)}, u32[]{:S(2)}, u32[]{:S(2)}) %collective-permute-start.15) | collective-permute-done | bytes 393248 | tf_op jit(solution)/shard_map/ppermute | solution.py:623
  373.4 5.8 %shard_map.188 = bf16[4,512,384]{2,1,0:T(8,128)(2,1)} custom-call(s32[1]{0:T(128)} %bitcast.31.flag_ref, bf16[4,256,512]{2,1,0:T(8,128)(2,1)S(1)} %copy-done.13, bf16[2,256,512]{2,1,0:T(8,128)(2,1)S(1)} %copy-done.29, bf16[2,16,256]{2,1,0:T(8,128)(2,1)S(1)} %get-tuple-element.352.l_ref, bf16[4,384,1024]{2,1,0:T(8,128)(2,1)} %all-to-all-done.2.w_ref, ...), custom_call_target="tpu_custom_call" | custom-call | flops 1610612 | bytes 8000 | tf_op jit(solution)/shard_map/pallas_call | solution.py:418
  393.8 10.3 %collective-permute-done.17 = bf16[1,384,512]{2,1,0:T(8,128)(2,1)S(1)} collective-permute-done((bf16[1,384,512]{2,1,0:T(8,128)(2,1)S(1)}, bf16[1,384,512]{2,1,0:T(8,128)(2,1)S(1)}, u32[]{:S(2)}, u32[]{:S(2)}) %collective-permute-start.17) | collective-permute-done | bytes 393248 | tf_op jit(solution)/shard_map/ppermute | solution.py:623
  404.9 5.1 shard_map.190
  412.8 4.4 all-to-all-start.9
  425.1 8.2 %collective-permute-done.27.refs_6_ = bf16[2,384,640]{2,1,0:T(8,128)(2,1)S(1)} collective-permute-done((bf16[2,384,640]{2,1,0:T(8,128)(2,1)}, bf16[2,384,640]{2,1,0:T(8,128)(2,1)S(1)}, u32[]{:S(2)}, u32[]{:S(2)}) %collective-permute-start.27) | collective-permute-done | bytes 983072 | tf_op jit(solution)/shard_map/ppermute | solution.py:623
  434.4 5.8 %collective-permute-done.26 = bf16[1,384,512]{2,1,0:T(8,128)(2,1)S(1)} collective-permute-done((bf16[1,384,512]{2,1,0:T(8,128)(2,1)S(1)}, bf16[1,384,512]{2,1,0:T(8,128)(2,1)S(1)}, u32[]{:S(2)}, u32[]{:S(2)}) %collective-permute-start.26) | collective-permute-done | bytes 393248 | tf_op jit(solution)/shard_map/ppermute | solution.py:623
  445.5 4.2 all-to-all-start.10
  453.8 18.5 %collective-permute-done.28 = bf16[1,384,640]{2,1,0:T(8,128)(2,1)} collective-permute-done((bf16[1,384,640]{2,1,0:T(8,128)(2,1)}, bf16[1,384,640]{2,1,0:T(8,128)(2,1)}, u32[]{:S(2)}, u32[]{:S(2)}) %collective-permute-start.28) | collective-permute-done | bytes 491552 | tf_op jit(solution)/shard_map/ppermute | solution.py:623
  (419 shorter events, 198.4 us)
Async XLA Ops:
  6.1 25.0 %all-to-all-start = ((bf16[4,528,384]{2,1,0:T(8,128)(2,1)}), bf16[4,528,384]{2,1,0:T(8,128)(2,1)S(1)}, u32[]{:S(2)}, u32[]{:S(2)}) async-start(bf16[4,528,384]{2,1,0:T(8,128)(2,1)} %broadcast_in_dim.157), calls=%async_computation | async-start | bytes 3244032 | tf_op jit(solution)/shard_map/all_to_all | solution.py:631
  32.2 30.8 %all-to-all-start.1 = ((bf16[4,384,768]{2,1,0:T(8,128)(2,1)}), bf16[4,384,768]{2,1,0:T(8,128)(2,1)S(1)}, u32[]{:S(2)}, u32[]{:S(2)}) async-start(bf16[4,384,768]{2,1,0:T(8,128)(2,1)} %pad_maximum_fusion.1), calls=%async_computation.1 | async-start | bytes 4718592 | tf_op jit(solution)/shard_map/all_to_all | solution.py:631
  63.0 40.3 %all-to-all-start.2 = ((bf16[4,384,1024]{2,1,0:T(8,128)(2,1)}), bf16[4,384,1024]{2,1,0:T(8,128)(2,1)}, u32[]{:S(2)}, u32[]{:S(2)}) async-start(bf16[4,384,1024]{2,1,0:T(8,128)(2,1)} %pad_maximum_fusion), calls=%async_computation.2 | async-start | bytes 6291456 | tf_op jit(solution)/shard_map/all_to_all | solution.py:631
  67.7 57.3 %collective-permute-start.1 = (bf16[4,384,768]{2,1,0:T(8,128)(2,1)S(1)}, bf16[4,384,768]{2,1,0:T(8,128)(2,1)}, u32[]{:S(2)}, u32[]{:S(2)}) collective-permute-start(bf16[4,384,768]{2,1,0:T(8,128)(2,1)S(1)} %all-to-all-done.1.wa_ref), channel_id=1, source_target_pairs={{0,8},{8,0},{16,24},{24,16},{1,9},{9,1},{17,25},{25,17},{2,10},{10... | collective-permute-start | bytes 7077896 | tf_op jit(solution)/shard_map/ppermute | solution.py:623
  72.1 45.4 %collective-permute-start = (bf16[4,512,384]{2,1,0:T(8,128)(2,1)}, bf16[4,512,384]{2,1,0:T(8,128)(2,1)}, u32[]{:S(2)}, u32[]{:S(2)}) collective-permute-start(bf16[4,512,384]{2,1,0:T(8,128)(2,1)} %slice.206.x_ref), channel_id=1, source_target_pairs={{0,4},{4,0},{1,5},{5,1},{2,6},{6,2},{3,7},{7,3},{8,12},{12,8},{9,1... | collective-permute-start | bytes 4718600 | tf_op jit(solution)/shard_map/ppermute | solution.py:623
  104.6 38.9 %all-to-all-start.3 = ((bf16[4,512,384]{2,1,0:T(8,128)(2,1)}), bf16[4,512,384]{2,1,0:T(8,128)(2,1)}, u32[]{:S(2)}, u32[]{:S(2)}) async-start(bf16[4,512,384]{2,1,0:T(8,128)(2,1)} %broadcast_in_dim.158), calls=%async_computation.3 | async-start | bytes 3145728 | tf_op jit(solution)/shard_map/all_to_all | solution.py:631
  172.6 23.8 %all-to-all-start.5 = ((bf16[4,512,384]{2,1,0:T(8,128)(2,1)}), bf16[4,512,384]{2,1,0:T(8,128)(2,1)S(1)}, u32[]{:S(2)}, u32[]{:S(2)}) async-start(bf16[4,512,384]{2,1,0:T(8,128)(2,1)} %broadcast_in_dim.162), calls=%async_computation.5 | async-start | bytes 3145728 | tf_op jit(solution)/shard_map/all_to_all | solution.py:631
  176.6 20.9 %collective-permute-start.4 = (bf16[4,512,384]{2,1,0:T(8,128)(2,1)}, bf16[4,512,384]{2,1,0:T(8,128)(2,1)S(1)}, u32[]{:S(2)}, u32[]{:S(2)}) collective-permute-start(bf16[4,512,384]{2,1,0:T(8,128)(2,1)} %all-to-all-done.3.g_ref.refs_1_), channel_id=1, source_target_pairs={{0,4},{4,0},{1,5},{5,1},{2,6},{6,2},{3,7},{7,3},{8,12},{12,8},{9,1... | collective-permute-start | bytes 4718600 | tf_op jit(solution)/shard_map/ppermute | solution.py:623
  229.7 25.4 %all-to-all-start.6 = ((bf16[4,512,384]{2,1,0:T(8,128)(2,1)}), bf16[4,512,384]{2,1,0:T(8,128)(2,1)}, u32[]{:S(2)}, u32[]{:S(2)}) async-start(bf16[4,512,384]{2,1,0:T(8,128)(2,1)} %add_convert_fusion.2), calls=%async_computation.6 | async-start | bytes 3145728 | tf_op jit(solution)/shard_map/all_to_all | solution.py:631
  235.5 19.7 %collective-permute-start.9 = (f32[4,128]{1,0:T(4,128)S(1)}, f32[4,128]{1,0:T(4,128)S(1)}, u32[]{:S(2)}, u32[]{:S(2)}) collective-permute-start(f32[4,128]{1,0:T(4,128)S(1)} %bitcast.199), channel_id=1, source_target_pairs={{0,3},{1,2},{2,1},{3,0},{4,7},{5,6},{6,5},{7,4},{8,11},{9,10},{10,... | collective-permute-start | bytes 6152 | tf_op jit(solution)/shard_map/ppermute | solution.py:623
  274.7 23.0 %all-to-all-start.7 = ((bf16[4,1536,128]{2,1,0:T(8,128)(2,1)}), bf16[4,1536,128]{2,1,0:T(8,128)(2,1)}, u32[]{:S(2)}, u32[]{:S(2)}) async-start(bf16[4,1536,128]{2,1,0:T(8,128)(2,1)} %copy-done.32), calls=%async_computation.7 | async-start | bytes 3145728 | tf_op jit(solution)/shard_map/all_to_all | solution.py:631
  297.7 20.7 %collective-permute-start.12 = (bf16[4,512,384]{2,1,0:T(8,128)(2,1)}, bf16[4,512,384]{2,1,0:T(8,128)(2,1)S(1)}, u32[]{:S(2)}, u32[]{:S(2)}) collective-permute-start(bf16[4,512,384]{2,1,0:T(8,128)(2,1)} %copy-done.72), channel_id=1, source_target_pairs={{0,4},{4,0},{1,5},{5,1},{2,6},{6,2},{3,7},{7,3},{8,12},{12,8},{9,1... | collective-permute-start | bytes 4718600 | tf_op jit(solution)/shard_map/ppermute | solution.py:623
  297.7 50.0 %collective-permute-start.16 = (bf16[2,384,512]{2,1,0:T(8,128)(2,1)}, bf16[2,384,512]{2,1,0:T(8,128)(2,1)}, u32[]{:S(2)}, u32[]{:S(2)}) collective-permute-start(bf16[2,384,512]{2,1,0:T(8,128)(2,1)} %copy-done.64), channel_id=1, source_target_pairs={{0,8},{8,0},{16,24},{24,16},{1,9},{9,1},{17,25},{25,17},{2,10},{10... | collective-permute-start | bytes 2359304 | tf_op jit(solution)/shard_map/ppermute | solution.py:623
  299.4 44.3 %collective-permute-start.14 = (bf16[2,384,512]{2,1,0:T(8,128)(2,1)}, bf16[2,384,512]{2,1,0:T(8,128)(2,1)}, u32[]{:S(2)}, u32[]{:S(2)}) collective-permute-start(bf16[2,384,512]{2,1,0:T(8,128)(2,1)} %copy-done.65), channel_id=1, source_target_pairs={{0,8},{8,0},{16,24},{24,16},{1,9},{9,1},{17,25},{25,17},{2,10},{10... | collective-permute-start | bytes 2359304 | tf_op jit(solution)/shard_map/ppermute | solution.py:623
  319.9 51.2 %all-to-all-start.8 = ((bf16[4,512,384]{2,1,0:T(8,128)(2,1)}), bf16[4,512,384]{2,1,0:T(8,128)(2,1)}, u32[]{:S(2)}, u32[]{:S(2)}) async-start(bf16[4,512,384]{2,1,0:T(8,128)(2,1)} %add_convert_fusion.1), calls=%async_computation.8 | async-start | bytes 3145728 | tf_op jit(solution)/shard_map/all_to_all | solution.py:631
  324.7 27.5 %collective-permute-start.13 = (bf16[1,384,512]{2,1,0:T(8,128)(2,1)}, bf16[1,384,512]{2,1,0:T(8,128)(2,1)}, u32[]{:S(2)}, u32[]{:S(2)}) collective-permute-start(bf16[1,384,512]{2,1,0:T(8,128)(2,1)} %copy-done.75), channel_id=1, source_target_pairs={{0,16},{8,24},{16,0},{24,8},{1,17},{9,25},{17,1},{25,9},{2,18},{10... | collective-permute-start | bytes 1179656 | tf_op jit(solution)/shard_map/ppermute | solution.py:623
  330.6 39.7 %collective-permute-start.18 = (bf16[2,384,512]{2,1,0:T(8,128)(2,1)S(1)}, bf16[2,384,512]{2,1,0:T(8,128)(2,1)S(1)}, u32[]{:S(2)}, u32[]{:S(2)}) collective-permute-start(bf16[2,384,512]{2,1,0:T(8,128)(2,1)S(1)} %shard_map.183), channel_id=1, source_target_pairs={{0,8},{8,0},{16,24},{24,16},{1,9},{9,1},{17,25},{25,17},{2,10},{10... | collective-permute-start | bytes 2359304 | tf_op jit(solution)/shard_map/ppermute | solution.py:623
  347.7 20.0 %collective-permute-start.15 = (bf16[1,384,512]{2,1,0:T(8,128)(2,1)S(1)}, bf16[1,384,512]{2,1,0:T(8,128)(2,1)}, u32[]{:S(2)}, u32[]{:S(2)}) collective-permute-start(bf16[1,384,512]{2,1,0:T(8,128)(2,1)S(1)} %get-tuple-element.144), channel_id=1, source_target_pairs={{0,16},{8,24},{16,0},{24,8},{1,17},{9,25},{17,1},{25,9},{2,18},{10... | collective-permute-start | bytes 1179656 | tf_op jit(solution)/shard_map/ppermute | solution.py:623
  379.2 30.7 %collective-permute-start.19 = (bf16[4,512,384]{2,1,0:T(8,128)(2,1)}, bf16[4,512,384]{2,1,0:T(8,128)(2,1)}, u32[]{:S(2)}, u32[]{:S(2)}) collective-permute-start(bf16[4,512,384]{2,1,0:T(8,128)(2,1)} %shard_map.188), channel_id=1, source_target_pairs={{0,4},{4,0},{1,5},{5,1},{2,6},{6,2},{3,7},{7,3},{8,12},{12,8},{9,1... | collective-permute-start | bytes 4718600 | tf_op jit(solution)/shard_map/ppermute | solution.py:623
  382.4 21.7 %collective-permute-start.17 = (bf16[1,384,512]{2,1,0:T(8,128)(2,1)S(1)}, bf16[1,384,512]{2,1,0:T(8,128)(2,1)S(1)}, u32[]{:S(2)}, u32[]{:S(2)}) collective-permute-start(bf16[1,384,512]{2,1,0:T(8,128)(2,1)S(1)} %copy-done.74), channel_id=1, source_target_pairs={{0,16},{8,24},{16,0},{24,8},{1,17},{9,25},{17,1},{25,9},{2,18},{10... | collective-permute-start | bytes 1179656 | tf_op jit(solution)/shard_map/ppermute | solution.py:623
  386.9 58.6 %collective-permute-start.29 = (bf16[2,96,768]{2,1,0:T(8,128)(2,1)}, bf16[2,96,768]{2,1,0:T(8,128)(2,1)}, u32[]{:S(2)}, u32[]{:S(2)}) collective-permute-start(bf16[2,96,768]{2,1,0:T(8,128)(2,1)} %pad_maximum_fusion.11), channel_id=1, source_target_pairs={{0,8},{8,0},{16,24},{24,16},{1,9},{9,1},{17,25},{25,17},{2,10},{10... | collective-permute-start | bytes 884744 | tf_op jit(solution)/shard_map/ppermute | solution.py:623
  387.4 58.1 %collective-permute-start.24 = (f32[4,128]{1,0:T(4,128)S(1)}, f32[4,128]{1,0:T(4,128)S(1)}, u32[]{:S(2)}, u32[]{:S(2)}) collective-permute-start(f32[4,128]{1,0:T(4,128)S(1)} %bitcast.195), channel_id=1, source_target_pairs={{0,3},{1,2},{2,1},{3,0},{4,7},{5,6},{6,5},{7,4},{8,11},{9,10},{10,... | collective-permute-start | bytes 6152 | tf_op jit(solution)/shard_map/ppermute | solution.py:623
  388.8 56.7 %collective-permute-start.23 = (f32[4,128]{1,0:T(4,128)S(1)}, f32[4,128]{1,0:T(4,128)S(1)}, u32[]{:S(2)}, u32[]{:S(2)}) collective-permute-start(f32[4,128]{1,0:T(4,128)S(1)} %bitcast.196), channel_id=1, source_target_pairs={{0,2},{1,3},{2,0},{3,1},{4,6},{5,7},{6,4},{7,5},{8,10},{9,11},{10,... | collective-permute-start | bytes 6152 | tf_op jit(solution)/shard_map/ppermute | solution.py:623
  404.1 29.1 %collective-permute-start.27 = (bf16[2,384,640]{2,1,0:T(8,128)(2,1)}, bf16[2,384,640]{2,1,0:T(8,128)(2,1)S(1)}, u32[]{:S(2)}, u32[]{:S(2)}) collective-permute-start(bf16[2,384,640]{2,1,0:T(8,128)(2,1)} %shard_map.187), channel_id=1, source_target_pairs={{0,8},{8,0},{16,24},{24,16},{1,9},{9,1},{17,25},{25,17},{2,10},{10... | collective-permute-start | bytes 2949128 | tf_op jit(solution)/shard_map/ppermute | solution.py:623
  412.8 32.6 %all-to-all-start.9 = ((bf16[4,512,384]{2,1,0:T(8,128)(2,1)}), bf16[4,512,384]{2,1,0:T(8,128)(2,1)}, u32[]{:S(2)}, u32[]{:S(2)}) async-start(bf16[4,512,384]{2,1,0:T(8,128)(2,1)} %add_convert_fusion), calls=%async_computation.9 | async-start | bytes 3145728 | tf_op jit(solution)/shard_map/all_to_all | solution.py:631
  419.8 20.4 %collective-permute-start.26 = (bf16[1,384,512]{2,1,0:T(8,128)(2,1)S(1)}, bf16[1,384,512]{2,1,0:T(8,128)(2,1)S(1)}, u32[]{:S(2)}, u32[]{:S(2)}) collective-permute-start(bf16[1,384,512]{2,1,0:T(8,128)(2,1)S(1)} %copy-done.77), channel_id=1, source_target_pairs={{0,16},{8,24},{16,0},{24,8},{1,17},{9,25},{17,1},{25,9},{2,18},{10... | collective-permute-start | bytes 1179656 | tf_op jit(solution)/shard_map/ppermute | solution.py:623
  445.2 27.1 %collective-permute-start.28 = (bf16[1,384,640]{2,1,0:T(8,128)(2,1)}, bf16[1,384,640]{2,1,0:T(8,128)(2,1)}, u32[]{:S(2)}, u32[]{:S(2)}) collective-permute-start(bf16[1,384,640]{2,1,0:T(8,128)(2,1)} %get-tuple-element.169), channel_id=1, source_target_pairs={{0,16},{8,24},{16,0},{24,8},{1,17},{9,25},{17,1},{25,9},{2,18},{10... | collective-permute-start | bytes 1474568 | tf_op jit(solution)/shard_map/ppermute | solution.py:623
  445.5 34.9 %all-to-all-start.10 = ((bf16[4,96,1536]{2,1,0:T(8,128)(2,1)}), bf16[4,96,1536]{2,1,0:T(8,128)(2,1)S(1)}, u32[]{:S(2)}, u32[]{:S(2)}) async-start(bf16[4,96,1536]{2,1,0:T(8,128)(2,1)} %bitcast.169), calls=%async_computation.10 | async-start | bytes 2359296 | tf_op jit(solution)/shard_map/all_to_all | solution.py:631
  450.9 26.8 %collective-permute-start.30 = (bf16[1,96,768]{2,1,0:T(8,128)(2,1)S(1)}, bf16[1,96,768]{2,1,0:T(8,128)(2,1)S(1)}, u32[]{:S(2)}, u32[]{:S(2)}) collective-permute-start(bf16[1,96,768]{2,1,0:T(8,128)(2,1)S(1)} %slice.266), channel_id=1, source_target_pairs={{0,16},{8,24},{16,0},{24,8},{1,17},{9,25},{17,1},{25,9},{2,18},{10... | collective-permute-start | bytes 442376 | tf_op jit(solution)/shard_map/ppermute | solution.py:623
  453.8 24.5 %collective-permute-start.20 = (bf16[512,384]{1,0:T(8,128)(2,1)S(1)}, bf16[512,384]{1,0:T(8,128)(2,1)S(1)}, u32[]{:S(2)}, u32[]{:S(2)}) collective-permute-start(bf16[512,384]{1,0:T(8,128)(2,1)S(1)} %multiply_convert_fusion), channel_id=1, source_target_pairs={{0,4},{4,0},{1,5},{5,1},{2,6},{6,2},{3,7},{7,3},{8,12},{12,8},{9,1... | collective-permute-start | bytes 1179656 | tf_op jit(solution)/shard_map/ppermute | solution.py:623
  480.4 28.5 %all-to-all-start.11 = ((bf16[4,96,1152]{2,1,0:T(8,128)(2,1)}), bf16[4,96,1152]{2,1,0:T(8,128)(2,1)S(1)}, u32[]{:S(2)}, u32[]{:S(2)}) async-start(bf16[4,96,1152]{2,1,0:T(8,128)(2,1)} %bitcast.170), calls=%async_computation.11 | async-start | bytes 1769472 | tf_op jit(solution)/shard_map/all_to_all | solution.py:631
  484.0 24.2 %collective-permute-start.31 = (bf16[96,768]{1,0:T(8,128)(2,1)}, bf16[96,768]{1,0:T(8,128)(2,1)S(1)}, u32[]{:S(2)}, u32[]{:S(2)}) collective-permute-start(bf16[96,768]{1,0:T(8,128)(2,1)} %fusion.18), channel_id=1, source_target_pairs={{0,0},{1,8},{2,16},{3,24},{8,1},{9,9},{10,17},{11,25},{16,2},{17,1... | collective-permute-start | bytes 442376 | tf_op jit(solution)/shard_map/ppermute | solution.py:934
  (111 other events, 692.6 us)
